TPU v7x, 32 devices: a whole 2x2x4 slice. The times are simulated.
32 devices in a mesh: gx: 8 (over z, core), gy: 2 (over y), gz: 2 (over x).
Axes of the slice: x: 2, y: 2, z: 4, core: 2. Of those that a mesh axis runs over, the one named last changes fastest.
Arguments:
- adjoint: float32 [2, 4, 16, 64, 256], P(None, None, 'gz', 'gx', 'gy'), may hold values from -6 to 6
- saved_state: float32 [4, 4, 16, 64, 256], P(None, None, 'gz', 'gx', 'gy'), may hold values from -6 to 6
- wind_field: float32 [3, 16, 64, 256], P(None, 'gz', 'gx', 'gy'), may hold values from -0.3 to 0.3
- facade_slot: int32 [16, 64, 256], P('gz', 'gx', 'gy'), may hold values from 0 to 64, as said below
- facade_table: int32 [2, 8, 2, 64], P('gz', 'gx', 'gy'), may hold values from 0 to 1023, as said below
- impedance: float32 [1024], replicated, may hold values from 0.1 to 1
Outputs:
- adjoint_out: float32 [2, 4, 16, 64, 256], P(None, None, 'gz', 'gx', 'gy')
- gradient: float32 [1024], P(('gx', 'gy', 'gz'))
Inputs may be any that keep to these rules, and one draw needn't show every extreme that they name: `facade_slot`: slots name entries of the cell's own device block table. `facade_table`: A block's facades are owned by that block's device or by one of the two devices beside it along gx (wrapping), the owner of facade f being the device of index f // 32 along gx+gy+gz; ids may repeat within and across tables.
All inputs are finite; a program needn't handle non-finite values.
Results may differ from a plain program's by a relative error of at most 0.00013.
Values sent between devices are 32-bit elements; how exact they have to be, the bound alone decides.
No kernel may reach another device: no remote copies, remote signals or barrier semaphores. Data moves between devices by JAX's collectives and lax.ppermute only.
A program may use at most 64 MiB of HBM per device.

v0:
```python
import jax
import jax.numpy as jnp
from jax import lax
from jax.sharding import PartitionSpec as P

FAC_DEV = 32


TIME_STEP = 0.3


def padded(cells, sides, width):
    for axis, dim in sides:
        count = lax.axis_size(axis)
        ends = count - 1
        head = lax.slice_in_dim(cells, 0, width, axis=dim)
        tail = lax.slice_in_dim(cells, cells.shape[dim] - width, cells.shape[dim], axis=dim)
        cells = jnp.concatenate(
            [
                lax.ppermute(tail, axis, [(i, (i + 1) % count) for i in range(ends)]),
                cells,
                lax.ppermute(head, axis, [((i + 1) % count, i) for i in range(ends)]),
            ],
            axis=dim,
        )
    return cells


def shifted(block, axis, distance):
    devices = range(lax.axis_size(axis))
    route = [((i - distance) % len(devices), i) for i in devices]
    return lax.ppermute(block, axis, route)


def trimmed(field, axis_k, offset):
    selector = [slice(None)] * field.ndim
    for j in range(3):
        dim = field.ndim - 3 + j
        length = field.shape[dim]
        if j == axis_k:
            selector[dim] = slice(1 + offset, length - 1 + offset)
        else:
            selector[dim] = slice(1, length - 1)
    return field[tuple(selector)]


def interior(field):
    return trimmed(field, 0, 0)


def central_diff(field, axis_k):
    return 0.5 * (trimmed(field, axis_k, 1) - trimmed(field, axis_k, -1))


def tendency(state_pad, wind_pad, damping_pad):
    pressure = state_pad[0]
    damping = interior(damping_pad)
    result = []
    for index in range(4):
        component = state_pad[index]
        advection = (
            central_diff(wind_pad[0] * component, 0)
            + central_diff(wind_pad[1] * component, 1)
            + central_diff(wind_pad[2] * component, 2)
        )
        if index == 0:
            coupling = (
                central_diff(state_pad[1], 0)
                + central_diff(state_pad[2], 1)
                + central_diff(state_pad[3], 2)
            )
        else:
            coupling = central_diff(pressure, index - 1)
        result.append(advection + coupling - damping * interior(component))
    return jnp.stack(result)


def inside_line(position_index, count, length):
    position = position_index * length + jnp.arange(length + 2, dtype=jnp.int32) - 1
    return ((position >= 0) & (position < length * count)).astype(jnp.float32)


def owner_bucket(slot_names, slot_terms, offset):
    index_x = lax.axis_index("gx")
    index_y = lax.axis_index("gy")
    index_z = lax.axis_index("gz")
    count_x = lax.axis_size("gx")
    count_y = lax.axis_size("gy")
    count_z = lax.axis_size("gz")
    owner = ((index_x + offset + count_x) % count_x * count_y + index_y) * count_z + index_z
    targets = owner * FAC_DEV + jnp.arange(FAC_DEV, dtype=jnp.int32)
    return jnp.sum(
        jnp.where(slot_names[:, None] == targets[None, :], slot_terms[:, None], jnp.float32(0.0)),
        axis=0,
    )


def local(adjoint, saved_state, wind_field, facade_slot, facade_table, impedance):
    depth_z, depth_x, depth_y = facade_slot.shape
    slot_names = facade_table.reshape(-1)
    slot_count = slot_names.shape[0]
    local_damping = impedance[slot_names]
    levels = jnp.arange(1, slot_count + 1, dtype=jnp.int32)
    one_hot = (facade_slot[None] == levels[:, None, None, None]).astype(jnp.float32)
    damping = jnp.tensordot(local_damping, one_hot, axes=1, precision=lax.Precision.HIGHEST)
    static = jnp.concatenate([wind_field, damping[None]], axis=0)
    width = 2
    static_pad = padded(static, (("gx", 2), ("gy", 3), ("gz", 1)), width)
    upper = adjoint[0]
    middle = adjoint[1]
    products = jnp.zeros((depth_z, depth_x, depth_y), jnp.float32)
    step_count = saved_state.shape[0]
    line_z = inside_line(lax.axis_index("gz"), lax.axis_size("gz"), depth_z)
    line_x = inside_line(lax.axis_index("gx"), lax.axis_size("gx"), depth_x)
    line_y = inside_line(lax.axis_index("gy"), lax.axis_size("gy"), depth_y)
    inside = line_z[:, None, None] * line_x[None, :, None] * line_y[None, None, :]
    wind_inner = interior(static_pad[:3])
    damping_inner = interior(static_pad[3])
    for step in range(0, step_count, 2):
        stacked = padded(jnp.stack([upper, middle]), (("gx", 3), ("gy", 4), ("gz", 2)), 2)
        products = products + jnp.sum(middle * saved_state[step], axis=0)
        first_new = (
            interior(stacked[0])
            + 2.0 * TIME_STEP * tendency(stacked[1], static_pad[:3], static_pad[3])
        ) * inside
        first_core = interior(first_new)
        products = products + jnp.sum(first_core * saved_state[step + 1], axis=0)
        second_new = middle + 2.0 * TIME_STEP * tendency(first_new, wind_inner, damping_inner)
        upper, middle = (first_core, second_new)
    terms = -2.0 * TIME_STEP * products
    slot_terms = jnp.tensordot(one_hot, terms, axes=3, precision=lax.Precision.HIGHEST)
    own_part = owner_bucket(slot_names, slot_terms, 0)
    upward = owner_bucket(slot_names, slot_terms, 1)
    downward = owner_bucket(slot_names, slot_terms, -1)
    lower_part = shifted(upward, "gx", 1)
    upper_part = shifted(downward, "gx", -1)
    gradient = own_part + lower_part + upper_part
    return (jnp.stack([upper, middle]), gradient)


def solution(mesh):
    return jax.shard_map(
        local,
        mesh=mesh,
        in_specs=(
            P(None, None, "gz", "gx", "gy"),
            P(None, None, "gz", "gx", "gy"),
            P(None, "gz", "gx", "gy"),
            P("gz", "gx", "gy"),
            P("gz", "gx", "gy", None),
            P(),
        ),
        out_specs=(P(None, None, "gz", "gx", "gy"), P(("gx", "gy", "gz"))),
        check_vma=False,
    )
```

profile of v0, /device:TPU:0, one launch (start us, length us, event | category | flops | bytes accessed | tf_op | source)
XLA Modules:
  0.0 107.5 jit_solution(7380261531197359499)
XLA Ops:
  0.7 0.7 fusion.165
  1.4 1.1 %broadcast_compare_fusion = pred[64,8,8,128]{3,2,1,0:T(8,128)(4,1)S(1)} fusion(s32[8,8,128]{2,1,0:T(8,128)} %param.9, s32[64]{0:T(128)S(1)} %iota_add_fusion.3), kind=kLoop, calls=%fused_computation.8 | loop fusion | flops 524288 | bytes 557312 | tf_op jit(solution)/shard_map/eq | solution.py:104
  2.5 0.7 gather_fusion
  3.3 0.7 fusion.2
  4.0 2.4 %collective-permute-start.6 = (f32[4,8,2,128]{3,2,1,0:T(2,128)S(1)}, f32[4,8,2,128]{3,2,1,0:T(2,128)S(1)}, u32[]{:S(2)}, u32[]{:S(2)}) collective-permute-start(f32[4,8,2,128]{3,2,1,0:T(2,128)S(1)} %get-tuple-element.100), channel_id=1, source_target_pairs={{0,4},{4,8},{8,12},{12,16},{16,20},{20,24},{24,28},{1,5},{5,9},{9,... | collective-permute-start | bytes 98312 | tf_op jit(solution)/shard_map/ppermute | solution.py:20
  6.4 1.3 %collective-permute-start.7 = (f32[4,8,2,128]{3,2,1,0:T(2,128)S(1)}, f32[4,8,2,128]{3,2,1,0:T(2,128)S(1)}, u32[]{:S(2)}, u32[]{:S(2)}) collective-permute-start(f32[4,8,2,128]{3,2,1,0:T(2,128)S(1)} %get-tuple-element.101), channel_id=1, source_target_pairs={{4,0},{8,4},{12,8},{16,12},{20,16},{24,20},{28,24},{5,1},{9,5},{13... | collective-permute-start | bytes 98312 | tf_op jit(solution)/shard_map/ppermute | solution.py:22
  7.7 5.2 %collective-permute-start = (f32[2,4,8,2,128]{4,3,2,1,0:T(2,128)S(1)}, f32[2,4,8,2,128]{4,3,2,1,0:T(2,128)S(1)}, u32[]{:S(2)}, u32[]{:S(2)}) collective-permute-start(f32[2,4,8,2,128]{4,3,2,1,0:T(2,128)S(1)} %get-tuple-element.98), channel_id=1, source_target_pairs={{0,4},{4,8},{8,12},{12,16},{16,20},{20,24},{24,28},{1,5},{5,9},{9,... | collective-permute-start | bytes 196616 | tf_op jit(solution)/shard_map/ppermute | solution.py:20
  13.0 1.3 %collective-permute-start.1 = (f32[2,4,8,2,128]{4,3,2,1,0:T(2,128)S(1)}, f32[2,4,8,2,128]{4,3,2,1,0:T(2,128)S(1)}, u32[]{:S(2)}, u32[]{:S(2)}) collective-permute-start(f32[2,4,8,2,128]{4,3,2,1,0:T(2,128)S(1)} %get-tuple-element.99), channel_id=1, source_target_pairs={{4,0},{8,4},{12,8},{16,12},{20,16},{24,20},{28,24},{5,1},{9,5},{13... | collective-permute-start | bytes 196616 | tf_op jit(solution)/shard_map/ppermute | solution.py:22
  14.7 3.4 %collective-permute-start.8 = (f32[4,8,12,2]{3,2,1,0:T(8,128)S(1)}, f32[4,8,12,2]{3,2,1,0:T(8,128)S(1)}, u32[]{:S(2)}, u32[]{:S(2)}) collective-permute-start(f32[4,8,12,2]{3,2,1,0:T(8,128)S(1)} %get-tuple-element.96), channel_id=1, source_target_pairs={{0,2},{1,3},{4,6},{5,7},{8,10},{9,11},{12,14},{13,15},{16,18},{17,... | collective-permute-start | bytes 9224 | tf_op jit(solution)/shard_map/ppermute | solution.py:20
  18.1 1.3 %collective-permute-start.9 = (f32[4,8,12,2]{3,2,1,0:T(8,128)S(1)}, f32[4,8,12,2]{3,2,1,0:T(8,128)S(1)}, u32[]{:S(2)}, u32[]{:S(2)}) collective-permute-start(f32[4,8,12,2]{3,2,1,0:T(8,128)S(1)} %get-tuple-element.97), channel_id=1, source_target_pairs={{2,0},{3,1},{6,4},{7,5},{10,8},{11,9},{14,12},{15,13},{18,16},{19,... | collective-permute-start | bytes 9224 | tf_op jit(solution)/shard_map/ppermute | solution.py:22
  19.8 4.6 %collective-permute-start.2 = (f32[2,4,8,12,2]{4,3,2,1,0:T(8,128)S(1)}, f32[2,4,8,12,2]{4,3,2,1,0:T(8,128)S(1)}, u32[]{:S(2)}, u32[]{:S(2)}) collective-permute-start(f32[2,4,8,12,2]{4,3,2,1,0:T(8,128)S(1)} %get-tuple-element.92), channel_id=1, source_target_pairs={{0,2},{1,3},{4,6},{5,7},{8,10},{9,11},{12,14},{13,15},{16,18},{17,... | collective-permute-start | bytes 18440 | tf_op jit(solution)/shard_map/ppermute | solution.py:20
  24.4 1.3 %collective-permute-start.3 = (f32[2,4,8,12,2]{4,3,2,1,0:T(8,128)S(1)}, f32[2,4,8,12,2]{4,3,2,1,0:T(8,128)S(1)}, u32[]{:S(2)}, u32[]{:S(2)}) collective-permute-start(f32[2,4,8,12,2]{4,3,2,1,0:T(8,128)S(1)} %get-tuple-element.93), channel_id=1, source_target_pairs={{2,0},{3,1},{6,4},{7,5},{10,8},{11,9},{14,12},{15,13},{18,16},{19,... | collective-permute-start | bytes 18440 | tf_op jit(solution)/shard_map/ppermute | solution.py:22
  25.7 2.4 %collective-permute-done.9 = f32[4,8,12,2]{3,2,1,0:T(8,128)S(1)} collective-permute-done((f32[4,8,12,2]{3,2,1,0:T(8,128)S(1)}, f32[4,8,12,2]{3,2,1,0:T(8,128)S(1)}, u32[]{:S(2)}, u32[]{:S(2)}) %collective-permute-start.9) | collective-permute-done | bytes 3104 | tf_op jit(solution)/shard_map/ppermute | solution.py:22
  28.3 3.4 %collective-permute-start.10 = (f32[4,2,12,132]{3,2,1,0:T(8,128)S(1)}, f32[4,2,12,132]{3,2,1,0:T(8,128)S(1)}, u32[]{:S(2)}, u32[]{:S(2)}) collective-permute-start(f32[4,2,12,132]{3,2,1,0:T(8,128)S(1)} %get-tuple-element.79), channel_id=1, source_target_pairs={{0,1},{2,3},{4,5},{6,7},{8,9},{10,11},{12,13},{14,15},{16,17},{18,... | collective-permute-start | bytes 152072 | tf_op jit(solution)/shard_map/ppermute | solution.py:20
  31.7 1.3 %collective-permute-start.11 = (f32[4,2,12,132]{3,2,1,0:T(8,128)S(1)}, f32[4,2,12,132]{3,2,1,0:T(8,128)S(1)}, u32[]{:S(2)}, u32[]{:S(2)}) collective-permute-start(f32[4,2,12,132]{3,2,1,0:T(8,128)S(1)} %get-tuple-element.80), channel_id=1, source_target_pairs={{1,0},{3,2},{5,4},{7,6},{9,8},{11,10},{13,12},{15,14},{17,16},{19,... | collective-permute-start | bytes 152072 | tf_op jit(solution)/shard_map/ppermute | solution.py:22
  33.0 2.7 %collective-permute-done.2 = f32[2,4,8,12,2]{4,3,2,1,0:T(8,128)S(1)} collective-permute-done((f32[2,4,8,12,2]{4,3,2,1,0:T(8,128)S(1)}, f32[2,4,8,12,2]{4,3,2,1,0:T(8,128)S(1)}, u32[]{:S(2)}, u32[]{:S(2)}) %collective-permute-start.2) | collective-permute-done | bytes 6176 | tf_op jit(solution)/shard_map/ppermute | solution.py:20
  35.8 4.7 %collective-permute-done.3 = f32[2,4,8,12,2]{4,3,2,1,0:T(8,128)S(1)} collective-permute-done((f32[2,4,8,12,2]{4,3,2,1,0:T(8,128)S(1)}, f32[2,4,8,12,2]{4,3,2,1,0:T(8,128)S(1)}, u32[]{:S(2)}, u32[]{:S(2)}) %collective-permute-start.3) | collective-permute-done | bytes 6176 | tf_op jit(solution)/shard_map/ppermute | solution.py:22
  40.9 3.4 %collective-permute-start.4 = (f32[2,4,2,12,132]{4,3,2,1,0:T(8,128)S(1)}, f32[2,4,2,12,132]{4,3,2,1,0:T(8,128)S(1)}, u32[]{:S(2)}, u32[]{:S(2)}) collective-permute-start(f32[2,4,2,12,132]{4,3,2,1,0:T(8,128)S(1)} %get-tuple-element.63), channel_id=1, source_target_pairs={{0,1},{2,3},{4,5},{6,7},{8,9},{10,11},{12,13},{14,15},{16,17},{18,... | collective-permute-start | bytes 304136 | tf_op jit(solution)/shard_map/ppermute | solution.py:20
  44.3 1.3 %collective-permute-start.5 = (f32[2,4,2,12,132]{4,3,2,1,0:T(8,128)S(1)}, f32[2,4,2,12,132]{4,3,2,1,0:T(8,128)S(1)}, u32[]{:S(2)}, u32[]{:S(2)}) collective-permute-start(f32[2,4,2,12,132]{4,3,2,1,0:T(8,128)S(1)} %get-tuple-element.64), channel_id=1, source_target_pairs={{1,0},{3,2},{5,4},{7,6},{9,8},{11,10},{13,12},{15,14},{17,16},{19,... | collective-permute-start | bytes 304136 | tf_op jit(solution)/shard_map/ppermute | solution.py:22
  46.1 4.3 %collective-permute-done.4 = f32[2,4,2,12,132]{4,3,2,1,0:T(8,128)S(1)} collective-permute-done((f32[2,4,2,12,132]{4,3,2,1,0:T(8,128)S(1)}, f32[2,4,2,12,132]{4,3,2,1,0:T(8,128)S(1)}, u32[]{:S(2)}, u32[]{:S(2)}) %collective-permute-start.4) | collective-permute-done | bytes 101408 | tf_op jit(solution)/shard_map/ppermute | solution.py:20
  50.4 4.1 %collective-permute-done.5 = f32[2,4,2,12,132]{4,3,2,1,0:T(8,128)S(1)} collective-permute-done((f32[2,4,2,12,132]{4,3,2,1,0:T(8,128)S(1)}, f32[2,4,2,12,132]{4,3,2,1,0:T(8,128)S(1)}, u32[]{:S(2)}, u32[]{:S(2)}) %collective-permute-start.5) | collective-permute-done | bytes 101408 | tf_op jit(solution)/shard_map/ppermute | solution.py:22
  54.5 0.8 pad_maximum_fusion
  56.1 0.6 fusion.54
  56.7 0.5 fusion.48
  57.1 0.5 fusion.42
  57.6 0.4 fusion.36
  60.2 1.3 %collective-permute-start.12 = (f32[2,4,8,2,128]{4,3,2,1,0:T(2,128)S(1)}, f32[2,4,8,2,128]{4,3,2,1,0:T(2,128)S(1)}, u32[]{:S(2)}, u32[]{:S(2)}) collective-permute-start(f32[2,4,8,2,128]{4,3,2,1,0:T(2,128)S(1)} %get-tuple-element.94), channel_id=1, source_target_pairs={{0,4},{4,8},{8,12},{12,16},{16,20},{20,24},{24,28},{1,5},{5,9},{9,... | collective-permute-start | bytes 196616 | tf_op jit(solution)/shard_map/ppermute | solution.py:20
  61.5 1.3 %collective-permute-start.13 = (f32[2,4,8,2,128]{4,3,2,1,0:T(2,128)S(1)}, f32[2,4,8,2,128]{4,3,2,1,0:T(2,128)S(1)}, u32[]{:S(2)}, u32[]{:S(2)}) collective-permute-start(f32[2,4,8,2,128]{4,3,2,1,0:T(2,128)S(1)} %get-tuple-element.95), channel_id=1, source_target_pairs={{4,0},{8,4},{12,8},{16,12},{20,16},{24,20},{28,24},{5,1},{9,5},{13... | collective-permute-start | bytes 196616 | tf_op jit(solution)/shard_map/ppermute | solution.py:22
  62.8 2.8 %collective-permute-done.13 = f32[2,4,8,2,128]{4,3,2,1,0:T(2,128)S(1)} collective-permute-done((f32[2,4,8,2,128]{4,3,2,1,0:T(2,128)S(1)}, f32[2,4,8,2,128]{4,3,2,1,0:T(2,128)S(1)}, u32[]{:S(2)}, u32[]{:S(2)}) %collective-permute-start.13) | collective-permute-done | bytes 65568 | tf_op jit(solution)/shard_map/ppermute | solution.py:22
  65.7 1.2 %fusion.167 = (f32[2,4,8,12,2]{4,3,2,1,0:T(8,128)}, f32[2,4,8,12,2]{4,3,2,1,0:T(8,128)}) fusion(f32[2,4,8,12,128]{4,3,2,1,0:T(8,128)S(1)} %pad_maximum_fusion.4), kind=kLoop, calls=%fused_computation.336 | loop fusion | bytes 24576 | tf_op jit(solution)/shard_map/slice | solution.py:17
  66.9 1.5 %collective-permute-start.14 = (f32[2,4,8,12,2]{4,3,2,1,0:T(8,128)}, f32[2,4,8,12,2]{4,3,2,1,0:T(8,128)S(1)}, u32[]{:S(2)}, u32[]{:S(2)}) collective-permute-start(f32[2,4,8,12,2]{4,3,2,1,0:T(8,128)} %get-tuple-element.90), channel_id=1, source_target_pairs={{0,2},{1,3},{4,6},{5,7},{8,10},{9,11},{12,14},{13,15},{16,18},{17,... | collective-permute-start | bytes 18440 | tf_op jit(solution)/shard_map/ppermute | solution.py:20
  68.4 1.3 %collective-permute-start.15 = (f32[2,4,8,12,2]{4,3,2,1,0:T(8,128)}, f32[2,4,8,12,2]{4,3,2,1,0:T(8,128)S(1)}, u32[]{:S(2)}, u32[]{:S(2)}) collective-permute-start(f32[2,4,8,12,2]{4,3,2,1,0:T(8,128)} %get-tuple-element.91), channel_id=1, source_target_pairs={{2,0},{3,1},{6,4},{7,5},{10,8},{11,9},{14,12},{15,13},{18,16},{19,... | collective-permute-start | bytes 18440 | tf_op jit(solution)/shard_map/ppermute | solution.py:22
  69.7 9.2 %collective-permute-done.14 = f32[2,4,8,12,2]{4,3,2,1,0:T(8,128)S(1)} collective-permute-done((f32[2,4,8,12,2]{4,3,2,1,0:T(8,128)}, f32[2,4,8,12,2]{4,3,2,1,0:T(8,128)S(1)}, u32[]{:S(2)}, u32[]{:S(2)}) %collective-permute-start.14) | collective-permute-done | bytes 6176 | tf_op jit(solution)/shard_map/ppermute | solution.py:20
  78.9 4.6 %collective-permute-done.15 = f32[2,4,8,12,2]{4,3,2,1,0:T(8,128)S(1)} collective-permute-done((f32[2,4,8,12,2]{4,3,2,1,0:T(8,128)}, f32[2,4,8,12,2]{4,3,2,1,0:T(8,128)S(1)}, u32[]{:S(2)}, u32[]{:S(2)}) %collective-permute-start.15) | collective-permute-done | bytes 6176 | tf_op jit(solution)/shard_map/ppermute | solution.py:22
  83.9 1.5 %collective-permute-start.16 = (f32[2,4,2,12,132]{4,3,2,1,0:T(8,128)S(1)}, f32[2,4,2,12,132]{4,3,2,1,0:T(8,128)S(1)}, u32[]{:S(2)}, u32[]{:S(2)}) collective-permute-start(f32[2,4,2,12,132]{4,3,2,1,0:T(8,128)S(1)} %get-tuple-element.49), channel_id=1, source_target_pairs={{0,1},{2,3},{4,5},{6,7},{8,9},{10,11},{12,13},{14,15},{16,17},{18,... | collective-permute-start | bytes 304136 | tf_op jit(solution)/shard_map/ppermute | solution.py:20
  85.3 1.5 %collective-permute-start.17 = (f32[2,4,2,12,132]{4,3,2,1,0:T(8,128)S(1)}, f32[2,4,2,12,132]{4,3,2,1,0:T(8,128)S(1)}, u32[]{:S(2)}, u32[]{:S(2)}) collective-permute-start(f32[2,4,2,12,132]{4,3,2,1,0:T(8,128)S(1)} %get-tuple-element.50), channel_id=1, source_target_pairs={{1,0},{3,2},{5,4},{7,6},{9,8},{11,10},{13,12},{15,14},{17,16},{19,... | collective-permute-start | bytes 304136 | tf_op jit(solution)/shard_map/ppermute | solution.py:22
  86.8 4.4 %collective-permute-done.16 = f32[2,4,2,12,132]{4,3,2,1,0:T(8,128)S(1)} collective-permute-done((f32[2,4,2,12,132]{4,3,2,1,0:T(8,128)S(1)}, f32[2,4,2,12,132]{4,3,2,1,0:T(8,128)S(1)}, u32[]{:S(2)}, u32[]{:S(2)}) %collective-permute-start.16) | collective-permute-done | bytes 101408 | tf_op jit(solution)/shard_map/ppermute | solution.py:20
  91.2 4.7 %collective-permute-done.17 = f32[2,4,2,12,132]{4,3,2,1,0:T(8,128)S(1)} collective-permute-done((f32[2,4,2,12,132]{4,3,2,1,0:T(8,128)S(1)}, f32[2,4,2,12,132]{4,3,2,1,0:T(8,128)S(1)}, u32[]{:S(2)}, u32[]{:S(2)}) %collective-permute-start.17) | collective-permute-done | bytes 101408 | tf_op jit(solution)/shard_map/ppermute | solution.py:22
  95.9 0.8 pad_maximum_fusion.1
  97.0 0.5 fusion.22
  97.5 0.5 fusion.16
  98.0 0.6 fusion.28
  98.6 0.4 fusion.10
  99.7 0.8 copy-done.5
  100.8 1.0 fusion.4
  102.3 3.2 %collective-permute-start.19 = (f32[32]{0:T(128)S(1)}, f32[32]{0:T(128)S(1)}, u32[]{:S(2)}, u32[]{:S(2)}) collective-permute-start(f32[32]{0:T(128)S(1)} %get-tuple-element.7), channel_id=1, source_target_pairs={{4,0},{8,4},{12,8},{16,12},{20,16},{24,20},{28,24},{0,28},{5,1},{9... | collective-permute-start | bytes 392 | tf_op jit(solution)/shard_map/ppermute | solution.py:32
  106.3 0.7 pad_maximum_fusion.17
  107.0 0.5 add_add_fusion
  (87 shorter events, 7.7 us)
Async XLA Ops:
  0.6 1.9 %copy-start = (f32[1024]{0:T(1024)S(1)}, f32[1024]{0:T(1024)}, u32[]{:S(2)}) copy-start(f32[1024]{0:T(1024)} %param.11) | copy-start | bytes 12292
  0.6 3.3 %copy-start.2 = (f32[3,8,8,128]{3,2,1,0:T(8,128)S(1)}, f32[3,8,8,128]{3,2,1,0:T(8,128)}, u32[]{:S(2)}) copy-start(f32[3,8,8,128]{3,2,1,0:T(8,128)} %param.8) | copy-start | bytes 294916
  0.7 7.0 %copy-start.1 = (f32[2,4,8,8,128]{4,3,2,1,0:T(8,128)S(1)}, f32[2,4,8,8,128]{4,3,2,1,0:T(8,128)}, u32[]{:S(2)}) copy-start(f32[2,4,8,8,128]{4,3,2,1,0:T(8,128)} %param.6) | copy-start | bytes 786436
  2.5 11.9 %copy-start.3 = (pred[64,8,8,128]{3,2,1,0:T(8,128)(4,1)}, pred[64,8,8,128]{3,2,1,0:T(8,128)(4,1)S(1)}, u32[]{:S(2)}) copy-start(pred[64,8,8,128]{3,2,1,0:T(8,128)(4,1)S(1)} %broadcast_compare_fusion) | copy-start | bytes 1572868
  4.0 10.5 %collective-permute-start.6 = (f32[4,8,2,128]{3,2,1,0:T(2,128)S(1)}, f32[4,8,2,128]{3,2,1,0:T(2,128)S(1)}, u32[]{:S(2)}, u32[]{:S(2)}) collective-permute-start(f32[4,8,2,128]{3,2,1,0:T(2,128)S(1)} %get-tuple-element.100), channel_id=1, source_target_pairs={{0,4},{4,8},{8,12},{12,16},{16,20},{20,24},{24,28},{1,5},{5,9},{9,... | collective-permute-start | bytes 98312 | tf_op jit(solution)/shard_map/ppermute | solution.py:20
  6.4 8.1 %collective-permute-start.7 = (f32[4,8,2,128]{3,2,1,0:T(2,128)S(1)}, f32[4,8,2,128]{3,2,1,0:T(2,128)S(1)}, u32[]{:S(2)}, u32[]{:S(2)}) collective-permute-start(f32[4,8,2,128]{3,2,1,0:T(2,128)S(1)} %get-tuple-element.101), channel_id=1, source_target_pairs={{4,0},{8,4},{12,8},{16,12},{20,16},{24,20},{28,24},{5,1},{9,5},{13... | collective-permute-start | bytes 98312 | tf_op jit(solution)/shard_map/ppermute | solution.py:22
  7.7 11.7 %collective-permute-start = (f32[2,4,8,2,128]{4,3,2,1,0:T(2,128)S(1)}, f32[2,4,8,2,128]{4,3,2,1,0:T(2,128)S(1)}, u32[]{:S(2)}, u32[]{:S(2)}) collective-permute-start(f32[2,4,8,2,128]{4,3,2,1,0:T(2,128)S(1)} %get-tuple-element.98), channel_id=1, source_target_pairs={{0,4},{4,8},{8,12},{12,16},{16,20},{20,24},{24,28},{1,5},{5,9},{9,... | collective-permute-start | bytes 196616 | tf_op jit(solution)/shard_map/ppermute | solution.py:20
  13.0 6.5 %collective-permute-start.1 = (f32[2,4,8,2,128]{4,3,2,1,0:T(2,128)S(1)}, f32[2,4,8,2,128]{4,3,2,1,0:T(2,128)S(1)}, u32[]{:S(2)}, u32[]{:S(2)}) collective-permute-start(f32[2,4,8,2,128]{4,3,2,1,0:T(2,128)S(1)} %get-tuple-element.99), channel_id=1, source_target_pairs={{4,0},{8,4},{12,8},{16,12},{20,16},{24,20},{28,24},{5,1},{9,5},{13... | collective-permute-start | bytes 196616 | tf_op jit(solution)/shard_map/ppermute | solution.py:22
  14.7 11.0 %collective-permute-start.8 = (f32[4,8,12,2]{3,2,1,0:T(8,128)S(1)}, f32[4,8,12,2]{3,2,1,0:T(8,128)S(1)}, u32[]{:S(2)}, u32[]{:S(2)}) collective-permute-start(f32[4,8,12,2]{3,2,1,0:T(8,128)S(1)} %get-tuple-element.96), channel_id=1, source_target_pairs={{0,2},{1,3},{4,6},{5,7},{8,10},{9,11},{12,14},{13,15},{16,18},{17,... | collective-permute-start | bytes 9224 | tf_op jit(solution)/shard_map/ppermute | solution.py:20
  18.1 10.0 %collective-permute-start.9 = (f32[4,8,12,2]{3,2,1,0:T(8,128)S(1)}, f32[4,8,12,2]{3,2,1,0:T(8,128)S(1)}, u32[]{:S(2)}, u32[]{:S(2)}) collective-permute-start(f32[4,8,12,2]{3,2,1,0:T(8,128)S(1)} %get-tuple-element.97), channel_id=1, source_target_pairs={{2,0},{3,1},{6,4},{7,5},{10,8},{11,9},{14,12},{15,13},{18,16},{19,... | collective-permute-start | bytes 9224 | tf_op jit(solution)/shard_map/ppermute | solution.py:22
  19.8 16.0 %collective-permute-start.2 = (f32[2,4,8,12,2]{4,3,2,1,0:T(8,128)S(1)}, f32[2,4,8,12,2]{4,3,2,1,0:T(8,128)S(1)}, u32[]{:S(2)}, u32[]{:S(2)}) collective-permute-start(f32[2,4,8,12,2]{4,3,2,1,0:T(8,128)S(1)} %get-tuple-element.92), channel_id=1, source_target_pairs={{0,2},{1,3},{4,6},{5,7},{8,10},{9,11},{12,14},{13,15},{16,18},{17,... | collective-permute-start | bytes 18440 | tf_op jit(solution)/shard_map/ppermute | solution.py:20
  24.4 16.1 %collective-permute-start.3 = (f32[2,4,8,12,2]{4,3,2,1,0:T(8,128)S(1)}, f32[2,4,8,12,2]{4,3,2,1,0:T(8,128)S(1)}, u32[]{:S(2)}, u32[]{:S(2)}) collective-permute-start(f32[2,4,8,12,2]{4,3,2,1,0:T(8,128)S(1)} %get-tuple-element.93), channel_id=1, source_target_pairs={{2,0},{3,1},{6,4},{7,5},{10,8},{11,9},{14,12},{15,13},{18,16},{19,... | collective-permute-start | bytes 18440 | tf_op jit(solution)/shard_map/ppermute | solution.py:22
  28.3 17.3 %collective-permute-start.10 = (f32[4,2,12,132]{3,2,1,0:T(8,128)S(1)}, f32[4,2,12,132]{3,2,1,0:T(8,128)S(1)}, u32[]{:S(2)}, u32[]{:S(2)}) collective-permute-start(f32[4,2,12,132]{3,2,1,0:T(8,128)S(1)} %get-tuple-element.79), channel_id=1, source_target_pairs={{0,1},{2,3},{4,5},{6,7},{8,9},{10,11},{12,13},{14,15},{16,17},{18,... | collective-permute-start | bytes 152072 | tf_op jit(solution)/shard_map/ppermute | solution.py:20
  31.7 13.9 %collective-permute-start.11 = (f32[4,2,12,132]{3,2,1,0:T(8,128)S(1)}, f32[4,2,12,132]{3,2,1,0:T(8,128)S(1)}, u32[]{:S(2)}, u32[]{:S(2)}) collective-permute-start(f32[4,2,12,132]{3,2,1,0:T(8,128)S(1)} %get-tuple-element.80), channel_id=1, source_target_pairs={{1,0},{3,2},{5,4},{7,6},{9,8},{11,10},{13,12},{15,14},{17,16},{19,... | collective-permute-start | bytes 152072 | tf_op jit(solution)/shard_map/ppermute | solution.py:22
  40.9 9.5 %collective-permute-start.4 = (f32[2,4,2,12,132]{4,3,2,1,0:T(8,128)S(1)}, f32[2,4,2,12,132]{4,3,2,1,0:T(8,128)S(1)}, u32[]{:S(2)}, u32[]{:S(2)}) collective-permute-start(f32[2,4,2,12,132]{4,3,2,1,0:T(8,128)S(1)} %get-tuple-element.63), channel_id=1, source_target_pairs={{0,1},{2,3},{4,5},{6,7},{8,9},{10,11},{12,13},{14,15},{16,17},{18,... | collective-permute-start | bytes 304136 | tf_op jit(solution)/shard_map/ppermute | solution.py:20
  44.3 10.2 %collective-permute-start.5 = (f32[2,4,2,12,132]{4,3,2,1,0:T(8,128)S(1)}, f32[2,4,2,12,132]{4,3,2,1,0:T(8,128)S(1)}, u32[]{:S(2)}, u32[]{:S(2)}) collective-permute-start(f32[2,4,2,12,132]{4,3,2,1,0:T(8,128)S(1)} %get-tuple-element.64), channel_id=1, source_target_pairs={{1,0},{3,2},{5,4},{7,6},{9,8},{11,10},{13,12},{15,14},{17,16},{19,... | collective-permute-start | bytes 304136 | tf_op jit(solution)/shard_map/ppermute | solution.py:22
  59.2 0.6 copy-start.6
  59.4 2.1 %copy-start.10 = (f32[8,8,128]{2,1,0:T(8,128)}, f32[8,8,128]{2,1,0:T(8,128)S(1)}, u32[]{:S(2)}) copy-start(f32[8,8,128]{2,1,0:T(8,128)S(1)} %fusion.158) | copy-start | bytes 98308
  59.6 0.6 copy-start.8
  60.2 2.6 %collective-permute-start.12 = (f32[2,4,8,2,128]{4,3,2,1,0:T(2,128)S(1)}, f32[2,4,8,2,128]{4,3,2,1,0:T(2,128)S(1)}, u32[]{:S(2)}, u32[]{:S(2)}) collective-permute-start(f32[2,4,8,2,128]{4,3,2,1,0:T(2,128)S(1)} %get-tuple-element.94), channel_id=1, source_target_pairs={{0,4},{4,8},{8,12},{12,16},{16,20},{20,24},{24,28},{1,5},{5,9},{9,... | collective-permute-start | bytes 196616 | tf_op jit(solution)/shard_map/ppermute | solution.py:20
  61.5 4.1 %collective-permute-start.13 = (f32[2,4,8,2,128]{4,3,2,1,0:T(2,128)S(1)}, f32[2,4,8,2,128]{4,3,2,1,0:T(2,128)S(1)}, u32[]{:S(2)}, u32[]{:S(2)}) collective-permute-start(f32[2,4,8,2,128]{4,3,2,1,0:T(2,128)S(1)} %get-tuple-element.95), channel_id=1, source_target_pairs={{4,0},{8,4},{12,8},{16,12},{20,16},{24,20},{28,24},{5,1},{9,5},{13... | collective-permute-start | bytes 196616 | tf_op jit(solution)/shard_map/ppermute | solution.py:22
  66.9 12.0 %collective-permute-start.14 = (f32[2,4,8,12,2]{4,3,2,1,0:T(8,128)}, f32[2,4,8,12,2]{4,3,2,1,0:T(8,128)S(1)}, u32[]{:S(2)}, u32[]{:S(2)}) collective-permute-start(f32[2,4,8,12,2]{4,3,2,1,0:T(8,128)} %get-tuple-element.90), channel_id=1, source_target_pairs={{0,2},{1,3},{4,6},{5,7},{8,10},{9,11},{12,14},{13,15},{16,18},{17,... | collective-permute-start | bytes 18440 | tf_op jit(solution)/shard_map/ppermute | solution.py:20
  68.4 15.1 %collective-permute-start.15 = (f32[2,4,8,12,2]{4,3,2,1,0:T(8,128)}, f32[2,4,8,12,2]{4,3,2,1,0:T(8,128)S(1)}, u32[]{:S(2)}, u32[]{:S(2)}) collective-permute-start(f32[2,4,8,12,2]{4,3,2,1,0:T(8,128)} %get-tuple-element.91), channel_id=1, source_target_pairs={{2,0},{3,1},{6,4},{7,5},{10,8},{11,9},{14,12},{15,13},{18,16},{19,... | collective-permute-start | bytes 18440 | tf_op jit(solution)/shard_map/ppermute | solution.py:22
  83.9 7.4 %collective-permute-start.16 = (f32[2,4,2,12,132]{4,3,2,1,0:T(8,128)S(1)}, f32[2,4,2,12,132]{4,3,2,1,0:T(8,128)S(1)}, u32[]{:S(2)}, u32[]{:S(2)}) collective-permute-start(f32[2,4,2,12,132]{4,3,2,1,0:T(8,128)S(1)} %get-tuple-element.49), channel_id=1, source_target_pairs={{0,1},{2,3},{4,5},{6,7},{8,9},{10,11},{12,13},{14,15},{16,17},{18,... | collective-permute-start | bytes 304136 | tf_op jit(solution)/shard_map/ppermute | solution.py:20
  85.3 10.6 %collective-permute-start.17 = (f32[2,4,2,12,132]{4,3,2,1,0:T(8,128)S(1)}, f32[2,4,2,12,132]{4,3,2,1,0:T(8,128)S(1)}, u32[]{:S(2)}, u32[]{:S(2)}) collective-permute-start(f32[2,4,2,12,132]{4,3,2,1,0:T(8,128)S(1)} %get-tuple-element.50), channel_id=1, source_target_pairs={{1,0},{3,2},{5,4},{7,6},{9,8},{11,10},{13,12},{15,14},{17,16},{19,... | collective-permute-start | bytes 304136 | tf_op jit(solution)/shard_map/ppermute | solution.py:22
  99.5 1.0 copy-start.5
  99.5 1.0 copy-start.7
  99.5 1.0 copy-start.9
  99.5 1.0 copy-start.11
  99.6 1.2 %copy-start.4 = (pred[64,8,8,128]{3,2,1,0:T(8,128)(4,1)S(1)}, pred[64,8,8,128]{3,2,1,0:T(8,128)(4,1)}, u32[]{:S(2)}) copy-start(pred[64,8,8,128]{3,2,1,0:T(8,128)(4,1)} %copy-done.3) | copy-start | bytes 1572868
  99.7 2.0 %copy-start.12 = (s32[1,1,1,64]{3,2,1,0:T(1,128)S(1)}, s32[1,1,1,64]{3,2,1,0:T(1,128)}, u32[]{:S(2)}) copy-start(s32[1,1,1,64]{3,2,1,0:T(1,128)} %param.10) | copy-start | bytes 772
  102.0 5.0 %collective-permute-start.18 = (f32[32]{0:T(128)S(1)}, f32[32]{0:T(128)S(1)}, u32[]{:S(2)}, u32[]{:S(2)}) collective-permute-start(f32[32]{0:T(128)S(1)} %get-tuple-element.6), channel_id=1, source_target_pairs={{28,0},{0,4},{4,8},{8,12},{12,16},{16,20},{20,24},{24,28},{29,1},{... | collective-permute-start | bytes 392 | tf_op jit(solution)/shard_map/ppermute | solution.py:32
  102.3 4.6 %collective-permute-start.19 = (f32[32]{0:T(128)S(1)}, f32[32]{0:T(128)S(1)}, u32[]{:S(2)}, u32[]{:S(2)}) collective-permute-start(f32[32]{0:T(128)S(1)} %get-tuple-element.7), channel_id=1, source_target_pairs={{4,0},{8,4},{12,8},{16,12},{20,16},{24,20},{28,24},{0,28},{5,1},{9... | collective-permute-start | bytes 392 | tf_op jit(solution)/shard_map/ppermute | solution.py:32
where the time goes:
time: 109 us; the launch traced here: 108 us
  waiting for transfers between devices  44 us (40%)
  starting transfers between devices  42.1 us (39%)
  other arithmetic  14.4 us (13%)
  local copies, waits for them, and re-layouts  4.05 us (4%)
  matrix products  1.63 us (1%)
  between operations  1.4 us (1%)
    ppermute x9, starting transfers between devices, padded(): lax.ppermute(tail, axis, [(i, (i + 1) % count) for i in range(ends)])  26.7 us
    ppermute x9, waiting for transfers between devices, padded(): lax.ppermute(head, axis, [((i + 1) % count, i) for i in range(ends)])  23.3 us
    ppermute x9, waiting for transfers between devices, padded(): lax.ppermute(tail, axis, [(i, (i + 1) % count) for i in range(ends)])  20.6 us
    ppermute x9, starting transfers between devices, padded(): lax.ppermute(head, axis, [((i + 1) % count, i) for i in range(ends)])  11.8 us
    another operation x12, other arithmetic, tendency(): return jnp.stack(result)  4.52 us
    ppermute x2, starting transfers between devices, shifted(): return lax.ppermute(block, axis, route)  3.59 us
    concatenate x6, other arithmetic, padded(): jnp.concatenate([lax.ppermute(tail, axis, [(i, (i + 1) % count) for i in...  2.19 us
  transfers between devices with their start and end apart: 20, of which 10 were waited for; matrix products, arithmetic and copies ran while one was open for 3% of the time, Pallas kernels for 0%

commit v1 on v0

v1 whole, which is shorter than its diff:
```python
import functools

import jax
import jax.numpy as jnp
from jax import lax
from jax.experimental import pallas as pl
from jax.experimental.pallas import tpu as pltpu
from jax.sharding import PartitionSpec as P

FAC_DEV = 32
TIME_STEP = 0.3
SCALE = 2.0 * TIME_STEP

FIELDS = 12
DEPTH = 4
Z_PLANES = [(f, t) for t in (1, 2, 3) for f in range(FIELDS)] + [(f, 4) for f in (0, 1, 2, 3, 8)]
D_PLANES = [(f, t) for t in (1, 2) for f in range(FIELDS)] + [(f, 3) for f in (0, 1, 2, 3, 8, 10)]
E_PLANES = [(f, t) for t in (1, 2) for f in range(FIELDS)] + [(f, 3) for f in (0, 1, 2, 3, 8, 9)]
GROUPS = 32


def z_of(s, depth_z):
    return jnp.where(lax.axis_index("gz") == 0, depth_z - 1 - s, s)


def own_planes(depth_z):
    return [(f, s) for f in range(FIELDS) for s in range(depth_z)]


def lane_iota():
    return lax.broadcasted_iota(jnp.int32, (8, 128), 1)


def row_iota():
    return lax.broadcasted_iota(jnp.int32, (8, 128), 0)


def pack_lanes(load, planes, send_high):
    lanes = lane_iota() // DEPTH
    packed = []
    for start in range(0, len(planes), GROUPS):
        row = jnp.zeros((8, 128), jnp.float32)
        for j, plane in enumerate(planes[start:start + GROUPS]):
            shift = lax.rem(DEPTH * j + jnp.where(send_high, DEPTH, 0), 128)
            row = jnp.where(lanes == j, pltpu.roll(load(*plane), shift, 1), row)
        packed.append(row)
    return packed


def pack_rows(first, second, send_high, rows):
    turned = pltpu.roll(second, 4, 0)
    low = jnp.where(rows < 4, first, turned)
    high = jnp.where(rows < 4, turned, first)
    return jnp.where(send_high, high, low)


def unpack_rows(got_a, got_b, even, rows):
    from_high = jnp.where(even, got_a, got_b)
    from_low = jnp.where(even, got_b, got_a)
    first = jnp.where(rows < 4, from_high, from_low)
    second = pltpu.roll(jnp.where(rows < 4, from_low, from_high), 4, 0)
    return first, second


def owner_of(offset):
    count_x, count_y, count_z = (lax.axis_size(a) for a in ("gx", "gy", "gz"))
    x = lax.rem(lax.axis_index("gx") + (offset + count_x), count_x)
    return (x * count_y + lax.axis_index("gy")) * count_z + lax.axis_index("gz")


def pack_kernel(sides, adjoint, wind, slots, table, impedance, *outs):
    damping, zb = outs[:2]
    ys = outs[2:2 + sides]
    ds = outs[2 + sides:2 + 2 * sides]
    xa, xb = outs[2 + 2 * sides:4 + 2 * sides]
    names = outs[4 + 2 * sides]
    depth_z = slots.shape[0]
    names[...] = jnp.zeros((8, 128), jnp.int32)
    names[:, :table.shape[1]] = jnp.broadcast_to(table[...], (8, table.shape[1]))
    ids = names[...]
    local = jnp.zeros((8, 128), jnp.float32)
    for offset in (-1, 0, 1):
        row = owner_of(offset) * FAC_DEV // 128
        values = jnp.broadcast_to(impedance[pl.ds(row, 1), :], (8, 128))
        local = jnp.where(ids // 128 == row, jnp.take_along_axis(values, ids % 128, axis=1), local)
    for z in range(depth_z):
        slot = slots[z]
        found = jnp.take_along_axis(local, jnp.maximum(slot - 1, 0), axis=1)
        damping[z] = jnp.where(slot > 0, found, 0.0)

    def load(f, s):
        z = z_of(s, depth_z)
        if f < 4:
            return adjoint[1, f, z]
        if f < 8:
            return adjoint[0, f - 4, z]
        if f < 11:
            return wind[f - 8, z]
        return damping[z]

    for i, (f, t) in enumerate(Z_PLANES):
        zb[i] = load(f, t - 1)
    even_y = lax.rem(lax.axis_index("gy"), 2) == 0
    for side in range(sides):
        send_high = even_y if side == 0 else jnp.logical_not(even_y)
        for i, row in enumerate(pack_lanes(load, own_planes(depth_z), send_high)):
            ys[side][i] = row
        for i, row in enumerate(pack_lanes(lambda f, t: load(f, t - 1), D_PLANES, send_high)):
            ds[side][i] = row
    even_x = lax.rem(lax.axis_index("gx"), 2) == 0
    rows = row_iota()
    planes = own_planes(depth_z)
    for i in range(len(planes) // 2):
        first, second = load(*planes[2 * i]), load(*planes[2 * i + 1])
        xa[i] = pack_rows(first, second, even_x, rows)
        xb[i] = pack_rows(first, second, jnp.logical_not(even_x), rows)


def edge_kernel(sides, zb, *rest):
    ys = rest[:sides]
    ds = rest[sides:2 * sides]
    xa, xb = rest[2 * sides:]
    loads = [functools.partial(lambda i: zb[i], Z_PLANES.index(p)) for p in E_PLANES]
    for ref in ys + ds:
        loads += [functools.partial(lambda ref, i: ref[i], ref, i) for i in range(ref.shape[0])]
    even_x = lax.rem(lax.axis_index("gx"), 2) == 0
    rows = row_iota()
    for i in range(len(loads) // 2):
        first, second = loads[2 * i](), loads[2 * i + 1]()
        xa[i] = pack_rows(first, second, even_x, rows)
        xb[i] = pack_rows(first, second, jnp.logical_not(even_x), rows)


def coupled(middle, c, k):
    if c == 0:
        return middle[1 + k]
    if c == 1 + k:
        return middle[0]
    return None


def flux(wind, middle, c, k):
    value = wind * middle[c]
    other = coupled(middle, c, k)
    return value if other is None else value + other


def step_kernel(sides, adjoint, wind, damping, saved, slots, table, zb, *rest):
    ys = rest[:sides]
    ds = rest[sides:2 * sides]
    oa, ob, ea, eb, out, own, part_a, part_b, cells, prod, acc = rest[2 * sides:]
    depth_z = slots.shape[0]
    rows, lanes = row_iota(), lane_iota()
    even_x = lax.rem(lax.axis_index("gx"), 2) == 0
    even_y = lax.rem(lax.axis_index("gy"), 2) == 0
    zero = jnp.zeros((8, 128), jnp.float32)
    far = DEPTH + depth_z

    def put(f, slot, tx, ty, value):
        cells[f, slot, 8 * tx:8 * tx + 8, 128 * ty:128 * ty + 128] = value

    for s in range(depth_z):
        z = z_of(s, depth_z)
        for f in range(4):
            put(f, DEPTH + s, 0, 0, adjoint[1, f, z])
            put(4 + f, DEPTH + s, 0, 0, adjoint[0, f, z])
        for f in range(3):
            put(8 + f, DEPTH + s, 0, 0, wind[f, z])
        put(11, DEPTH + s, 0, 0, damping[z])
    for i, (f, t) in enumerate(Z_PLANES):
        put(f, DEPTH - t, 0, 0, zb[i])
    planes = own_planes(depth_z)
    for i in range(len(planes) // 2):
        pair = unpack_rows(oa[i], ob[i], even_x, rows)
        for (f, s), value in zip(planes[2 * i:2 * i + 2], pair):
            put(f, DEPTH + s, 1, 0, value)
    edges = []
    for i in range(ea.shape[0]):
        edges += unpack_rows(ea[i], eb[i], even_x, rows)
    for (f, t), value in zip(E_PLANES, edges):
        put(f, DEPTH - t, 1, 0, value)
    edges = edges[len(E_PLANES):]
    packs = [ref[i] for ref in ys + ds for i in range(ref.shape[0])]
    y_rows = ys[0].shape[0]

    def spread(packed, j, side):
        high = even_y if side == 0 else jnp.logical_not(even_y)
        shift = lax.rem(256 - DEPTH * j - jnp.where(high, 0, DEPTH), 128)
        start = jnp.where(high, 0, 128 - DEPTH)
        return jnp.where((lanes >= start) & (lanes < start + DEPTH), pltpu.roll(packed, shift, 1), 0.0)

    def spread_all(index, j):
        for tx, source in ((0, packs), (1, edges)):
            value = spread(source[index(0)], j, 0)
            if sides > 1:
                value = value + spread(source[index(1)], j, 1)
            yield tx, value

    for i, (f, s) in enumerate(planes):
        for tx, value in spread_all(lambda side: side * y_rows + i // GROUPS, i % GROUPS):
            put(f, DEPTH + s, tx, 1, value)
    for i, (f, t) in enumerate(D_PLANES):
        for tx, value in spread_all(lambda side: sides * y_rows + side, i):
            put(f, DEPTH - t, tx, 1, value)
    for tx in range(2):
        for ty in range(2):
            for f in range(9):
                put(f, far, tx, ty, zero)
            if tx + ty:
                for f in (0, 1, 2, 3, 8):
                    put(f, 0, tx, ty, zero)
                for f in (4, 5, 6, 7, 9, 10, 11):
                    if not (f == 9 and ty == 0) and not (f == 10 and ty == 1):
                        put(f, 1, tx, ty, zero)

    grid_row = lax.broadcasted_iota(jnp.int32, (16, 256), 0)
    grid_lane = lax.broadcasted_iota(jnp.int32, (16, 256), 1)
    x, y = lax.axis_index("gx"), lax.axis_index("gy")
    row_end = jnp.where(x == lax.axis_size("gx") - 1, 8, 12)
    row_restart = jnp.where(x == 0, 16, 12)
    lane_end = jnp.where(y == lax.axis_size("gy") - 1, 128, 192)
    lane_restart = jnp.where(y == 0, 256, 192)
    inside = (grid_row < row_end) | (grid_row >= row_restart)
    inside &= (grid_lane < lane_end) | (grid_lane >= lane_restart)
    factor = jnp.where(inside, jnp.float32(0.5 * SCALE), 0.0)
    sign = jnp.where(lax.axis_index("gz") == 0, jnp.float32(-1.0), jnp.float32(1.0))

    def full_step(first, middle_at, upper_at):
        def body(slot, carry):
            middle = [cells[middle_at + c, slot] for c in range(4)]
            above = [cells[middle_at + c, slot + 1] for c in range(4)]
            below = [cells[middle_at + c, slot - 1] for c in range(4)]
            wind_up, wind_down = cells[8, slot + 1], cells[8, slot - 1]
            wind_x, wind_y = cells[9, slot], cells[10, slot]
            loss = SCALE * cells[11, slot]
            for c in range(4):
                total = sign * (flux(wind_up, above, c, 0) - flux(wind_down, below, c, 0))
                along = flux(wind_x, middle, c, 1)
                total += pltpu.roll(along, 15, 0) - pltpu.roll(along, 1, 0)
                along = flux(wind_y, middle, c, 2)
                total += pltpu.roll(along, 255, 1) - pltpu.roll(along, 1, 1)
                cells[upper_at + c, slot] = cells[upper_at + c, slot] + factor * total - loss * middle[c]
            return carry

        lax.fori_loop(first, far, body, 0)

    def last_step(middle_at, upper_at):
        def body(s, carry):
            slot = DEPTH + s
            own_part = (slice(0, 8), slice(0, 128))
            middle = [cells[(middle_at + c, slot) + own_part] for c in range(4)]
            above = [cells[(middle_at + c, slot + 1) + own_part] for c in range(4)]
            below = [cells[(middle_at + c, slot - 1) + own_part] for c in range(4)]
            mid_x = [cells[middle_at + c, slot, :, 0:128] for c in range(4)]
            mid_y = [cells[middle_at + c, slot, 0:8, :] for c in range(4)]
            wind_up, wind_down = cells[(8, slot + 1) + own_part], cells[(8, slot - 1) + own_part]
            wind_x, wind_y = cells[9, slot, :, 0:128], cells[10, slot, 0:8, :]
            loss = SCALE * cells[(11, slot) + own_part]
            z = z_of(s, depth_z)
            for c in range(4):
                total = sign * (flux(wind_up, above, c, 0) - flux(wind_down, below, c, 0))
                along = flux(wind_x, mid_x, c, 1)
                total += (pltpu.roll(along, 15, 0) - pltpu.roll(along, 1, 0))[0:8]
                along = flux(wind_y, mid_y, c, 2)
                total += (pltpu.roll(along, 255, 1) - pltpu.roll(along, 1, 1))[:, 0:128]
                upper = cells[(upper_at + c, slot) + own_part]
                out[0, c, z] = middle[c]
                out[1, c, z] = upper + jnp.float32(0.5 * SCALE) * total - loss * middle[c]
            return carry

        lax.fori_loop(0, depth_z, body, 0)

    def products(step, middle_at, slot, z):
        return sum(cells[middle_at + c, slot, 0:8, 0:128] * saved[step, c, z] for c in range(4))

    full_step(1, 0, 4)
    for s in range(depth_z):
        z = z_of(s, depth_z)
        prod[z] = products(0, 0, DEPTH + s, z) + products(1, 4, DEPTH + s, z)
    full_step(2, 4, 0)
    full_step(3, 0, 4)
    for s in range(depth_z):
        z = z_of(s, depth_z)
        prod[z] = -SCALE * (prod[z] + (products(2, 0, DEPTH + s, z) + products(3, 4, DEPTH + s, z)))
    last_step(4, 0)

    slot_count = table.shape[1]
    level = lax.broadcasted_iota(jnp.int32, (slot_count, 128), 0) + 1
    acc[...] = jnp.zeros((slot_count, 128), jnp.float32)

    def by_slot(z, carry):
        total = acc[...]
        for row in range(8):
            cell_slot = jnp.broadcast_to(slots[z, row:row + 1, :], (slot_count, 128))
            term = jnp.broadcast_to(prod[z, row:row + 1, :], (slot_count, 128))
            total = total + jnp.where(cell_slot == level, term, 0.0)
        acc[...] = total
        return carry

    lax.fori_loop(0, depth_z, by_slot, 0)
    slot_terms = jnp.sum(acc[...], axis=1, keepdims=True)
    names = jnp.broadcast_to(table[...], (slot_count, slot_count))
    diagonal = lax.broadcasted_iota(jnp.int32, (slot_count, slot_count), 0) == lax.broadcasted_iota(
        jnp.int32, (slot_count, slot_count), 1
    )
    column = jnp.sum(jnp.where(diagonal, names, 0).astype(jnp.float32), axis=1, keepdims=True)
    lane = lax.broadcasted_iota(jnp.int32, (slot_count, 128), 1)

    def bucket(offset):
        target = jnp.where(lane < FAC_DEV, owner_of(offset) * FAC_DEV + lane, -1).astype(jnp.float32)
        return jnp.sum(jnp.where(column == target, slot_terms, 0.0), axis=0, keepdims=True)

    upward, downward = bucket(1), bucket(-1)
    own[...] = bucket(0)
    part_a[...] = jnp.where(even_x, upward, downward)
    part_b[...] = jnp.where(even_x, downward, upward)


def swap_a(block, axis):
    return lax.ppermute(block, axis, [(i, i ^ 1) for i in range(lax.axis_size(axis))])


def swap_b(block, axis, wrap=False):
    count = lax.axis_size(axis)
    pairs = [(i, (i + 1 if i % 2 else i - 1) % count) for i in range(count)]
    if not wrap:
        pairs = pairs[1:-1]
    return lax.ppermute(block, axis, pairs)


def swap_diagonal(block, side):
    count_y, count_z = lax.axis_size("gy"), lax.axis_size("gz")
    pairs = []
    for y in range(count_y):
        step = 1 if (y % 2 == 0) == (side == 0) else -1
        if 0 <= y + step < count_y:
            pairs += [(y * count_z + z, (y + step) * count_z + (z ^ 1)) for z in range(count_z)]
    return lax.ppermute(block, ("gy", "gz"), pairs)


def vmem(count):
    return [pl.BlockSpec(memory_space=pltpu.VMEM)] * count


def rows_of(count):
    return jax.ShapeDtypeStruct((count, 8, 128), jnp.float32)


def local(adjoint, saved_state, wind_field, facade_slot, facade_table, impedance):
    depth_z = facade_slot.shape[0]
    sides = 1 if lax.axis_size("gy") == 2 else 2
    table = facade_table.reshape(1, -1)
    rates = impedance.reshape(-1, 128)
    own_count = FIELDS * depth_z
    y_rows = -(-own_count // GROUPS)
    packed = pl.pallas_call(
        functools.partial(pack_kernel, sides),
        out_shape=[rows_of(depth_z), rows_of(len(Z_PLANES))]
        + [rows_of(y_rows)] * sides
        + [rows_of(1)] * sides
        + [rows_of(own_count // 2)] * 2,
        in_specs=vmem(5),
        out_specs=vmem(4 + 2 * sides),
        scratch_shapes=[pltpu.VMEM((8, 128), jnp.int32)],
        name="pack",
    )(adjoint, wind_field, facade_slot, table, rates)
    damping, zb = packed[:2]
    ys, ds = packed[2:2 + sides], packed[2 + sides:2 + 2 * sides]
    xa, xb = packed[2 + 2 * sides:]
    with jax.named_scope("z_swap"):
        zb = swap_a(zb, "gz")
    with jax.named_scope("y_swap"):
        ys = [swap_a(b, "gy") if side == 0 else swap_b(b, "gy") for side, b in enumerate(ys)]
    with jax.named_scope("d_swap"):
        ds = [swap_diagonal(b, side) for side, b in enumerate(ds)]
    with jax.named_scope("x_swap"):
        xb = swap_b(xb, "gx")
        xa = swap_a(xa, "gx")
    edge_count = (len(E_PLANES) + sides * (y_rows + 1)) // 2
    ea, eb = pl.pallas_call(
        functools.partial(edge_kernel, sides),
        out_shape=[rows_of(edge_count)] * 2,
        in_specs=vmem(1 + 2 * sides),
        out_specs=vmem(2),
        name="edges",
    )(zb, *ys, *ds)
    with jax.named_scope("e_swap"):
        eb = swap_b(eb, "gx")
        ea = swap_a(ea, "gx")
    slot_count = table.shape[1]
    row = jax.ShapeDtypeStruct((1, 128), jnp.float32)
    out, own, part_a, part_b = pl.pallas_call(
        functools.partial(step_kernel, sides),
        out_shape=[jax.ShapeDtypeStruct(adjoint.shape, jnp.float32), row, row, row],
        in_specs=vmem(11 + 2 * sides),
        out_specs=vmem(4),
        scratch_shapes=[
            pltpu.VMEM((FIELDS, DEPTH + depth_z + 1, 16, 256), jnp.float32),
            pltpu.VMEM((depth_z, 8, 128), jnp.float32),
            pltpu.VMEM((slot_count, 128), jnp.float32),
        ],
        name="steps",
    )(adjoint, wind_field, damping, saved_state, facade_slot, table, zb, *ys, *ds, xa, xb, ea, eb)
    with jax.named_scope("g_swap"):
        part_b = swap_b(part_b, "gx", wrap=True)
        part_a = swap_a(part_a, "gx")
    gradient = (own + part_a + part_b)[0, :FAC_DEV]
    return out, gradient


def solution(mesh):
    return jax.shard_map(
        local,
        mesh=mesh,
        in_specs=(
            P(None, None, "gz", "gx", "gy"),
            P(None, None, "gz", "gx", "gy"),
            P(None, "gz", "gx", "gy"),
            P("gz", "gx", "gy"),
            P("gz", "gx", "gy", None),
            P(),
        ),
        out_specs=(P(None, None, "gz", "gx", "gy"), P(("gx", "gy", "gz"))),
        check_vma=False,
    )
```

time: 109 us -> 37.1 us (0.34); the launches traced: 108 us -> 36.9 us
  waiting for transfers between devices: 44 us -> 6.17 us
  starting transfers between devices: 42.1 us -> 16.1 us
  other arithmetic: 14.4 us -> 0.01 us
  Pallas kernels: 0 us -> 10.8 us
  matrix products: 1.63 us -> 0 us
    ppermute x20 -> x9, waiting for transfers between devices: 44 us -> 6.17 us  [the longest x1 4.45 us: swap_diagonal(): return lax.ppermute(block, ('gy', 'gz'), pairs)]
    ppermute x20 -> x9, starting transfers between devices: 42.1 us -> 16.1 us  [the longest x5 11 us: swap_a(): lax.ppermute(block, axis, [(i, i ^ 1) for i in range(lax.axis_size(axis))])]
    pallas_call x0 -> x3, Pallas kernels: none -> 10.8 us  [the longest x1 7.04 us: local(): pl.pallas_call(functools.partial(step_kernel, sides), out_shape=[jax.Shap...]
    another operation x13 -> x0, other arithmetic: 5.25 us -> none  [the longest x12 4.52 us: tendency(): return jnp.stack(result)]
    mul x14 -> x0, other arithmetic: 2.36 us -> none  [the longest x7 1.29 us: tendency(): wind_pad[0] * component]
    concatenate x6 -> x0, other arithmetic: 2.19 us -> none  [padded(): jnp.concatenate([lax.ppermute(tail, axis, [(i, (i + 1) % count) for i in...]
    dot_general x2 -> x0, matrix products: 1.63 us -> none  [the longest x1 0.97 us: local(): jnp.tensordot(one_hot, terms, axes=3, precision=lax.Precision.HIGHEST)]
    slice x4 -> x0, local copies, waits for them, and re-layouts: 1.55 us -> none  [padded(): lax.slice_in_dim(cells, cells.shape[dim] - width, cells.shape[dim], axis=...]
  transfers between devices with their start and end apart: 20 -> 9, of which waited for: 10 -> 3; matrix products, arithmetic and copies ran while one was open for 3% -> 0% of each run, Pallas kernels for 0% -> 4%
where the time goes in v1:
time: 37.1 us; the launch traced here: 36.9 us
  starting transfers between devices  16.1 us (43%)
  Pallas kernels  10.8 us (29%)
  waiting for transfers between devices  6.17 us (17%)
  local copies, waits for them, and re-layouts  3.11 us (8%)
  between operations  0.7 us (2%)
    ppermute x5, starting transfers between devices, swap_a(): lax.ppermute(block, axis, [(i, i ^ 1) for i in range(lax.axis_size(axis))])  11 us
    pallas_call x1, Pallas kernels, local(): pl.pallas_call(functools.partial(step_kernel, sides), out_shape=[jax.Shap...  7.04 us
    ppermute x3, starting transfers between devices, swap_b(): return lax.ppermute(block, axis, pairs)  5.07 us
    ppermute x1, waiting for transfers between devices, swap_diagonal(): return lax.ppermute(block, ('gy', 'gz'), pairs)  4.45 us
    unnamed x22, local copies, waits for them, and re-layouts  2.6 us
    pallas_call x1, Pallas kernels, local(): pl.pallas_call(functools.partial(pack_kernel, sides), out_shape=[rows_of(...  2.1 us
    pallas_call x1, Pallas kernels, local(): pl.pallas_call(functools.partial(edge_kernel, sides), out_shape=[rows_of(...  1.62 us
    ppermute x3, waiting for transfers between devices, swap_b(): return lax.ppermute(block, axis, pairs)  1.3 us
  transfers between devices with their start and end apart: 9, of which 3 were waited for; matrix products, arithmetic and copies ran while one was open for 0% of the time, Pallas kernels for 4%

profile of v1, /device:TPU:0, one launch (start us, length us, event | category | flops | bytes accessed | tf_op | source)
XLA Modules:
  0.0 36.9 jit_solution(7027312346160984649)
XLA Ops:
  0.6 2.1 %pack.1 = (f32[8,8,128]{2,1,0:T(8,128)}, f32[41,8,128]{2,1,0:T(8,128)}, f32[3,8,128]{2,1,0:T(8,128)}, f32[1,8,128]{2,1,0:T(8,128)}, f32[48,8,128]{2,1,0:T(8,128)}, /*index=5*/f32[48,8,128]{2,1,0:T(8,128)}) custom-call(f32[2,4,8,8,128]{4,3,2,1,0:T(8,128)} %adjoint.3, f32[3,8,8,128]{3,2,1,0:T(8,128)} %wind.3, s32[8,8,128]{2,1,0:T(8,128)} %slots.3, ...), custom_call_target="tpu_custom_call" | custom-call | tf_op jit(solution)/shard_map/pack/pallas_call | solution.py:356
  2.7 0.0 copy-start.8
  2.7 3.0 %collective-permute-start = (f32[41,8,128]{2,1,0:T(8,128)}, f32[41,8,128]{2,1,0:T(8,128)S(1)}, u32[]{:S(2)}, u32[]{:S(2)}) collective-permute-start(f32[41,8,128]{2,1,0:T(8,128)} %get-tuple-element.15), channel_id=1, source_target_pairs={{0,1},{1,0},{2,3},{3,2},{4,5},{5,4},{6,7},{7,6},{8,9},{9,8},{10,11... | collective-permute-start | bytes 503816 | tf_op jit(solution)/shard_map/z_swap/ppermute | solution.py:320
  5.7 0.0 collective-permute-start.3
  5.7 0.7 %collective-permute-start.4 = (f32[48,8,128]{2,1,0:T(8,128)}, f32[48,8,128]{2,1,0:T(8,128)S(1)}, u32[]{:S(2)}, u32[]{:S(2)}) collective-permute-start(f32[48,8,128]{2,1,0:T(8,128)} %get-tuple-element.19), channel_id=1, source_target_pairs={{4,8},{8,4},{12,16},{16,12},{20,24},{24,20},{5,9},{9,5},{13,17},{1... | collective-permute-start | bytes 589832 | tf_op jit(solution)/shard_map/x_swap/ppermute | solution.py:328
  6.4 1.6 %collective-permute-start.1 = (f32[3,8,128]{2,1,0:T(8,128)}, f32[3,8,128]{2,1,0:T(8,128)S(1)}, u32[]{:S(2)}, u32[]{:S(2)}) collective-permute-start(f32[3,8,128]{2,1,0:T(8,128)} %get-tuple-element.16), channel_id=1, source_target_pairs={{0,2},{2,0},{1,3},{3,1},{4,6},{6,4},{5,7},{7,5},{8,10},{10,8},{9,1... | collective-permute-start | bytes 36872 | tf_op jit(solution)/shard_map/y_swap/ppermute | solution.py:320
  8.0 0.0 copy-done.8
  8.0 0.1 collective-permute-start.2
  8.0 4.4 %collective-permute-done.2.rest_1_ = f32[1,8,128]{2,1,0:T(8,128)S(1)} collective-permute-done((f32[1,8,128]{2,1,0:T(8,128)S(1)}, f32[1,8,128]{2,1,0:T(8,128)S(1)}, u32[]{:S(2)}, u32[]{:S(2)}) %collective-permute-start.2) | collective-permute-done | bytes 4128 | tf_op jit(solution)/shard_map/d_swap/ppermute | solution.py:338
  12.5 0.0 copy-start.6
  12.5 0.0 collective-permute-done.1.rest_0_
  12.5 0.0 copy-start.5
  12.5 0.0 collective-permute-done.zb
  12.5 0.6 %copy-done.6 = f32[1,8,128]{2,1,0:T(8,128)} copy-done((f32[1,8,128]{2,1,0:T(8,128)}, f32[1,8,128]{2,1,0:T(8,128)S(1)}, u32[]{:S(2)}) %copy-start.6) | copy-done | bytes 4120
  13.1 0.0 copy-done.5
  13.1 0.0 copy-start
  13.1 0.7 %copy-done = f32[41,8,128]{2,1,0:T(8,128)} copy-done((f32[41,8,128]{2,1,0:T(8,128)}, f32[41,8,128]{2,1,0:T(8,128)S(1)}, u32[]{:S(2)}) %copy-start) | copy-done | bytes 167960
  13.8 1.6 %edges.1 = (f32[17,8,128]{2,1,0:T(8,128)}, f32[17,8,128]{2,1,0:T(8,128)}) custom-call(f32[41,8,128]{2,1,0:T(8,128)} %copy-done, f32[3,8,128]{2,1,0:T(8,128)} %copy-done.5, f32[1,8,128]{2,1,0:T(8,128)} %copy-done.6), custom_call_target="tpu_custom_call" | custom-call | tf_op jit(solution)/shard_map/edges/pallas_call | solution.py:380
  15.4 1.5 %collective-permute-start.5 = (f32[17,8,128]{2,1,0:T(8,128)}, f32[17,8,128]{2,1,0:T(8,128)S(1)}, u32[]{:S(2)}, u32[]{:S(2)}) collective-permute-start(f32[17,8,128]{2,1,0:T(8,128)} %get-tuple-element.20), channel_id=1, source_target_pairs={{0,4},{4,0},{8,12},{12,8},{16,20},{20,16},{24,28},{28,24},{1,5},{5... | collective-permute-start | bytes 208904 | tf_op jit(solution)/shard_map/e_swap/ppermute | solution.py:320
  16.9 0.7 %collective-permute-start.6 = (f32[17,8,128]{2,1,0:T(8,128)}, f32[17,8,128]{2,1,0:T(8,128)S(1)}, u32[]{:S(2)}, u32[]{:S(2)}) collective-permute-start(f32[17,8,128]{2,1,0:T(8,128)} %get-tuple-element.21), channel_id=1, source_target_pairs={{4,8},{8,4},{12,16},{16,12},{20,24},{24,20},{5,9},{9,5},{13,17},{1... | collective-permute-start | bytes 208904 | tf_op jit(solution)/shard_map/e_swap/ppermute | solution.py:328
  17.5 0.0 collective-permute-done.3.rest_2_
  17.5 0.0 copy-start.1
  17.6 0.0 collective-permute-done.4.rest_3_
  17.6 0.0 copy-start.2
  17.6 0.4 %collective-permute-done.5.rest_4_ = f32[17,8,128]{2,1,0:T(8,128)S(1)} collective-permute-done((f32[17,8,128]{2,1,0:T(8,128)}, f32[17,8,128]{2,1,0:T(8,128)S(1)}, u32[]{:S(2)}, u32[]{:S(2)}) %collective-permute-start.5) | collective-permute-done | bytes 69664 | tf_op jit(solution)/shard_map/e_swap/ppermute | solution.py:320
  18.0 0.0 copy-start.3
  18.0 0.0 collective-permute-done.6.rest_5_
  18.0 0.0 copy-start.4
  18.0 0.2 copy-done.1
  18.2 0.1 copy-done.2
  18.3 0.3 copy-done.3
  18.6 0.0 copy-done.4
  18.7 7.0 %steps.1 = (f32[2,4,8,8,128]{4,3,2,1,0:T(8,128)}, f32[1,128]{1,0:T(1,128)}, f32[1,128]{1,0:T(1,128)}, f32[1,128]{1,0:T(1,128)}) custom-call(f32[2,4,8,8,128]{4,3,2,1,0:T(8,128)} %adjoint.3, f32[3,8,8,128]{3,2,1,0:T(8,128)} %wind.3, f32[8,8,128]{2,1,0:T(8,128)} %get-tuple-element.14.damping, f32[4,4,8,8,128]{4,3,2,1,0:T(8,128)} %saved.1, s32[8,8,128]{2,1,0:T(8,128)} %slots.3, ...), custom_call_target="tpu_custom_call" | custom-call | tf_op jit(solution)/shard_map/steps/pallas_call | solution.py:392
  25.7 0.0 copy-start.10
  25.7 0.7 %copy-done.10 = f32[1,128]{1,0:T(1,128)S(1)} copy-done((f32[1,128]{1,0:T(1,128)S(1)}, f32[1,128]{1,0:T(1,128)}, u32[]{:S(2)}) %copy-start.10) | copy-done | bytes 536
  26.4 0.0 copy-start.9
  26.4 4.9 %collective-permute-start.7 = (f32[1,128]{1,0:T(1,128)S(1)}, f32[1,128]{1,0:T(1,128)S(1)}, u32[]{:S(2)}, u32[]{:S(2)}) collective-permute-start(f32[1,128]{1,0:T(1,128)S(1)} %copy-done.10), channel_id=1, source_target_pairs={{0,4},{4,0},{8,12},{12,8},{16,20},{20,16},{24,28},{28,24},{1,5},{5... | collective-permute-start | bytes 1544 | tf_op jit(solution)/shard_map/g_swap/ppermute | solution.py:320
  31.3 0.0 copy-done.9
  31.3 0.0 copy-start.7
  31.3 3.8 %collective-permute-start.8 = (f32[1,128]{1,0:T(1,128)S(1)}, f32[1,128]{1,0:T(1,128)S(1)}, u32[]{:S(2)}, u32[]{:S(2)}) collective-permute-start(f32[1,128]{1,0:T(1,128)S(1)} %copy-done.9), channel_id=1, source_target_pairs={{0,28},{4,8},{8,4},{12,16},{16,12},{20,24},{24,20},{28,0},{1,29},{... | collective-permute-start | bytes 1544 | tf_op jit(solution)/shard_map/g_swap/ppermute | solution.py:328
  35.1 0.0 collective-permute-done.7
  35.1 1.3 %collective-permute-done.8 = f32[1,128]{1,0:T(1,128)S(1)} collective-permute-done((f32[1,128]{1,0:T(1,128)S(1)}, f32[1,128]{1,0:T(1,128)S(1)}, u32[]{:S(2)}, u32[]{:S(2)}) %collective-permute-start.8) | collective-permute-done | bytes 544 | tf_op jit(solution)/shard_map/g_swap/ppermute | solution.py:328
  36.4 0.0 copy-done.7
  36.4 0.5 %slice_bitcast_fusion = f32[32]{0:T(128)} fusion(f32[1,128]{1,0:T(1,128)S(1)} %add_add_fusion), kind=kLoop, calls=%fused_computation | loop fusion | bytes 256 | tf_op jit(solution)/shard_map/squeeze | solution.py:407
  (1 shorter events, 0.0 us)
Async XLA Ops:
  2.7 5.2 %copy-start.8 = (f32[1,8,128]{2,1,0:T(8,128)S(1)}, f32[1,8,128]{2,1,0:T(8,128)}, u32[]{:S(2)}) copy-start(f32[1,8,128]{2,1,0:T(8,128)} %get-tuple-element.17) | copy-start | bytes 12292
  2.7 9.8 %collective-permute-start = (f32[41,8,128]{2,1,0:T(8,128)}, f32[41,8,128]{2,1,0:T(8,128)S(1)}, u32[]{:S(2)}, u32[]{:S(2)}) collective-permute-start(f32[41,8,128]{2,1,0:T(8,128)} %get-tuple-element.15), channel_id=1, source_target_pairs={{0,1},{1,0},{2,3},{3,2},{4,5},{5,4},{6,7},{7,6},{8,9},{9,8},{10,11... | collective-permute-start | bytes 503816 | tf_op jit(solution)/shard_map/z_swap/ppermute | solution.py:320
  5.7 11.8 %collective-permute-start.3 = (f32[48,8,128]{2,1,0:T(8,128)}, f32[48,8,128]{2,1,0:T(8,128)S(1)}, u32[]{:S(2)}, u32[]{:S(2)}) collective-permute-start(f32[48,8,128]{2,1,0:T(8,128)} %get-tuple-element.18), channel_id=1, source_target_pairs={{0,4},{4,0},{8,12},{12,8},{16,20},{20,16},{24,28},{28,24},{1,5},{5... | collective-permute-start | bytes 589832 | tf_op jit(solution)/shard_map/x_swap/ppermute | solution.py:320
  5.7 11.8 %collective-permute-start.4 = (f32[48,8,128]{2,1,0:T(8,128)}, f32[48,8,128]{2,1,0:T(8,128)S(1)}, u32[]{:S(2)}, u32[]{:S(2)}) collective-permute-start(f32[48,8,128]{2,1,0:T(8,128)} %get-tuple-element.19), channel_id=1, source_target_pairs={{4,8},{8,4},{12,16},{16,12},{20,24},{24,20},{5,9},{9,5},{13,17},{1... | collective-permute-start | bytes 589832 | tf_op jit(solution)/shard_map/x_swap/ppermute | solution.py:328
  6.4 6.1 %collective-permute-start.1 = (f32[3,8,128]{2,1,0:T(8,128)}, f32[3,8,128]{2,1,0:T(8,128)S(1)}, u32[]{:S(2)}, u32[]{:S(2)}) collective-permute-start(f32[3,8,128]{2,1,0:T(8,128)} %get-tuple-element.16), channel_id=1, source_target_pairs={{0,2},{2,0},{1,3},{3,1},{4,6},{6,4},{5,7},{7,5},{8,10},{10,8},{9,1... | collective-permute-start | bytes 36872 | tf_op jit(solution)/shard_map/y_swap/ppermute | solution.py:320
  8.0 4.5 %collective-permute-start.2 = (f32[1,8,128]{2,1,0:T(8,128)S(1)}, f32[1,8,128]{2,1,0:T(8,128)S(1)}, u32[]{:S(2)}, u32[]{:S(2)}) collective-permute-start(f32[1,8,128]{2,1,0:T(8,128)S(1)} %copy-done.8), channel_id=1, source_target_pairs={{0,3},{1,2},{2,1},{3,0},{4,7},{5,6},{6,5},{7,4},{8,11},{9,10},{10,... | collective-permute-start | bytes 12296 | tf_op jit(solution)/shard_map/d_swap/ppermute | solution.py:338
  12.5 0.6 %copy-start.6 = (f32[1,8,128]{2,1,0:T(8,128)}, f32[1,8,128]{2,1,0:T(8,128)S(1)}, u32[]{:S(2)}) copy-start(f32[1,8,128]{2,1,0:T(8,128)S(1)} %collective-permute-done.2.rest_1_) | copy-start | bytes 12292
  12.5 0.6 %copy-start.5 = (f32[3,8,128]{2,1,0:T(8,128)}, f32[3,8,128]{2,1,0:T(8,128)S(1)}, u32[]{:S(2)}) copy-start(f32[3,8,128]{2,1,0:T(8,128)S(1)} %collective-permute-done.1.rest_0_) | copy-start | bytes 36868
  13.1 0.7 %copy-start = (f32[41,8,128]{2,1,0:T(8,128)}, f32[41,8,128]{2,1,0:T(8,128)S(1)}, u32[]{:S(2)}) copy-start(f32[41,8,128]{2,1,0:T(8,128)S(1)} %collective-permute-done.zb) | copy-start | bytes 503812
  15.4 2.6 %collective-permute-start.5 = (f32[17,8,128]{2,1,0:T(8,128)}, f32[17,8,128]{2,1,0:T(8,128)S(1)}, u32[]{:S(2)}, u32[]{:S(2)}) collective-permute-start(f32[17,8,128]{2,1,0:T(8,128)} %get-tuple-element.20), channel_id=1, source_target_pairs={{0,4},{4,0},{8,12},{12,8},{16,20},{20,16},{24,28},{28,24},{1,5},{5... | collective-permute-start | bytes 208904 | tf_op jit(solution)/shard_map/e_swap/ppermute | solution.py:320
  16.9 1.1 %collective-permute-start.6 = (f32[17,8,128]{2,1,0:T(8,128)}, f32[17,8,128]{2,1,0:T(8,128)S(1)}, u32[]{:S(2)}, u32[]{:S(2)}) collective-permute-start(f32[17,8,128]{2,1,0:T(8,128)} %get-tuple-element.21), channel_id=1, source_target_pairs={{4,8},{8,4},{12,16},{16,12},{20,24},{24,20},{5,9},{9,5},{13,17},{1... | collective-permute-start | bytes 208904 | tf_op jit(solution)/shard_map/e_swap/ppermute | solution.py:328
  17.5 0.7 %copy-start.1 = (f32[48,8,128]{2,1,0:T(8,128)}, f32[48,8,128]{2,1,0:T(8,128)S(1)}, u32[]{:S(2)}) copy-start(f32[48,8,128]{2,1,0:T(8,128)S(1)} %collective-permute-done.3.rest_2_) | copy-start | bytes 589828
  17.6 0.7 %copy-start.2 = (f32[48,8,128]{2,1,0:T(8,128)}, f32[48,8,128]{2,1,0:T(8,128)S(1)}, u32[]{:S(2)}) copy-start(f32[48,8,128]{2,1,0:T(8,128)S(1)} %collective-permute-done.4.rest_3_) | copy-start | bytes 589828
  18.0 0.6 %copy-start.3 = (f32[17,8,128]{2,1,0:T(8,128)}, f32[17,8,128]{2,1,0:T(8,128)S(1)}, u32[]{:S(2)}) copy-start(f32[17,8,128]{2,1,0:T(8,128)S(1)} %collective-permute-done.5.rest_4_) | copy-start | bytes 208900
  18.0 0.7 %copy-start.4 = (f32[17,8,128]{2,1,0:T(8,128)}, f32[17,8,128]{2,1,0:T(8,128)S(1)}, u32[]{:S(2)}) copy-start(f32[17,8,128]{2,1,0:T(8,128)S(1)} %collective-permute-done.6.rest_5_) | copy-start | bytes 208900
  25.7 0.7 %copy-start.10 = (f32[1,128]{1,0:T(1,128)S(1)}, f32[1,128]{1,0:T(1,128)}, u32[]{:S(2)}) copy-start(f32[1,128]{1,0:T(1,128)} %get-tuple-element.24) | copy-start | bytes 1540
  26.4 4.9 %copy-start.9 = (f32[1,128]{1,0:T(1,128)S(1)}, f32[1,128]{1,0:T(1,128)}, u32[]{:S(2)}) copy-start(f32[1,128]{1,0:T(1,128)} %get-tuple-element.25) | copy-start | bytes 1540
  26.4 8.7 %collective-permute-start.7 = (f32[1,128]{1,0:T(1,128)S(1)}, f32[1,128]{1,0:T(1,128)S(1)}, u32[]{:S(2)}, u32[]{:S(2)}) collective-permute-start(f32[1,128]{1,0:T(1,128)S(1)} %copy-done.10), channel_id=1, source_target_pairs={{0,4},{4,0},{8,12},{12,8},{16,20},{20,16},{24,28},{28,24},{1,5},{5... | collective-permute-start | bytes 1544 | tf_op jit(solution)/shard_map/g_swap/ppermute | solution.py:320
  31.3 5.1 %copy-start.7 = (f32[1,128]{1,0:T(1,128)S(1)}, f32[1,128]{1,0:T(1,128)}, u32[]{:S(2)}) copy-start(f32[1,128]{1,0:T(1,128)} %get-tuple-element.23) | copy-start | bytes 1540
  31.3 5.1 %collective-permute-start.8 = (f32[1,128]{1,0:T(1,128)S(1)}, f32[1,128]{1,0:T(1,128)S(1)}, u32[]{:S(2)}, u32[]{:S(2)}) collective-permute-start(f32[1,128]{1,0:T(1,128)S(1)} %copy-done.9), channel_id=1, source_target_pairs={{0,28},{4,8},{8,4},{12,16},{16,12},{20,24},{24,20},{28,0},{1,29},{... | collective-permute-start | bytes 1544 | tf_op jit(solution)/shard_map/g_swap/ppermute | solution.py:328

commit v2 on v1

--- a/solution.py
+++ b/solution.py
@@ -21,6 +21,10 @@
 
 def z_of(s, depth_z):
     return jnp.where(lax.axis_index("gz") == 0, depth_z - 1 - s, s)
+
+
+def z_sign():
+    return jnp.where(lax.axis_index("gz") == 0, jnp.float32(-1.0), jnp.float32(1.0))
 
 
 def own_planes(depth_z):
@@ -68,15 +72,22 @@
     return (x * count_y + lax.axis_index("gy")) * count_z + lax.axis_index("gz")
 
 
-def pack_kernel(sides, adjoint, wind, slots, table, impedance, *outs):
-    damping, zb = outs[:2]
-    ys = outs[2:2 + sides]
-    ds = outs[2 + sides:2 + 2 * sides]
-    xa, xb = outs[2 + 2 * sides:4 + 2 * sides]
-    names = outs[4 + 2 * sides]
+def pack_kernel(sides, *refs):
+    sources = refs[:5]
+    adjoint, wind, slots, table, damping, zb = refs[5:11]
+    ys = refs[11:11 + sides]
+    ds = refs[11 + sides:11 + 2 * sides]
+    xa, xb, impedance, names, sems = refs[11 + 2 * sides:]
+    targets = (adjoint, wind, slots, table, impedance)
+    copies = [pltpu.make_async_copy(a, b, sems.at[i]) for i, (a, b) in enumerate(zip(sources, targets))]
+    for i in (3, 4, 2, 0, 1):
+        copies[i].start()
     depth_z = slots.shape[0]
     names[...] = jnp.zeros((8, 128), jnp.int32)
+    copies[3].wait()
     names[:, :table.shape[1]] = jnp.broadcast_to(table[...], (8, table.shape[1]))
+    copies[4].wait()
+    copies[2].wait()
     ids = names[...]
     local = jnp.zeros((8, 128), jnp.float32)
     for offset in (-1, 0, 1):
@@ -87,6 +98,9 @@
         slot = slots[z]
         found = jnp.take_along_axis(local, jnp.maximum(slot - 1, 0), axis=1)
         damping[z] = jnp.where(slot > 0, found, 0.0)
+
+    copies[0].wait()
+    copies[1].wait()
 
     def load(f, s):
         z = z_of(s, depth_z)
@@ -145,73 +159,83 @@
     return value if other is None else value + other
 
 
-def step_kernel(sides, adjoint, wind, damping, saved, slots, table, zb, *rest):
+def put(cells, f, slot, tx, ty, value):
+    cells[f, slot, 8 * tx:8 * tx + 8, 128 * ty:128 * ty + 128] = value
+
+
+def spread(packed, j, side):
+    lanes = lane_iota()
+    high = (lax.rem(lax.axis_index("gy"), 2) == 0) == (side == 0)
+    shift = lax.rem(256 - DEPTH * j - jnp.where(high, 0, DEPTH), 128)
+    start = jnp.where(high, 0, 128 - DEPTH)
+    return jnp.where((lanes >= start) & (lanes < start + DEPTH), pltpu.roll(packed, shift, 1), 0.0)
+
+
+def spread_y(cells, depth_z, tx, groups):
+    planes = own_planes(depth_z)
+    for i, (f, s) in enumerate(planes):
+        value = sum(spread(rows[i // GROUPS], i % GROUPS, side) for side, rows in enumerate(groups))
+        put(cells, f, DEPTH + s, tx, 1, value)
+    for i, (f, t) in enumerate(D_PLANES):
+        value = sum(spread(rows[-1], i, side) for side, rows in enumerate(groups))
+        put(cells, f, DEPTH - t, tx, 1, value)
+
+
+def fill_kernel(sides, adjoint, wind, damping, saved_source, zb, *rest):
     ys = rest[:sides]
     ds = rest[sides:2 * sides]
-    oa, ob, ea, eb, out, own, part_a, part_b, cells, prod, acc = rest[2 * sides:]
-    depth_z = slots.shape[0]
-    rows, lanes = row_iota(), lane_iota()
+    oa, ob, cells, saved, sem = rest[2 * sides:]
+    copy = pltpu.make_async_copy(saved_source, saved, sem)
+    copy.start()
+    depth_z = damping.shape[0]
+    rows = row_iota()
     even_x = lax.rem(lax.axis_index("gx"), 2) == 0
-    even_y = lax.rem(lax.axis_index("gy"), 2) == 0
     zero = jnp.zeros((8, 128), jnp.float32)
-    far = DEPTH + depth_z
-
-    def put(f, slot, tx, ty, value):
-        cells[f, slot, 8 * tx:8 * tx + 8, 128 * ty:128 * ty + 128] = value
-
     for s in range(depth_z):
         z = z_of(s, depth_z)
         for f in range(4):
-            put(f, DEPTH + s, 0, 0, adjoint[1, f, z])
-            put(4 + f, DEPTH + s, 0, 0, adjoint[0, f, z])
+            put(cells, f, DEPTH + s, 0, 0, adjoint[1, f, z])
+            put(cells, 4 + f, DEPTH + s, 0, 0, adjoint[0, f, z])
         for f in range(3):
-            put(8 + f, DEPTH + s, 0, 0, wind[f, z])
-        put(11, DEPTH + s, 0, 0, damping[z])
+            put(cells, 8 + f, DEPTH + s, 0, 0, wind[f, z])
+        put(cells, 11, DEPTH + s, 0, 0, damping[z])
     for i, (f, t) in enumerate(Z_PLANES):
-        put(f, DEPTH - t, 0, 0, zb[i])
+        put(cells, f, DEPTH - t, 0, 0, zb[i])
     planes = own_planes(depth_z)
     for i in range(len(planes) // 2):
         pair = unpack_rows(oa[i], ob[i], even_x, rows)
         for (f, s), value in zip(planes[2 * i:2 * i + 2], pair):
-            put(f, DEPTH + s, 1, 0, value)
+            put(cells, f, DEPTH + s, 1, 0, value)
+    spread_y(cells, depth_z, 0, [[r[i] for r in (y, d) for i in range(r.shape[0])] for y, d in zip(ys, ds)])
+    for tx in range(2):
+        for ty in range(2):
+            for f in range(9):
+                put(cells, f, DEPTH + depth_z, tx, ty, zero)
+            if tx + ty:
+                for f in (0, 1, 2, 3, 8):
+                    put(cells, f, 0, tx, ty, zero)
+                for f in (4, 5, 6, 7, 9, 10, 11):
+                    if not (f == 9 and ty == 0) and not (f == 10 and ty == 1):
+                        put(cells, f, 1, tx, ty, zero)
+    copy.wait()
+
+
+def step_kernel(sides, cells_in, ea, eb, saved, slots, table, cells, own, part_a, part_b, prod, acc):
+    del cells_in
+    depth_z = slots.shape[0]
+    rows = row_iota()
+    even_x = lax.rem(lax.axis_index("gx"), 2) == 0
+    far = DEPTH + depth_z
     edges = []
     for i in range(ea.shape[0]):
         edges += unpack_rows(ea[i], eb[i], even_x, rows)
     for (f, t), value in zip(E_PLANES, edges):
-        put(f, DEPTH - t, 1, 0, value)
+        put(cells, f, DEPTH - t, 1, 0, value)
     edges = edges[len(E_PLANES):]
-    packs = [ref[i] for ref in ys + ds for i in range(ref.shape[0])]
-    y_rows = ys[0].shape[0]
-
-    def spread(packed, j, side):
-        high = even_y if side == 0 else jnp.logical_not(even_y)
-        shift = lax.rem(256 - DEPTH * j - jnp.where(high, 0, DEPTH), 128)
-        start = jnp.where(high, 0, 128 - DEPTH)
-        return jnp.where((lanes >= start) & (lanes < start + DEPTH), pltpu.roll(packed, shift, 1), 0.0)
-
-    def spread_all(index, j):
-        for tx, source in ((0, packs), (1, edges)):
-            value = spread(source[index(0)], j, 0)
-            if sides > 1:
-                value = value + spread(source[index(1)], j, 1)
-            yield tx, value
-
-    for i, (f, s) in enumerate(planes):
-        for tx, value in spread_all(lambda side: side * y_rows + i // GROUPS, i % GROUPS):
-            put(f, DEPTH + s, tx, 1, value)
-    for i, (f, t) in enumerate(D_PLANES):
-        for tx, value in spread_all(lambda side: sides * y_rows + side, i):
-            put(f, DEPTH - t, tx, 1, value)
-    for tx in range(2):
-        for ty in range(2):
-            for f in range(9):
-                put(f, far, tx, ty, zero)
-            if tx + ty:
-                for f in (0, 1, 2, 3, 8):
-                    put(f, 0, tx, ty, zero)
-                for f in (4, 5, 6, 7, 9, 10, 11):
-                    if not (f == 9 and ty == 0) and not (f == 10 and ty == 1):
-                        put(f, 1, tx, ty, zero)
+    y_rows = len(edges) // sides - 1
+    spread_y(cells, depth_z, 1, [
+        edges[side * y_rows:(side + 1) * y_rows] + [edges[sides * y_rows + side]] for side in range(sides)
+    ])
 
     grid_row = lax.broadcasted_iota(jnp.int32, (16, 256), 0)
     grid_lane = lax.broadcasted_iota(jnp.int32, (16, 256), 1)
@@ -223,7 +247,7 @@
     inside = (grid_row < row_end) | (grid_row >= row_restart)
     inside &= (grid_lane < lane_end) | (grid_lane >= lane_restart)
     factor = jnp.where(inside, jnp.float32(0.5 * SCALE), 0.0)
-    sign = jnp.where(lax.axis_index("gz") == 0, jnp.float32(-1.0), jnp.float32(1.0))
+    sign = z_sign()
 
     def full_step(first, middle_at, upper_at):
         def body(slot, carry):
@@ -244,32 +268,6 @@
 
         lax.fori_loop(first, far, body, 0)
 
-    def last_step(middle_at, upper_at):
-        def body(s, carry):
-            slot = DEPTH + s
-            own_part = (slice(0, 8), slice(0, 128))
-            middle = [cells[(middle_at + c, slot) + own_part] for c in range(4)]
-            above = [cells[(middle_at + c, slot + 1) + own_part] for c in range(4)]
-            below = [cells[(middle_at + c, slot - 1) + own_part] for c in range(4)]
-            mid_x = [cells[middle_at + c, slot, :, 0:128] for c in range(4)]
-            mid_y = [cells[middle_at + c, slot, 0:8, :] for c in range(4)]
-            wind_up, wind_down = cells[(8, slot + 1) + own_part], cells[(8, slot - 1) + own_part]
-            wind_x, wind_y = cells[9, slot, :, 0:128], cells[10, slot, 0:8, :]
-            loss = SCALE * cells[(11, slot) + own_part]
-            z = z_of(s, depth_z)
-            for c in range(4):
-                total = sign * (flux(wind_up, above, c, 0) - flux(wind_down, below, c, 0))
-                along = flux(wind_x, mid_x, c, 1)
-                total += (pltpu.roll(along, 15, 0) - pltpu.roll(along, 1, 0))[0:8]
-                along = flux(wind_y, mid_y, c, 2)
-                total += (pltpu.roll(along, 255, 1) - pltpu.roll(along, 1, 1))[:, 0:128]
-                upper = cells[(upper_at + c, slot) + own_part]
-                out[0, c, z] = middle[c]
-                out[1, c, z] = upper + jnp.float32(0.5 * SCALE) * total - loss * middle[c]
-            return carry
-
-        lax.fori_loop(0, depth_z, body, 0)
-
     def products(step, middle_at, slot, z):
         return sum(cells[middle_at + c, slot, 0:8, 0:128] * saved[step, c, z] for c in range(4))
 
@@ -282,7 +280,6 @@
     for s in range(depth_z):
         z = z_of(s, depth_z)
         prod[z] = -SCALE * (prod[z] + (products(2, 0, DEPTH + s, z) + products(3, 4, DEPTH + s, z)))
-    last_step(4, 0)
 
     slot_count = table.shape[1]
     level = lax.broadcasted_iota(jnp.int32, (slot_count, 128), 0) + 1
@@ -316,6 +313,36 @@
     part_b[...] = jnp.where(even_x, downward, upward)
 
 
+def last_kernel(cells, out):
+    middle_at, upper_at = 4, 0
+    depth_z = out.shape[2]
+    sign = z_sign()
+    def body(s, carry):
+        slot = DEPTH + s
+        own_part = (slice(0, 8), slice(0, 128))
+        middle = [cells[(middle_at + c, slot) + own_part] for c in range(4)]
+        above = [cells[(middle_at + c, slot + 1) + own_part] for c in range(4)]
+        below = [cells[(middle_at + c, slot - 1) + own_part] for c in range(4)]
+        mid_x = [cells[middle_at + c, slot, :, 0:128] for c in range(4)]
+        mid_y = [cells[middle_at + c, slot, 0:8, :] for c in range(4)]
+        wind_up, wind_down = cells[(8, slot + 1) + own_part], cells[(8, slot - 1) + own_part]
+        wind_x, wind_y = cells[9, slot, :, 0:128], cells[10, slot, 0:8, :]
+        loss = SCALE * cells[(11, slot) + own_part]
+        z = z_of(s, depth_z)
+        for c in range(4):
+            total = sign * (flux(wind_up, above, c, 0) - flux(wind_down, below, c, 0))
+            along = flux(wind_x, mid_x, c, 1)
+            total += (pltpu.roll(along, 15, 0) - pltpu.roll(along, 1, 0))[0:8]
+            along = flux(wind_y, mid_y, c, 2)
+            total += (pltpu.roll(along, 255, 1) - pltpu.roll(along, 1, 1))[:, 0:128]
+            upper = cells[(upper_at + c, slot) + own_part]
+            out[0, c, z] = middle[c]
+            out[1, c, z] = upper + jnp.float32(0.5 * SCALE) * total - loss * middle[c]
+        return carry
+
+    lax.fori_loop(0, depth_z, body, 0)
+
+
 def swap_a(block, axis):
     return lax.ppermute(block, axis, [(i, i ^ 1) for i in range(lax.axis_size(axis))])
 
@@ -338,8 +365,26 @@
     return lax.ppermute(block, ("gy", "gz"), pairs)
 
 
-def vmem(count):
-    return [pl.BlockSpec(memory_space=pltpu.VMEM)] * count
+VMEM = pl.BlockSpec(memory_space=pltpu.VMEM)
+HBM = pl.BlockSpec(memory_space=pltpu.HBM)
+
+
+def call(kernel, name, limit, in_specs, out_shape, scratch=(), aliases=None, cost=None):
+    return pl.pallas_call(
+        kernel,
+        out_shape=[jax.ShapeDtypeStruct(o.shape, o.dtype) for o in out_shape],
+        in_specs=in_specs,
+        out_specs=[VMEM] * len(out_shape),
+        scratch_shapes=list(scratch),
+        input_output_aliases=aliases or {},
+        compiler_params=pltpu.CompilerParams(vmem_limit_bytes=limit << 20),
+        cost_estimate=cost and pl.CostEstimate(flops=cost, bytes_accessed=cost, transcendentals=0),
+        name=name,
+    )
+
+
+def in_hbm(array):
+    return pltpu.with_memory_space_constraint(array, pltpu.HBM)
 
 
 def rows_of(count):
@@ -353,20 +398,19 @@
     rates = impedance.reshape(-1, 128)
     own_count = FIELDS * depth_z
     y_rows = -(-own_count // GROUPS)
-    packed = pl.pallas_call(
+    packed = call(
         functools.partial(pack_kernel, sides),
-        out_shape=[rows_of(depth_z), rows_of(len(Z_PLANES))]
+        "pack", 4,
+        [HBM] * 5,
+        [adjoint, wind_field, facade_slot, table, rows_of(depth_z), rows_of(len(Z_PLANES))]
         + [rows_of(y_rows)] * sides
         + [rows_of(1)] * sides
         + [rows_of(own_count // 2)] * 2,
-        in_specs=vmem(5),
-        out_specs=vmem(4 + 2 * sides),
-        scratch_shapes=[pltpu.VMEM((8, 128), jnp.int32)],
-        name="pack",
-    )(adjoint, wind_field, facade_slot, table, rates)
-    damping, zb = packed[:2]
-    ys, ds = packed[2:2 + sides], packed[2 + sides:2 + 2 * sides]
-    xa, xb = packed[2 + 2 * sides:]
+        [pltpu.VMEM(rates.shape, jnp.float32), pltpu.VMEM((8, 128), jnp.int32), pltpu.SemaphoreType.DMA((5,))],
+    )(*map(in_hbm, (adjoint, wind_field, facade_slot, table, rates)))
+    adjoint, wind, slots, table, damping, zb = packed[:6]
+    ys, ds = packed[6:6 + sides], packed[6 + sides:6 + 2 * sides]
+    xa, xb = packed[6 + 2 * sides:]
     with jax.named_scope("z_swap"):
         zb = swap_a(zb, "gz")
     with jax.named_scope("y_swap"):
@@ -377,33 +421,37 @@
         xb = swap_b(xb, "gx")
         xa = swap_a(xa, "gx")
     edge_count = (len(E_PLANES) + sides * (y_rows + 1)) // 2
-    ea, eb = pl.pallas_call(
+    ea, eb = call(
         functools.partial(edge_kernel, sides),
-        out_shape=[rows_of(edge_count)] * 2,
-        in_specs=vmem(1 + 2 * sides),
-        out_specs=vmem(2),
-        name="edges",
+        "edges", 2,
+        [VMEM] * (1 + 2 * sides),
+        [rows_of(edge_count)] * 2,
     )(zb, *ys, *ds)
     with jax.named_scope("e_swap"):
         eb = swap_b(eb, "gx")
         ea = swap_a(ea, "gx")
-    slot_count = table.shape[1]
+    cells = jax.ShapeDtypeStruct((FIELDS, DEPTH + depth_z + 1, 16, 256), jnp.float32)
+    cells, saved = call(
+        functools.partial(fill_kernel, sides),
+        "fill", 2,
+        [VMEM] * 3 + [HBM] + [VMEM] * (3 + 2 * sides),
+        [cells, saved_state],
+        [pltpu.SemaphoreType.DMA],
+        cost=4000000,
+    )(adjoint, wind, damping, in_hbm(saved_state), zb, *ys, *ds, xa, xb)
     row = jax.ShapeDtypeStruct((1, 128), jnp.float32)
-    out, own, part_a, part_b = pl.pallas_call(
+    cells, own, part_a, part_b = call(
         functools.partial(step_kernel, sides),
-        out_shape=[jax.ShapeDtypeStruct(adjoint.shape, jnp.float32), row, row, row],
-        in_specs=vmem(11 + 2 * sides),
-        out_specs=vmem(4),
-        scratch_shapes=[
-            pltpu.VMEM((FIELDS, DEPTH + depth_z + 1, 16, 256), jnp.float32),
-            pltpu.VMEM((depth_z, 8, 128), jnp.float32),
-            pltpu.VMEM((slot_count, 128), jnp.float32),
-        ],
-        name="steps",
-    )(adjoint, wind_field, damping, saved_state, facade_slot, table, zb, *ys, *ds, xa, xb, ea, eb)
+        "steps", 2,
+        [VMEM] * 6,
+        [cells, row, row, row],
+        [pltpu.VMEM((depth_z, 8, 128), jnp.float32), pltpu.VMEM((table.shape[1], 128), jnp.float32)],
+        aliases={0: 0},
+    )(cells, ea, eb, saved, slots, table)
     with jax.named_scope("g_swap"):
         part_b = swap_b(part_b, "gx", wrap=True)
         part_a = swap_a(part_a, "gx")
+    out, = call(last_kernel, "last", 2, [VMEM], [adjoint], cost=4000000)(cells)
     gradient = (own + part_a + part_b)[0, :FAC_DEV]
     return out, gradient
 

time: 37.1 us -> 29.3 us (0.79)
  Pallas kernels: 10.8 us -> 8.07 us
  local copies, waits for them, and re-layouts: 3.11 us -> 0.51 us
  waiting for transfers between devices: 6.17 us -> 4.48 us
  starting transfers between devices: 16.1 us -> 15.3 us
    pallas_call x3 -> x5, Pallas kernels: 10.8 us -> 8.07 us  [the longest x1 4.03 us: local(): call(functools.partial(step_kernel, sides), 'steps', 2, [VMEM] * 6, [cell...]
    unnamed x22 -> x0, local copies, waits for them, and re-layouts: 2.6 us -> none
    ppermute x3, waiting for transfers between devices: 1.3 us -> 0.01 us  [swap_b(): return lax.ppermute(block, axis, pairs)]
    ppermute x5, starting transfers between devices: 11 us -> 10.2 us  [swap_a(): lax.ppermute(block, axis, [(i, i ^ 1) for i in range(lax.axis_size(axis))])]
    ppermute x5, waiting for transfers between devices: 0.43 us -> 0.01 us  [swap_a(): lax.ppermute(block, axis, [(i, i ^ 1) for i in range(lax.axis_size(axis))])]
  transfers between devices with their start and end apart: 9 -> 9, of which waited for: 3 -> 1; matrix products, arithmetic and copies ran while one was open for 0% -> 0% of each run, Pallas kernels for 4% -> 9%
where the time goes in v2:
time: 29.3 us; the launch traced here: 29.1 us
  starting transfers between devices  15.3 us (52%)
  Pallas kernels  8.07 us (28%)
  waiting for transfers between devices  4.48 us (15%)
  between operations  0.72 us (2%)
  local copies, waits for them, and re-layouts  0.51 us (2%)
    ppermute x5, starting transfers between devices, swap_a(): lax.ppermute(block, axis, [(i, i ^ 1) for i in range(lax.axis_size(axis))])  10.2 us
    ppermute x3, starting transfers between devices, swap_b(): return lax.ppermute(block, axis, pairs)  5.07 us
    ppermute x1, waiting for transfers between devices, swap_diagonal(): return lax.ppermute(block, ('gy', 'gz'), pairs)  4.46 us
    pallas_call x1, Pallas kernels, local(): call(functools.partial(step_kernel, sides), 'steps', 2, [VMEM] * 6, [cell...  4.03 us
    pallas_call x1, Pallas kernels, local(): out, = call(last_kernel, 'last', 2, [VMEM], [adjoint], cost=4000000)(cells)  1.44 us
    pallas_call x1, Pallas kernels, local(): call(functools.partial(pack_kernel, sides), 'pack', 4, [HBM] * 5, [adjoin...  1.31 us
    pallas_call x1, Pallas kernels, local(): call(functools.partial(fill_kernel, sides), 'fill', 2, [VMEM] * 3 + [HBM]...  1.27 us
  transfers between devices with their start and end apart: 9, of which 1 were waited for; matrix products, arithmetic and copies ran while one was open for 0% of the time, Pallas kernels for 9%

profile of v2, /device:TPU:0, one launch (start us, length us, event | category | flops | bytes accessed | tf_op | source)
XLA Modules:
  0.0 29.1 jit_solution(17563033482362746930)
XLA Ops:
  0.6 1.3 %pack.1 = (f32[2,4,8,8,128]{4,3,2,1,0:T(8,128)S(1)}, f32[3,8,8,128]{3,2,1,0:T(8,128)S(1)}, s32[8,8,128]{2,1,0:T(8,128)S(1)}, s32[1,64]{1,0:T(1,128)S(1)}, f32[8,...) custom-call(f32[2,4,8,8,128]{4,3,2,1,0:T(8,128)} %refs_0_.1, ...), custom_call_target="tpu_custom_call" | custom-call | tf_op jit(solution)/shard_map/pack/pallas_call | solution.py:401
  2.0 3.0 %collective-permute-start = (f32[41,8,128]{2,1,0:T(8,128)S(1)}, f32[41,8,128]{2,1,0:T(8,128)S(1)}, u32[]{:S(2)}, u32[]{:S(2)}) collective-permute-start(f32[41,8,128]{2,1,0:T(8,128)S(1)} %get-tuple-element.23), channel_id=1, source_target_pairs={{0,1},{1,0},{2,3},{3,2},{4,5},{5,4},{6,7},{7,6},{8,9},{9,8},{10,11... | collective-permute-start | bytes 503816 | tf_op jit(solution)/shard_map/z_swap/ppermute | solution.py:347
  5.0 0.0 collective-permute-start.3
  5.0 0.7 %collective-permute-start.4 = (f32[48,8,128]{2,1,0:T(8,128)S(1)}, f32[48,8,128]{2,1,0:T(8,128)S(1)}, u32[]{:S(2)}, u32[]{:S(2)}) collective-permute-start(f32[48,8,128]{2,1,0:T(8,128)S(1)} %get-tuple-element.27), channel_id=1, source_target_pairs={{4,8},{8,4},{12,16},{16,12},{20,24},{24,20},{5,9},{9,5},{13,17},{1... | collective-permute-start | bytes 589832 | tf_op jit(solution)/shard_map/x_swap/ppermute | solution.py:355
  5.7 1.6 %collective-permute-start.1 = (f32[3,8,128]{2,1,0:T(8,128)S(1)}, f32[3,8,128]{2,1,0:T(8,128)S(1)}, u32[]{:S(2)}, u32[]{:S(2)}) collective-permute-start(f32[3,8,128]{2,1,0:T(8,128)S(1)} %get-tuple-element.24), channel_id=1, source_target_pairs={{0,2},{2,0},{1,3},{3,1},{4,6},{6,4},{5,7},{7,5},{8,10},{10,8},{9,1... | collective-permute-start | bytes 36872 | tf_op jit(solution)/shard_map/y_swap/ppermute | solution.py:347
  7.2 0.1 collective-permute-start.2
  7.3 4.5 %collective-permute-done.2.rest_1_ = f32[1,8,128]{2,1,0:T(8,128)S(1)} collective-permute-done((f32[1,8,128]{2,1,0:T(8,128)S(1)}, f32[1,8,128]{2,1,0:T(8,128)S(1)}, u32[]{:S(2)}, u32[]{:S(2)}) %collective-permute-start.2) | collective-permute-done | bytes 4128 | tf_op jit(solution)/shard_map/d_swap/ppermute | solution.py:365
  11.8 0.0 collective-permute-done.1.rest_0_
  11.8 0.0 collective-permute-done.zb
  11.8 1.6 %collective-permute-start.5 = (f32[17,8,128]{2,1,0:T(8,128)S(1)}, f32[17,8,128]{2,1,0:T(8,128)S(1)}, u32[]{:S(2)}, u32[]{:S(2)}) collective-permute-start(f32[17,8,128]{2,1,0:T(8,128)S(1)} %get-tuple-element.29), channel_id=1, source_target_pairs={{0,4},{4,0},{8,12},{12,8},{16,20},{20,16},{24,28},{28,24},{1,5},{5... | collective-permute-start | bytes 208904 | tf_op jit(solution)/shard_map/e_swap/ppermute | solution.py:347
  13.3 0.7 %collective-permute-start.6 = (f32[17,8,128]{2,1,0:T(8,128)S(1)}, f32[17,8,128]{2,1,0:T(8,128)S(1)}, u32[]{:S(2)}, u32[]{:S(2)}) collective-permute-start(f32[17,8,128]{2,1,0:T(8,128)S(1)} %get-tuple-element.30), channel_id=1, source_target_pairs={{4,8},{8,4},{12,16},{16,12},{20,24},{24,20},{5,9},{9,5},{13,17},{1... | collective-permute-start | bytes 208904 | tf_op jit(solution)/shard_map/e_swap/ppermute | solution.py:355
  14.0 0.0 collective-permute-done.3.rest_2_
  14.0 0.0 collective-permute-done.4.rest_3_
  14.0 1.3 %fill.1 = (f32[12,13,16,256]{3,2,1,0:T(8,128)S(1)}, f32[4,4,8,8,128]{4,3,2,1,0:T(8,128)S(1)}) custom-call(f32[2,4,8,8,128]{4,3,2,1,0:T(8,128)S(1)} %get-tuple-element.20.adjoint, f32[3,8,8,128]{3,2,1,0:T(8,128)S(1)} %get-tuple-element.21.wind, f32[8,8,128]{2,1,0:T(8,128)S(1)} %get-tuple-element.22.damping, f32[4,4,8,8,128]{4,3,2,1,0:T(8,128)} %saved_source.1, ...), custom_call_target="tpu_custom_call" | custom-call | flops 4000000 | bytes 4000000 | tf_op jit(solution)/shard_map/fill/pallas_call | solution.py:434
  15.3 0.0 collective-permute-done.5.ea
  15.3 0.0 collective-permute-done.6.eb
  15.3 4.0 %steps.1 = (f32[12,13,16,256]{3,2,1,0:T(8,128)S(1)}, f32[1,128]{1,0:T(1,128)S(1)}, f32[1,128]{1,0:T(1,128)S(1)}, f32[1,128]{1,0:T(1,128)S(1)}) custom-call(f32[12,13,16,256]{3,2,1,0:T(8,128)S(1)} %get-tuple-element.28.cells_in, f32[17,8,128]{2,1,0:T(8,128)S(1)} %collective-permute-done.5.ea, ...), custom_call_target="tpu_custom_call", output_to_operand_aliasing={{0}: (0, {})} | custom-call | tf_op jit(solution)/shard_map/steps/pallas_call | solution.py:443
  19.4 4.0 %collective-permute-start.7 = (f32[1,128]{1,0:T(1,128)S(1)}, f32[1,128]{1,0:T(1,128)S(1)}, u32[]{:S(2)}, u32[]{:S(2)}) collective-permute-start(f32[1,128]{1,0:T(1,128)S(1)} %get-tuple-element.36), channel_id=1, source_target_pairs={{0,4},{4,0},{8,12},{12,8},{16,20},{20,16},{24,28},{28,24},{1,5},{5... | collective-permute-start | bytes 1544 | tf_op jit(solution)/shard_map/g_swap/ppermute | solution.py:347
  23.3 3.8 %collective-permute-start.8 = (f32[1,128]{1,0:T(1,128)S(1)}, f32[1,128]{1,0:T(1,128)S(1)}, u32[]{:S(2)}, u32[]{:S(2)}) collective-permute-start(f32[1,128]{1,0:T(1,128)S(1)} %get-tuple-element.37), channel_id=1, source_target_pairs={{0,28},{4,8},{8,4},{12,16},{16,12},{20,24},{24,20},{28,0},{1,29},{... | collective-permute-start | bytes 1544 | tf_op jit(solution)/shard_map/g_swap/ppermute | solution.py:355
  27.1 1.4 %last.1 = f32[2,4,8,8,128]{4,3,2,1,0:T(8,128)} custom-call(f32[12,13,16,256]{3,2,1,0:T(8,128)S(1)} %get-tuple-element.34.cells), custom_call_target="tpu_custom_call" | custom-call | flops 4000000 | bytes 4000000 | tf_op jit(solution)/shard_map/last/pallas_call | solution.py:454
  28.5 0.0 collective-permute-done.7
  28.5 0.0 collective-permute-done.8
  28.6 0.5 %slice_bitcast_fusion = f32[32]{0:T(128)} fusion(f32[1,128]{1,0:T(1,128)S(1)} %add_add_fusion), kind=kLoop, calls=%fused_computation | loop fusion | bytes 256 | tf_op jit(solution)/shard_map/squeeze | solution.py:455
  (2 shorter events, 0.0 us)
Async XLA Ops:
  2.0 9.8 %collective-permute-start = (f32[41,8,128]{2,1,0:T(8,128)S(1)}, f32[41,8,128]{2,1,0:T(8,128)S(1)}, u32[]{:S(2)}, u32[]{:S(2)}) collective-permute-start(f32[41,8,128]{2,1,0:T(8,128)S(1)} %get-tuple-element.23), channel_id=1, source_target_pairs={{0,1},{1,0},{2,3},{3,2},{4,5},{5,4},{6,7},{7,6},{8,9},{9,8},{10,11... | collective-permute-start | bytes 503816 | tf_op jit(solution)/shard_map/z_swap/ppermute | solution.py:347
  5.0 9.0 %collective-permute-start.3 = (f32[48,8,128]{2,1,0:T(8,128)S(1)}, f32[48,8,128]{2,1,0:T(8,128)S(1)}, u32[]{:S(2)}, u32[]{:S(2)}) collective-permute-start(f32[48,8,128]{2,1,0:T(8,128)S(1)} %get-tuple-element.26), channel_id=1, source_target_pairs={{0,4},{4,0},{8,12},{12,8},{16,20},{20,16},{24,28},{28,24},{1,5},{5... | collective-permute-start | bytes 589832 | tf_op jit(solution)/shard_map/x_swap/ppermute | solution.py:347
  5.0 9.0 %collective-permute-start.4 = (f32[48,8,128]{2,1,0:T(8,128)S(1)}, f32[48,8,128]{2,1,0:T(8,128)S(1)}, u32[]{:S(2)}, u32[]{:S(2)}) collective-permute-start(f32[48,8,128]{2,1,0:T(8,128)S(1)} %get-tuple-element.27), channel_id=1, source_target_pairs={{4,8},{8,4},{12,16},{16,12},{20,24},{24,20},{5,9},{9,5},{13,17},{1... | collective-permute-start | bytes 589832 | tf_op jit(solution)/shard_map/x_swap/ppermute | solution.py:355
  5.7 6.1 %collective-permute-start.1 = (f32[3,8,128]{2,1,0:T(8,128)S(1)}, f32[3,8,128]{2,1,0:T(8,128)S(1)}, u32[]{:S(2)}, u32[]{:S(2)}) collective-permute-start(f32[3,8,128]{2,1,0:T(8,128)S(1)} %get-tuple-element.24), channel_id=1, source_target_pairs={{0,2},{2,0},{1,3},{3,1},{4,6},{6,4},{5,7},{7,5},{8,10},{10,8},{9,1... | collective-permute-start | bytes 36872 | tf_op jit(solution)/shard_map/y_swap/ppermute | solution.py:347
  7.2 4.5 %collective-permute-start.2 = (f32[1,8,128]{2,1,0:T(8,128)S(1)}, f32[1,8,128]{2,1,0:T(8,128)S(1)}, u32[]{:S(2)}, u32[]{:S(2)}) collective-permute-start(f32[1,8,128]{2,1,0:T(8,128)S(1)} %get-tuple-element.25), channel_id=1, source_target_pairs={{0,3},{1,2},{2,1},{3,0},{4,7},{5,6},{6,5},{7,4},{8,11},{9,10},{10,... | collective-permute-start | bytes 12296 | tf_op jit(solution)/shard_map/d_swap/ppermute | solution.py:365
  11.8 3.5 %collective-permute-start.5 = (f32[17,8,128]{2,1,0:T(8,128)S(1)}, f32[17,8,128]{2,1,0:T(8,128)S(1)}, u32[]{:S(2)}, u32[]{:S(2)}) collective-permute-start(f32[17,8,128]{2,1,0:T(8,128)S(1)} %get-tuple-element.29), channel_id=1, source_target_pairs={{0,4},{4,0},{8,12},{12,8},{16,20},{20,16},{24,28},{28,24},{1,5},{5... | collective-permute-start | bytes 208904 | tf_op jit(solution)/shard_map/e_swap/ppermute | solution.py:347
  13.3 2.0 %collective-permute-start.6 = (f32[17,8,128]{2,1,0:T(8,128)S(1)}, f32[17,8,128]{2,1,0:T(8,128)S(1)}, u32[]{:S(2)}, u32[]{:S(2)}) collective-permute-start(f32[17,8,128]{2,1,0:T(8,128)S(1)} %get-tuple-element.30), channel_id=1, source_target_pairs={{4,8},{8,4},{12,16},{16,12},{20,24},{24,20},{5,9},{9,5},{13,17},{1... | collective-permute-start | bytes 208904 | tf_op jit(solution)/shard_map/e_swap/ppermute | solution.py:355
  19.4 9.2 %collective-permute-start.7 = (f32[1,128]{1,0:T(1,128)S(1)}, f32[1,128]{1,0:T(1,128)S(1)}, u32[]{:S(2)}, u32[]{:S(2)}) collective-permute-start(f32[1,128]{1,0:T(1,128)S(1)} %get-tuple-element.36), channel_id=1, source_target_pairs={{0,4},{4,0},{8,12},{12,8},{16,20},{20,16},{24,28},{28,24},{1,5},{5... | collective-permute-start | bytes 1544 | tf_op jit(solution)/shard_map/g_swap/ppermute | solution.py:347
  23.3 5.2 %collective-permute-start.8 = (f32[1,128]{1,0:T(1,128)S(1)}, f32[1,128]{1,0:T(1,128)S(1)}, u32[]{:S(2)}, u32[]{:S(2)}) collective-permute-start(f32[1,128]{1,0:T(1,128)S(1)} %get-tuple-element.37), channel_id=1, source_target_pairs={{0,28},{4,8},{8,4},{12,16},{16,12},{20,24},{24,20},{28,0},{1,29},{... | collective-permute-start | bytes 1544 | tf_op jit(solution)/shard_map/g_swap/ppermute | solution.py:355

commit v3 on v2

v3 whole, which is shorter than its diff:
```python
import functools

import jax
import jax.numpy as jnp
import numpy as np
from jax import lax
from jax.experimental import pallas as pl
from jax.experimental.pallas import tpu as pltpu
from jax.sharding import PartitionSpec as P


FAC_DEV = 32
TIME_STEP = 0.3
SCALE = 2.0 * TIME_STEP

FIELDS = 12
DEPTH = 4
GROUP = 2 * DEPTH
E_PLANES = [(f, t) for t in (1, 2) for f in range(FIELDS)] + [(f, 3) for f in (0, 1, 2, 3, 8, 9)]
R_PLANES = [(f, 3) for f in (4, 5, 6, 7, 10, 11)] + [(f, 4) for f in (0, 1, 2, 3, 8)]
Y_ROWS = FIELDS // 2
D_ROWS = FIELDS // 4


def z_of(s, depth_z):
    return jnp.where(lax.axis_index("gz") == 0, depth_z - 1 - s, s)


def z_sign():
    return jnp.where(lax.axis_index("gz") == 0, jnp.float32(-1.0), jnp.float32(1.0))


def own_planes(depth_z):
    return [(f, s) for f in range(FIELDS) for s in range(depth_z)]


def iota(dim, shape=(8, 128)):
    return lax.broadcasted_iota(jnp.int32, shape, dim)


def is_even(axis):
    return lax.rem(lax.axis_index(axis), 2) == 0


def at_end(axis):
    return (lax.axis_index(axis) == 0) | (lax.axis_index(axis) == lax.axis_size(axis) - 1)


def pack_groups(planes, load):
    groups = iota(1) // GROUP
    row = jnp.zeros((8, 128), jnp.float32)
    for group, plane in planes:
        edge = pltpu.roll(load(*plane), (GROUP * group + DEPTH) % 128, 1)
        row = jnp.where(groups == group, edge, row)
    return row


def unpack_strip(f, y_rows, d_rows):
    lanes = iota(1)
    start = DEPTH * GROUP
    own = pltpu.roll(y_rows[f // 2], (start - 64 * (f % 2)) % 128, 1)
    beyond = y_shift(d_rows[f // 4], -32 * (f % 4))
    return jnp.where(lanes < start, beyond, jnp.where(lanes < start + 64, own, 0.0))


def y_shift(row, shift):
    return pltpu.roll(row, shift % 128, 1) if shift % 128 else row


def merge_sides(parts):
    k = iota(1) % GROUP
    even = is_even("gy")
    if len(parts) == 1:
        start = jnp.where(even, DEPTH, 0)
        return jnp.where((k >= start) & (k < start + DEPTH), parts[0], 0.0)
    second = jnp.where(at_end("gy"), 0.0, parts[1])
    return jnp.where(k >= DEPTH, jnp.where(even, parts[0], second), jnp.where(even, second, parts[0]))


def merged_rows(refs):
    return [merge_sides([ref[i] for ref in refs]) for i in range(refs[0].shape[0])]


def pack_rows(first, second, send_high, rows):
    turned = pltpu.roll(second, 4, 0)
    low = jnp.where(rows < 4, first, turned)
    high = jnp.where(rows < 4, turned, first)
    return jnp.where(send_high, high, low)


def unpack_rows(got_a, got_b, even, rows):
    got_b = jnp.where(at_end("gx"), 0.0, got_b)
    from_high = jnp.where(even, got_a, got_b)
    from_low = jnp.where(even, got_b, got_a)
    first = jnp.where(rows < 4, from_high, from_low)
    second = pltpu.roll(jnp.where(rows < 4, from_low, from_high), 4, 0)
    return first, second


def pack_pairs(planes, xa, xb):
    even = is_even("gx")
    rows = iota(0)
    for i in range(-(-len(planes) // 2)):
        first = planes[2 * i]()
        second = planes[2 * i + 1]() if 2 * i + 1 < len(planes) else first
        xa[i] = pack_rows(first, second, even, rows)
        xb[i] = pack_rows(first, second, jnp.logical_not(even), rows)


def unpack_pairs(xa, xb):
    even = is_even("gx")
    rows = iota(0)
    values = []
    for i in range(xa.shape[0]):
        values += unpack_rows(xa[i], xb[i], even, rows)
    return values


def owner_of(offset):
    count_x, count_y, count_z = (lax.axis_size(a) for a in ("gx", "gy", "gz"))
    x = lax.rem(lax.axis_index("gx") + (offset + count_x), count_x)
    return (x * count_y + lax.axis_index("gy")) * count_z + lax.axis_index("gz")


def loader(adjoint, wind, damping):
    depth_z = damping.shape[0]

    def load(f, s):
        z = z_of(s, depth_z)
        if f < 4:
            return adjoint[1, f, z]
        if f < 8:
            return adjoint[0, f - 4, z]
        if f < 11:
            return wind[f - 8, z]
        return damping[z]

    return load


def pack_kernel(*refs):
    sources = refs[:5]
    adjoint, wind, slots, table, damping, zb, yb, db, impedance, names, sems = refs[5:]
    targets = (adjoint, wind, slots, table, impedance)
    copies = [pltpu.make_async_copy(a, b, sems.at[i]) for i, (a, b) in enumerate(zip(sources, targets))]
    for i in (3, 4, 2, 0, 1):
        copies[i].start()
    depth_z = slots.shape[0]
    names[...] = jnp.zeros((8, 128), jnp.int32)
    copies[3].wait()
    names[:, :table.shape[1]] = jnp.broadcast_to(table[...], (8, table.shape[1]))
    copies[4].wait()
    copies[2].wait()
    ids = names[...]
    local = jnp.zeros((8, 128), jnp.float32)
    for offset in (-1, 0, 1):
        row = owner_of(offset) * FAC_DEV // 128
        values = jnp.broadcast_to(impedance[pl.ds(row, 1), :], (8, 128))
        local = jnp.where(ids // 128 == row, jnp.take_along_axis(values, ids % 128, axis=1), local)
    for z in range(depth_z):
        slot = slots[z]
        found = jnp.take_along_axis(local, jnp.maximum(slot - 1, 0), axis=1)
        damping[z] = jnp.where(slot > 0, found, 0.0)
    copies[0].wait()
    copies[1].wait()
    load = loader(adjoint, wind, damping)
    for i, (f, t) in enumerate(E_PLANES):
        zb[i] = load(f, t - 1)
    for i in range(Y_ROWS):
        yb[i] = pack_groups([(8 * j + s, (2 * i + j, s)) for j in range(2) for s in range(depth_z)], load)
    for i in range(D_ROWS):
        db[i] = pack_groups([(4 * j + DEPTH - t, (4 * i + j, t - 1)) for j in range(4) for t in (1, 2, 3)], load)


def pack_x_kernel(adjoint, wind, damping, zr, xa, xb):
    load = loader(adjoint, wind, damping)
    for i, (f, t) in enumerate(R_PLANES):
        zr[i] = load(f, t - 1)
    pack_pairs([functools.partial(load, *p) for p in own_planes(damping.shape[0])], xa, xb)


def edge_kernel(sides, zb, *rest):
    y_rows = merged_rows(rest[:sides])
    d_rows = merged_rows(rest[sides:2 * sides])
    planes = [functools.partial(lambda i: zb[i], i) for i in range(len(E_PLANES))]
    planes += [functools.partial(lambda row: row, row) for row in y_rows + d_rows]
    pack_pairs(planes, *rest[2 * sides:])


def coupled(middle, c, k):
    if c == 0:
        return middle[1 + k]
    if c == 1 + k:
        return middle[0]
    return None


def flux(wind, middle, c, k):
    value = wind * middle[c]
    other = coupled(middle, c, k)
    return value if other is None else value + other


def put(cells, f, slot, tx, value):
    cells[f, slot, 8 * tx:8 * tx + 8, :] = value


def fill_kernel(sides, adjoint, wind, damping, saved_source, zb, zr, *rest):
    y_rows = merged_rows(rest[:sides])
    d_rows = merged_rows(rest[sides:2 * sides])
    xa, xb, cells, strips, saved, sem = rest[2 * sides:]
    copy = pltpu.make_async_copy(saved_source, saved, sem)
    copy.start()
    depth_z = damping.shape[0]
    zero = jnp.zeros((8, 128), jnp.float32)
    load = loader(adjoint, wind, damping)
    planes = own_planes(depth_z)
    for (f, s), value in zip(planes, unpack_pairs(xa, xb)):
        put(cells, f, DEPTH + s, 0, load(f, s))
        put(cells, f, DEPTH + s, 1, value)
    for ref, places in ((zb, E_PLANES), (zr, R_PLANES)):
        for i, (f, t) in enumerate(places):
            put(cells, f, DEPTH - t, 0, ref[i])
    for f in range(FIELDS):
        strips[f, 0:8, :] = unpack_strip(f, y_rows, d_rows)
    for f in range(9):
        put(cells, f, DEPTH + depth_z, 0, zero)
        put(cells, f, DEPTH + depth_z, 1, zero)
    for f, t in R_PLANES:
        put(cells, f, DEPTH - t, 1, zero)
    copy.wait()


def y_change(main, near, lanes):
    up = pltpu.roll(jnp.where(lanes == 0, near, main), 127, 1)
    return up - pltpu.roll(jnp.where(lanes == 127, near, main), 1, 1)


def step_kernel(cells_in, strips_in, ea, eb, saved, slots, table, cells, strips, own, part_a, part_b, prod, acc):
    del cells_in, strips_in
    depth_z = slots.shape[0]
    far = DEPTH + depth_z
    edges = unpack_pairs(ea, eb)
    for (f, t), value in zip(E_PLANES, edges):
        put(cells, f, DEPTH - t, 1, value)
    start = len(E_PLANES)
    for f in range(FIELDS):
        strips[f, 8:16, :] = unpack_strip(f, edges[start:start + Y_ROWS], edges[start + Y_ROWS:])

    tile = (16, 128)
    rows, lanes = iota(0, tile), iota(1, tile)
    groups, k = lanes // GROUP, lanes % GROUP
    x, y = lax.axis_index("gx"), lax.axis_index("gy")
    row_end = jnp.where(x == lax.axis_size("gx") - 1, 8, 12)
    row_restart = jnp.where(x == 0, 16, 12)
    inside = (rows < row_end) | (rows >= row_restart)
    k_first = jnp.where(y == 0, DEPTH, 0)
    k_end = jnp.where(y == lax.axis_size("gy") - 1, DEPTH, GROUP)
    factor = jnp.where(inside, jnp.float32(0.5 * SCALE), 0.0)
    side_factor = jnp.where((k >= k_first) & (k < k_end) & (lanes < GROUP * far), factor, 0.0)
    sign = z_sign()

    def full_step(first, middle_at, upper_at):
        side = [strips[middle_at + c] for c in range(4)]
        side_y = [flux(strips[10], side, c, 2) for c in range(4)]

        def body(slot, joined):
            middle = [cells[middle_at + c, slot] for c in range(4)]
            above = [cells[middle_at + c, slot + 1] for c in range(4)]
            below = [cells[middle_at + c, slot - 1] for c in range(4)]
            wind_up, wind_down = cells[8, slot + 1], cells[8, slot - 1]
            wind_x, wind_y = cells[9, slot], cells[10, slot]
            loss = SCALE * cells[11, slot]
            seen = []
            for c in range(4):
                total = sign * (flux(wind_up, above, c, 0) - flux(wind_down, below, c, 0))
                along = flux(wind_x, middle, c, 1)
                total += pltpu.roll(along, 15, 0) - pltpu.roll(along, 1, 0)
                along = flux(wind_y, middle, c, 2)
                total += y_change(along, pltpu.roll(side_y[c], 124 - GROUP * slot, 1), lanes)
                seen.append(jnp.where(groups == slot, pltpu.roll(along, GROUP * slot + DEPTH, 1), joined[c]))
                cells[upper_at + c, slot] = cells[upper_at + c, slot] + factor * total - loss * middle[c]
            return tuple(seen)

        joined = lax.fori_loop(first, far, body, tuple(jnp.zeros(tile, jnp.float32) for _ in range(4)))
        loss = SCALE * strips[11]
        for c in range(4):
            along = flux(strips[8], side, c, 0)
            total = sign * (pltpu.roll(along, 128 - GROUP, 1) - pltpu.roll(along, GROUP, 1))
            along = flux(strips[9], side, c, 1)
            total += pltpu.roll(along, 15, 0) - pltpu.roll(along, 1, 0)
            total += pltpu.roll(jnp.where(k == DEPTH, joined[c], side_y[c]), 127, 1)
            total -= pltpu.roll(jnp.where(k == DEPTH - 1, joined[c], side_y[c]), 1, 1)
            strips[upper_at + c] = strips[upper_at + c] + side_factor * total - loss * side[c]

    def products(step, middle_at, slot, z):
        return sum(cells[middle_at + c, slot, 0:8, :] * saved[step, c, z] for c in range(4))

    full_step(1, 0, 4)
    for s in range(depth_z):
        z = z_of(s, depth_z)
        prod[z] = products(0, 0, DEPTH + s, z) + products(1, 4, DEPTH + s, z)
    full_step(2, 4, 0)
    full_step(3, 0, 4)
    for s in range(depth_z):
        z = z_of(s, depth_z)
        prod[z] = -SCALE * (prod[z] + (products(2, 0, DEPTH + s, z) + products(3, 4, DEPTH + s, z)))

    slot_count = table.shape[1]
    level = iota(0, (slot_count, 128)) + 1
    acc[...] = jnp.zeros((slot_count, 128), jnp.float32)

    def by_slot(z, carry):
        total = acc[...]
        for row in range(8):
            cell_slot = jnp.broadcast_to(slots[z, row:row + 1, :], (slot_count, 128))
            term = jnp.broadcast_to(prod[z, row:row + 1, :], (slot_count, 128))
            total = total + jnp.where(cell_slot == level, term, 0.0)
        acc[...] = total
        return carry

    lax.fori_loop(0, depth_z, by_slot, 0)
    slot_terms = jnp.sum(acc[...], axis=1, keepdims=True)
    names = jnp.broadcast_to(table[...], (slot_count, slot_count))
    diagonal = iota(0, (slot_count, slot_count)) == iota(1, (slot_count, slot_count))
    column = jnp.sum(jnp.where(diagonal, names, 0).astype(jnp.float32), axis=1, keepdims=True)
    lane = iota(1, (slot_count, 128))

    def bucket(offset):
        target = jnp.where(lane < FAC_DEV, owner_of(offset) * FAC_DEV + lane, -1).astype(jnp.float32)
        return jnp.sum(jnp.where(column == target, slot_terms, 0.0), axis=0, keepdims=True)

    upward, downward = bucket(1), bucket(-1)
    own[...] = bucket(0)
    even = is_even("gx")
    part_a[...] = jnp.where(even, upward, downward)
    part_b[...] = jnp.where(even, downward, upward)


def last_kernel(cells, strips, out):
    middle_at, upper_at = 4, 0
    depth_z = out.shape[2]
    sign = z_sign()
    lanes = iota(1)
    side = [strips[middle_at + c, 0:8] for c in range(4)]
    side_y = [flux(strips[10, 0:8], side, c, 2) for c in range(4)]

    def body(s, carry):
        slot = DEPTH + s

        def plane(f, at):
            return cells[f, at, 0:8, :]

        middle = [plane(middle_at + c, slot) for c in range(4)]
        above = [plane(middle_at + c, slot + 1) for c in range(4)]
        below = [plane(middle_at + c, slot - 1) for c in range(4)]
        wide = [cells[middle_at + c, slot] for c in range(4)]
        wind_up, wind_down = plane(8, slot + 1), plane(8, slot - 1)
        wind_x, wind_y = cells[9, slot], plane(10, slot)
        loss = SCALE * plane(11, slot)
        z = z_of(s, depth_z)
        for c in range(4):
            total = sign * (flux(wind_up, above, c, 0) - flux(wind_down, below, c, 0))
            along = flux(wind_x, wide, c, 1)
            total += (pltpu.roll(along, 15, 0) - pltpu.roll(along, 1, 0))[0:8]
            along = flux(wind_y, middle, c, 2)
            total += y_change(along, pltpu.roll(side_y[c], 124 - GROUP * slot, 1), lanes)
            out[0, c, z] = middle[c]
            out[1, c, z] = plane(upper_at + c, slot) + jnp.float32(0.5 * SCALE) * total - loss * middle[c]
        return carry

    lax.fori_loop(0, depth_z, body, 0)


AXES = ("gx", "gy", "gz")


def swap(block, partner):
    counts = tuple(lax.axis_size(axis) for axis in AXES)
    pairs = []
    for place in np.ndindex(*counts):
        other = partner(*place, counts)
        pairs.append((int(np.ravel_multi_index(place, counts)), int(np.ravel_multi_index(other, counts))))
    return lax.ppermute(block, AXES, pairs)


def swap_z(x, y, z, counts):
    return x, y, z ^ 1


def swap_xa(x, y, z, counts):
    return x ^ 1, y, z


def swap_xb(x, y, z, counts):
    other = x + 1 if x % 2 else x - 1
    return (other, y, z) if 0 <= other < counts[0] else (x, y ^ 1, z)


def swap_ring(x, y, z, counts):
    return (x + 1 if x % 2 else x - 1) % counts[0], y, z


def swap_y(side, diagonal):
    def partner(x, y, z, counts):
        other = y ^ 1 if side == 0 else y + 1 if y % 2 else y - 1
        if 0 <= other < counts[1]:
            return x, other, z ^ 1 if diagonal else z
        return x, y, z ^ 1

    return partner


VMEM = pl.BlockSpec(memory_space=pltpu.VMEM)
HBM = pl.BlockSpec(memory_space=pltpu.HBM)


def call(kernel, limit, in_specs, out_shape, scratch=(), aliases=None, cost=None):
    return pl.pallas_call(
        kernel,
        out_shape=[jax.ShapeDtypeStruct(o.shape, o.dtype) for o in out_shape],
        in_specs=in_specs,
        out_specs=[VMEM] * len(out_shape),
        scratch_shapes=list(scratch),
        input_output_aliases=aliases or {},
        compiler_params=pltpu.CompilerParams(vmem_limit_bytes=limit << 20),
        cost_estimate=cost and pl.CostEstimate(flops=cost, bytes_accessed=cost, transcendentals=0),
    )


def in_hbm(array):
    return pltpu.with_memory_space_constraint(array, pltpu.HBM)


def rows_of(count):
    return jax.ShapeDtypeStruct((count, 8, 128), jnp.float32)


def local(adjoint, saved_state, wind_field, facade_slot, facade_table, impedance):
    depth_z = facade_slot.shape[0]
    sides = 1 if lax.axis_size("gy") == 2 else 2
    table = facade_table.reshape(1, -1)
    rates = impedance.reshape(-1, 128)
    adjoint, wind, slots, table, damping, zb, yb, db = call(
        pack_kernel,
        4,
        [HBM] * 5,
        [adjoint, wind_field, facade_slot, table, rows_of(depth_z), rows_of(len(E_PLANES)), rows_of(Y_ROWS), rows_of(D_ROWS)],
        [pltpu.VMEM(rates.shape, jnp.float32), pltpu.VMEM((8, 128), jnp.int32), pltpu.SemaphoreType.DMA((5,))],
    )(*map(in_hbm, (adjoint, wind_field, facade_slot, table, rates)))
    zr, xa, xb = call(
        pack_x_kernel, 2, [VMEM] * 3, [rows_of(len(R_PLANES))] + [rows_of(FIELDS * depth_z // 2)] * 2, cost=400000
    )(adjoint, wind, damping)
    zb = swap(zb, swap_z)
    ds = [swap(db, swap_y(side, True)) for side in range(sides)]
    ys = [swap(yb, swap_y(side, False)) for side in range(sides)]
    xa = swap(xa, swap_xa)
    xb = swap(xb, swap_xb)
    zr = swap(zr, swap_z)
    edge_count = (len(E_PLANES) + Y_ROWS + D_ROWS + 1) // 2
    ea, eb = call(
        functools.partial(edge_kernel, sides), 2, [VMEM] * (1 + 2 * sides), [rows_of(edge_count)] * 2
    )(zb, *ys, *ds)
    ea = swap(ea, swap_xa)
    eb = swap(eb, swap_xb)
    cells = jax.ShapeDtypeStruct((FIELDS, DEPTH + depth_z + 1, 16, 128), jnp.float32)
    strips = jax.ShapeDtypeStruct((FIELDS, 16, 128), jnp.float32)
    cells, strips, saved = call(
        functools.partial(fill_kernel, sides),
        2,
        [VMEM] * 3 + [HBM] + [VMEM] * (4 + 2 * sides),
        [cells, strips, saved_state],
        [pltpu.SemaphoreType.DMA],
        cost=4000000,
    )(adjoint, wind, damping, in_hbm(saved_state), zb, zr, *ys, *ds, xa, xb)
    row = jax.ShapeDtypeStruct((1, 128), jnp.float32)
    cells, strips, own, part_a, part_b = call(
        step_kernel,
        2,
        [VMEM] * 7,
        [cells, strips, row, row, row],
        [pltpu.VMEM((depth_z, 8, 128), jnp.float32), pltpu.VMEM((table.shape[1], 128), jnp.float32)],
        aliases={0: 0, 1: 1},
    )(cells, strips, ea, eb, saved, slots, table)
    part_b = swap(part_b, swap_ring)
    part_a = swap(part_a, swap_xa)
    out, = call(last_kernel, 2, [VMEM] * 2, [adjoint], cost=4000000)(cells, strips)
    gradient = (own + part_a + part_b)[0, :FAC_DEV]
    return out, gradient


def solution(mesh):
    return jax.shard_map(
        local,
        mesh=mesh,
        in_specs=(
            P(None, None, "gz", "gx", "gy"),
            P(None, None, "gz", "gx", "gy"),
            P(None, "gz", "gx", "gy"),
            P("gz", "gx", "gy"),
            P("gz", "gx", "gy", None),
            P(),
        ),
        out_specs=(P(None, None, "gz", "gx", "gy"), P(("gx", "gy", "gz"))),
        check_vma=False,
    )
```

time: 29.3 us -> 30 us (1.024)
  starting transfers between devices: 15.3 us -> 11.6 us
  waiting for transfers between devices: 4.48 us -> 6.92 us
  Pallas kernels: 8.07 us -> 10 us
    ppermute x9 -> x10, starting transfers between devices: 15.3 us -> 11.6 us  [swap(): return lax.ppermute(block, AXES, pairs)]
    ppermute x9 -> x10, waiting for transfers between devices: 4.48 us -> 6.92 us  [swap(): return lax.ppermute(block, AXES, pairs)]
    pallas_call x5 -> x6, Pallas kernels: 8.07 us -> 10 us  [the longest x1 5.68 us: local(): call(step_kernel, 2, [VMEM] * 7, [cells, strips, row, row, row], [pltpu.V...]
  transfers between devices with their start and end apart: 9 -> 10, of which waited for: 1 -> 3; matrix products, arithmetic and copies ran while one was open for 0% -> 0% of each run, Pallas kernels for 9% -> 10%
where the time goes in v3:
time: 30 us; the launch traced here: 29.8 us
  starting transfers between devices  11.6 us (39%)
  Pallas kernels  10 us (33%)
  waiting for transfers between devices  6.92 us (23%)
  between operations  0.7 us (2%)
  local copies, waits for them, and re-layouts  0.51 us (2%)
    ppermute x10, starting transfers between devices, swap(): return lax.ppermute(block, AXES, pairs)  11.6 us
    ppermute x10, waiting for transfers between devices, swap(): return lax.ppermute(block, AXES, pairs)  6.92 us
    pallas_call x1, Pallas kernels, local(): call(step_kernel, 2, [VMEM] * 7, [cells, strips, row, row, row], [pltpu.V...  5.68 us
    pallas_call x1, Pallas kernels, local(): call(last_kernel, 2, [VMEM] * 2, [adjoint], cost=4000000)(cells, strips)  1.9 us
    pallas_call x1, Pallas kernels, local(): call(pack_kernel, 4, [HBM] * 5, [adjoint, wind_field, facade_slot, table,...  1.28 us
    pallas_call x1, Pallas kernels, local(): call(functools.partial(fill_kernel, sides), 2, [VMEM] * 3 + [HBM] + [VMEM...  1.08 us
  transfers between devices with their start and end apart: 10, of which 3 were waited for; matrix products, arithmetic and copies ran while one was open for 0% of the time, Pallas kernels for 10%

profile of v3, /device:TPU:0, one launch (start us, length us, event | category | flops | bytes accessed | tf_op | source)
XLA Modules:
  0.0 29.8 jit_solution(13983808221625296936)
XLA Ops:
  0.6 1.3 %shard_map.77 = (f32[2,4,8,8,128]{4,3,2,1,0:T(8,128)S(1)}, f32[3,8,8,128]{3,2,1,0:T(8,128)S(1)}, s32[8,8,128]{2,1,0:T(8,128)S(1)}, s32[1,64]{1,0:T(1,128)S(1)}, ...) custom-call(f32[2,4,8,8,128]{4,3,2,1,0:T(8,128)} %refs_0_.1, ...), custom_call_target="tpu_custom_call" | custom-call | tf_op jit(solution)/shard_map/pallas_call | solution.py:444
  1.9 3.0 %collective-permute-start = (f32[30,8,128]{2,1,0:T(8,128)S(1)}, f32[30,8,128]{2,1,0:T(8,128)S(1)}, u32[]{:S(2)}, u32[]{:S(2)}) collective-permute-start(f32[30,8,128]{2,1,0:T(8,128)S(1)} %get-tuple-element.26), channel_id=1, source_target_pairs={{0,1},{1,0},{2,3},{3,2},{4,5},{5,4},{6,7},{7,6},{8,9},{9,8},{10,11... | collective-permute-start | bytes 368648 | tf_op jit(solution)/shard_map/ppermute | solution.py:384
  5.0 0.1 shard_map.78
  5.0 0.1 collective-permute-start.4
  5.1 1.6 %collective-permute-start.5 = (f32[48,8,128]{2,1,0:T(8,128)S(1)}, f32[48,8,128]{2,1,0:T(8,128)S(1)}, u32[]{:S(2)}, u32[]{:S(2)}) collective-permute-start(f32[48,8,128]{2,1,0:T(8,128)S(1)} %get-tuple-element.31), channel_id=1, source_target_pairs={{0,2},{1,3},{2,0},{3,1},{4,8},{5,9},{6,10},{7,11},{8,4},{9,5},{10,... | collective-permute-start | bytes 589832 | tf_op jit(solution)/shard_map/ppermute | solution.py:384
  6.7 0.5 %collective-permute-start.2 = (f32[6,8,128]{2,1,0:T(8,128)S(1)}, f32[6,8,128]{2,1,0:T(8,128)S(1)}, u32[]{:S(2)}, u32[]{:S(2)}) collective-permute-start(f32[6,8,128]{2,1,0:T(8,128)S(1)} %get-tuple-element.28), channel_id=1, source_target_pairs={{0,2},{1,3},{2,0},{3,1},{4,6},{5,7},{6,4},{7,5},{8,10},{9,11},{10,... | collective-permute-start | bytes 73736 | tf_op jit(solution)/shard_map/ppermute | solution.py:384
  7.2 1.5 %collective-permute-start.3 = (f32[3,8,128]{2,1,0:T(8,128)S(1)}, f32[3,8,128]{2,1,0:T(8,128)S(1)}, u32[]{:S(2)}, u32[]{:S(2)}) collective-permute-start(f32[3,8,128]{2,1,0:T(8,128)S(1)} %get-tuple-element.29), channel_id=1, source_target_pairs={{0,3},{1,2},{2,1},{3,0},{4,7},{5,6},{6,5},{7,4},{8,11},{9,10},{10,... | collective-permute-start | bytes 36872 | tf_op jit(solution)/shard_map/ppermute | solution.py:384
  8.7 3.2 %collective-permute-done.3.rest_1_ = f32[3,8,128]{2,1,0:T(8,128)S(1)} collective-permute-done((f32[3,8,128]{2,1,0:T(8,128)S(1)}, f32[3,8,128]{2,1,0:T(8,128)S(1)}, u32[]{:S(2)}, u32[]{:S(2)}) %collective-permute-start.3) | collective-permute-done | bytes 12320 | tf_op jit(solution)/shard_map/ppermute | solution.py:384
  11.8 0.0 collective-permute-done.2.rest_0_
  11.8 0.0 collective-permute-done.zb
  11.9 0.1 collective-permute-start.6
  12.0 1.5 %collective-permute-start.7 = (f32[20,8,128]{2,1,0:T(8,128)S(1)}, f32[20,8,128]{2,1,0:T(8,128)S(1)}, u32[]{:S(2)}, u32[]{:S(2)}) collective-permute-start(f32[20,8,128]{2,1,0:T(8,128)S(1)} %get-tuple-element.35), channel_id=1, source_target_pairs={{0,2},{1,3},{2,0},{3,1},{4,8},{5,9},{6,10},{7,11},{8,4},{9,5},{10,... | collective-permute-start | bytes 245768 | tf_op jit(solution)/shard_map/ppermute | solution.py:384
  13.5 0.5 %collective-permute-start.1 = (f32[11,8,128]{2,1,0:T(8,128)S(1)}, f32[11,8,128]{2,1,0:T(8,128)S(1)}, u32[]{:S(2)}, u32[]{:S(2)}) collective-permute-start(f32[11,8,128]{2,1,0:T(8,128)S(1)} %get-tuple-element.27), channel_id=1, source_target_pairs={{0,1},{1,0},{2,3},{3,2},{4,5},{5,4},{6,7},{7,6},{8,9},{9,8},{10,11... | collective-permute-start | bytes 135176 | tf_op jit(solution)/shard_map/ppermute | solution.py:384
  14.0 3.5 %collective-permute-done.1.zr = f32[11,8,128]{2,1,0:T(8,128)S(1)} collective-permute-done((f32[11,8,128]{2,1,0:T(8,128)S(1)}, f32[11,8,128]{2,1,0:T(8,128)S(1)}, u32[]{:S(2)}, u32[]{:S(2)}) %collective-permute-start.1) | collective-permute-done | bytes 45088 | tf_op jit(solution)/shard_map/ppermute | solution.py:384
  17.5 0.0 collective-permute-done.4.rest_2_
  17.5 0.0 collective-permute-done.5.rest_3_
  17.5 1.1 %shard_map.79 = (f32[12,13,16,128]{3,2,1,0:T(8,128)S(1)}, f32[12,16,128]{2,1,0:T(8,128)S(1)}, f32[4,4,8,8,128]{4,3,2,1,0:T(8,128)S(1)}) custom-call(f32[2,4,8,8,128]{4,3,2,1,0:T(8,128)S(1)} %get-tuple-element.23.adjoint, f32[3,8,8,128]{3,2,1,0:T(8,128)S(1)} %get-tuple-element.24.wind, f32[8,8,128]{2,1,0:T(8,128)S(1)} %get-tuple-element.25.damping, ...), custom_call_target="tpu_custom_call" | custom-call | flops 4000000 | bytes 4000000 | tf_op jit(solution)/shard_map/pallas_call | solution.py:468
  18.6 0.0 collective-permute-done.6.ea
  18.6 0.0 collective-permute-done.7.eb
  18.6 5.7 %shard_map.81 = (f32[12,13,16,128]{3,2,1,0:T(8,128)S(1)}, f32[12,16,128]{2,1,0:T(8,128)S(1)}, f32[1,128]{1,0:T(1,128)S(1)}, f32[1,128]{1,0:T(1,128)S(1)}, f32[1,128]{1,0:T(1,128)S(1)}) custom-call(f32[12,13,16,128]{3,2,1,0:T(8,128)S(1)} %get-tuple-element.32.cells_in, ...), custom_call_target="tpu_custom_call", output_to_operand_aliasing={{0}: (0, {}), {1}: (1, {})} | custom-call | tf_op jit(solution)/shard_map/pallas_call | solution.py:477
  24.3 0.1 collective-permute-start.8
  24.4 2.7 %collective-permute-start.9 = (f32[1,128]{1,0:T(1,128)S(1)}, f32[1,128]{1,0:T(1,128)S(1)}, u32[]{:S(2)}, u32[]{:S(2)}) collective-permute-start(f32[1,128]{1,0:T(1,128)S(1)} %get-tuple-element.43), channel_id=1, source_target_pairs={{0,28},{1,29},{2,30},{3,31},{4,8},{5,9},{6,10},{7,11},{8,4},{9,5},... | collective-permute-start | bytes 1544 | tf_op jit(solution)/shard_map/ppermute | solution.py:384
  27.1 1.9 %shard_map.82 = f32[2,4,8,8,128]{4,3,2,1,0:T(8,128)} custom-call(f32[12,13,16,128]{3,2,1,0:T(8,128)S(1)} %get-tuple-element.39.cells, f32[12,16,128]{2,1,0:T(8,128)S(1)} %get-tuple-element.40.strips), custom_call_target="tpu_custom_call" | custom-call | flops 4000000 | bytes 4000000 | tf_op jit(solution)/shard_map/pallas_call | solution.py:487
  29.0 0.0 collective-permute-done.8
  29.1 0.2 collective-permute-done.9
  29.3 0.5 %slice_bitcast_fusion = f32[32]{0:T(128)} fusion(f32[1,128]{1,0:T(1,128)S(1)} %add_add_fusion), kind=kLoop, calls=%fused_computation | loop fusion | bytes 256 | tf_op jit(solution)/shard_map/squeeze | solution.py:488
  (2 shorter events, 0.0 us)
Async XLA Ops:
  1.9 9.9 %collective-permute-start = (f32[30,8,128]{2,1,0:T(8,128)S(1)}, f32[30,8,128]{2,1,0:T(8,128)S(1)}, u32[]{:S(2)}, u32[]{:S(2)}) collective-permute-start(f32[30,8,128]{2,1,0:T(8,128)S(1)} %get-tuple-element.26), channel_id=1, source_target_pairs={{0,1},{1,0},{2,3},{3,2},{4,5},{5,4},{6,7},{7,6},{8,9},{9,8},{10,11... | collective-permute-start | bytes 368648 | tf_op jit(solution)/shard_map/ppermute | solution.py:384
  5.0 12.5 %collective-permute-start.4 = (f32[48,8,128]{2,1,0:T(8,128)S(1)}, f32[48,8,128]{2,1,0:T(8,128)S(1)}, u32[]{:S(2)}, u32[]{:S(2)}) collective-permute-start(f32[48,8,128]{2,1,0:T(8,128)S(1)} %get-tuple-element.30), channel_id=1, source_target_pairs={{0,4},{1,5},{2,6},{3,7},{4,0},{5,1},{6,2},{7,3},{8,12},{9,13},{10,... | collective-permute-start | bytes 589832 | tf_op jit(solution)/shard_map/ppermute | solution.py:384
  5.1 12.4 %collective-permute-start.5 = (f32[48,8,128]{2,1,0:T(8,128)S(1)}, f32[48,8,128]{2,1,0:T(8,128)S(1)}, u32[]{:S(2)}, u32[]{:S(2)}) collective-permute-start(f32[48,8,128]{2,1,0:T(8,128)S(1)} %get-tuple-element.31), channel_id=1, source_target_pairs={{0,2},{1,3},{2,0},{3,1},{4,8},{5,9},{6,10},{7,11},{8,4},{9,5},{10,... | collective-permute-start | bytes 589832 | tf_op jit(solution)/shard_map/ppermute | solution.py:384
  6.7 5.2 %collective-permute-start.2 = (f32[6,8,128]{2,1,0:T(8,128)S(1)}, f32[6,8,128]{2,1,0:T(8,128)S(1)}, u32[]{:S(2)}, u32[]{:S(2)}) collective-permute-start(f32[6,8,128]{2,1,0:T(8,128)S(1)} %get-tuple-element.28), channel_id=1, source_target_pairs={{0,2},{1,3},{2,0},{3,1},{4,6},{5,7},{6,4},{7,5},{8,10},{9,11},{10,... | collective-permute-start | bytes 73736 | tf_op jit(solution)/shard_map/ppermute | solution.py:384
  7.2 4.7 %collective-permute-start.3 = (f32[3,8,128]{2,1,0:T(8,128)S(1)}, f32[3,8,128]{2,1,0:T(8,128)S(1)}, u32[]{:S(2)}, u32[]{:S(2)}) collective-permute-start(f32[3,8,128]{2,1,0:T(8,128)S(1)} %get-tuple-element.29), channel_id=1, source_target_pairs={{0,3},{1,2},{2,1},{3,0},{4,7},{5,6},{6,5},{7,4},{8,11},{9,10},{10,... | collective-permute-start | bytes 36872 | tf_op jit(solution)/shard_map/ppermute | solution.py:384
  11.9 6.7 %collective-permute-start.6 = (f32[20,8,128]{2,1,0:T(8,128)S(1)}, f32[20,8,128]{2,1,0:T(8,128)S(1)}, u32[]{:S(2)}, u32[]{:S(2)}) collective-permute-start(f32[20,8,128]{2,1,0:T(8,128)S(1)} %get-tuple-element.34), channel_id=1, source_target_pairs={{0,4},{1,5},{2,6},{3,7},{4,0},{5,1},{6,2},{7,3},{8,12},{9,13},{10,... | collective-permute-start | bytes 245768 | tf_op jit(solution)/shard_map/ppermute | solution.py:384
  12.0 6.6 %collective-permute-start.7 = (f32[20,8,128]{2,1,0:T(8,128)S(1)}, f32[20,8,128]{2,1,0:T(8,128)S(1)}, u32[]{:S(2)}, u32[]{:S(2)}) collective-permute-start(f32[20,8,128]{2,1,0:T(8,128)S(1)} %get-tuple-element.35), channel_id=1, source_target_pairs={{0,2},{1,3},{2,0},{3,1},{4,8},{5,9},{6,10},{7,11},{8,4},{9,5},{10,... | collective-permute-start | bytes 245768 | tf_op jit(solution)/shard_map/ppermute | solution.py:384
  13.5 4.0 %collective-permute-start.1 = (f32[11,8,128]{2,1,0:T(8,128)S(1)}, f32[11,8,128]{2,1,0:T(8,128)S(1)}, u32[]{:S(2)}, u32[]{:S(2)}) collective-permute-start(f32[11,8,128]{2,1,0:T(8,128)S(1)} %get-tuple-element.27), channel_id=1, source_target_pairs={{0,1},{1,0},{2,3},{3,2},{4,5},{5,4},{6,7},{7,6},{8,9},{9,8},{10,11... | collective-permute-start | bytes 135176 | tf_op jit(solution)/shard_map/ppermute | solution.py:384
  24.3 4.7 %collective-permute-start.8 = (f32[1,128]{1,0:T(1,128)S(1)}, f32[1,128]{1,0:T(1,128)S(1)}, u32[]{:S(2)}, u32[]{:S(2)}) collective-permute-start(f32[1,128]{1,0:T(1,128)S(1)} %get-tuple-element.42), channel_id=1, source_target_pairs={{0,4},{1,5},{2,6},{3,7},{4,0},{5,1},{6,2},{7,3},{8,12},{9,13},{10,... | collective-permute-start | bytes 1544 | tf_op jit(solution)/shard_map/ppermute | solution.py:384
  24.4 4.9 %collective-permute-start.9 = (f32[1,128]{1,0:T(1,128)S(1)}, f32[1,128]{1,0:T(1,128)S(1)}, u32[]{:S(2)}, u32[]{:S(2)}) collective-permute-start(f32[1,128]{1,0:T(1,128)S(1)} %get-tuple-element.43), channel_id=1, source_target_pairs={{0,28},{1,29},{2,30},{3,31},{4,8},{5,9},{6,10},{7,11},{8,4},{9,5},... | collective-permute-start | bytes 1544 | tf_op jit(solution)/shard_map/ppermute | solution.py:384

commit v4 on v3

--- a/solution.py
+++ b/solution.py
@@ -15,7 +15,9 @@
 
 FIELDS = 12
 DEPTH = 4
+BASE = DEPTH + 1
 GROUP = 2 * DEPTH
+CHUNK = 6
 E_PLANES = [(f, t) for t in (1, 2) for f in range(FIELDS)] + [(f, 3) for f in (0, 1, 2, 3, 8, 9)]
 R_PLANES = [(f, 3) for f in (4, 5, 6, 7, 10, 11)] + [(f, 4) for f in (0, 1, 2, 3, 8)]
 Y_ROWS = FIELDS // 2
@@ -57,9 +59,9 @@
 
 def unpack_strip(f, y_rows, d_rows):
     lanes = iota(1)
-    start = DEPTH * GROUP
+    start = BASE * GROUP
     own = pltpu.roll(y_rows[f // 2], (start - 64 * (f % 2)) % 128, 1)
-    beyond = y_shift(d_rows[f // 4], -32 * (f % 4))
+    beyond = y_shift(d_rows[f // 4], GROUP - 32 * (f % 4))
     return jnp.where(lanes < start, beyond, jnp.where(lanes < start + 64, own, 0.0))
 
 
@@ -164,7 +166,7 @@
     copies[0].wait()
     copies[1].wait()
     load = loader(adjoint, wind, damping)
-    for i, (f, t) in enumerate(E_PLANES):
+    for i, (f, t) in enumerate(E_PLANES + R_PLANES):
         zb[i] = load(f, t - 1)
     for i in range(Y_ROWS):
         yb[i] = pack_groups([(8 * j + s, (2 * i + j, s)) for j in range(2) for s in range(depth_z)], load)
@@ -172,10 +174,8 @@
         db[i] = pack_groups([(4 * j + DEPTH - t, (4 * i + j, t - 1)) for j in range(4) for t in (1, 2, 3)], load)
 
 
-def pack_x_kernel(adjoint, wind, damping, zr, xa, xb):
+def pack_x_kernel(adjoint, wind, damping, xa, xb):
     load = loader(adjoint, wind, damping)
-    for i, (f, t) in enumerate(R_PLANES):
-        zr[i] = load(f, t - 1)
     pack_pairs([functools.partial(load, *p) for p in own_planes(damping.shape[0])], xa, xb)
 
 
@@ -205,44 +205,52 @@
     cells[f, slot, 8 * tx:8 * tx + 8, :] = value
 
 
-def fill_kernel(sides, adjoint, wind, damping, saved_source, zb, zr, *rest):
+def fetch_kernel(source, target, sem):
+    copy = pltpu.make_async_copy(source, target, sem)
+    copy.start()
+    copy.wait()
+
+
+def fill_kernel(sides, adjoint, wind, damping, zb, *rest):
     y_rows = merged_rows(rest[:sides])
     d_rows = merged_rows(rest[sides:2 * sides])
-    xa, xb, cells, strips, saved, sem = rest[2 * sides:]
-    copy = pltpu.make_async_copy(saved_source, saved, sem)
-    copy.start()
+    xa, xb, cells, strips = rest[2 * sides:]
     depth_z = damping.shape[0]
     zero = jnp.zeros((8, 128), jnp.float32)
     load = loader(adjoint, wind, damping)
     planes = own_planes(depth_z)
     for (f, s), value in zip(planes, unpack_pairs(xa, xb)):
-        put(cells, f, DEPTH + s, 0, load(f, s))
-        put(cells, f, DEPTH + s, 1, value)
-    for ref, places in ((zb, E_PLANES), (zr, R_PLANES)):
-        for i, (f, t) in enumerate(places):
-            put(cells, f, DEPTH - t, 0, ref[i])
+        put(cells, f, BASE + s, 0, load(f, s))
+        put(cells, f, BASE + s, 1, value)
+    for i, (f, t) in enumerate(E_PLANES + R_PLANES):
+        put(cells, f, BASE - t, 0, zb[i])
     for f in range(FIELDS):
         strips[f, 0:8, :] = unpack_strip(f, y_rows, d_rows)
-    for f in range(9):
-        put(cells, f, DEPTH + depth_z, 0, zero)
-        put(cells, f, DEPTH + depth_z, 1, zero)
+    for tx in range(2):
+        for f in range(9):
+            put(cells, f, BASE + depth_z, tx, zero)
+        for f in (0, 1, 2, 3, 8):
+            put(cells, f, 0, tx, zero)
+        for f in (4, 5, 6, 7, 9, 10, 11):
+            put(cells, f, 1, tx, zero)
     for f, t in R_PLANES:
-        put(cells, f, DEPTH - t, 1, zero)
-    copy.wait()
-
-
-def y_change(main, near, lanes):
-    up = pltpu.roll(jnp.where(lanes == 0, near, main), 127, 1)
-    return up - pltpu.roll(jnp.where(lanes == 127, near, main), 1, 1)
+        put(cells, f, BASE - t, 1, zero)
+
+
+def y_change(main, side, slot, lanes):
+    above = pltpu.roll(side, 127 - DEPTH - GROUP * slot, 1)
+    below = pltpu.roll(side, 129 - DEPTH - GROUP * slot, 1)
+    up = jnp.where(lanes == 127, above, pltpu.roll(main, 127, 1))
+    return up - jnp.where(lanes == 0, below, pltpu.roll(main, 1, 1))
 
 
 def step_kernel(cells_in, strips_in, ea, eb, saved, slots, table, cells, strips, own, part_a, part_b, prod, acc):
     del cells_in, strips_in
     depth_z = slots.shape[0]
-    far = DEPTH + depth_z
+    far = BASE + depth_z
     edges = unpack_pairs(ea, eb)
     for (f, t), value in zip(E_PLANES, edges):
-        put(cells, f, DEPTH - t, 1, value)
+        put(cells, f, BASE - t, 1, value)
     start = len(E_PLANES)
     for f in range(FIELDS):
         strips[f, 8:16, :] = unpack_strip(f, edges[start:start + Y_ROWS], edges[start + Y_ROWS:])
@@ -260,7 +268,8 @@
     side_factor = jnp.where((k >= k_first) & (k < k_end) & (lanes < GROUP * far), factor, 0.0)
     sign = z_sign()
 
-    def full_step(first, middle_at, upper_at):
+    def full_step(halo, middle_at, upper_at):
+        first = far - -(-(depth_z + halo) // CHUNK) * CHUNK
         side = [strips[middle_at + c] for c in range(4)]
         side_y = [flux(strips[10], side, c, 2) for c in range(4)]
 
@@ -277,12 +286,18 @@
                 along = flux(wind_x, middle, c, 1)
                 total += pltpu.roll(along, 15, 0) - pltpu.roll(along, 1, 0)
                 along = flux(wind_y, middle, c, 2)
-                total += y_change(along, pltpu.roll(side_y[c], 124 - GROUP * slot, 1), lanes)
+                total += y_change(along, side_y[c], slot, lanes)
                 seen.append(jnp.where(groups == slot, pltpu.roll(along, GROUP * slot + DEPTH, 1), joined[c]))
                 cells[upper_at + c, slot] = cells[upper_at + c, slot] + factor * total - loss * middle[c]
             return tuple(seen)
 
-        joined = lax.fori_loop(first, far, body, tuple(jnp.zeros(tile, jnp.float32) for _ in range(4)))
+        def chunk(i, joined):
+            for j in range(CHUNK):
+                joined = body(first + CHUNK * i + j, joined)
+            return joined
+
+        zeros = tuple(jnp.zeros(tile, jnp.float32) for _ in range(4))
+        joined = lax.fori_loop(0, (far - first) // CHUNK, chunk, zeros)
         loss = SCALE * strips[11]
         for c in range(4):
             along = flux(strips[8], side, c, 0)
@@ -296,15 +311,15 @@
     def products(step, middle_at, slot, z):
         return sum(cells[middle_at + c, slot, 0:8, :] * saved[step, c, z] for c in range(4))
 
+    full_step(3, 0, 4)
+    for s in range(depth_z):
+        z = z_of(s, depth_z)
+        prod[z] = products(0, 0, BASE + s, z) + products(1, 4, BASE + s, z)
+    full_step(2, 4, 0)
     full_step(1, 0, 4)
     for s in range(depth_z):
         z = z_of(s, depth_z)
-        prod[z] = products(0, 0, DEPTH + s, z) + products(1, 4, DEPTH + s, z)
-    full_step(2, 4, 0)
-    full_step(3, 0, 4)
-    for s in range(depth_z):
-        z = z_of(s, depth_z)
-        prod[z] = -SCALE * (prod[z] + (products(2, 0, DEPTH + s, z) + products(3, 4, DEPTH + s, z)))
+        prod[z] = -SCALE * (prod[z] + (products(2, 0, BASE + s, z) + products(3, 4, BASE + s, z)))
 
     slot_count = table.shape[1]
     level = iota(0, (slot_count, 128)) + 1
@@ -345,8 +360,8 @@
     side = [strips[middle_at + c, 0:8] for c in range(4)]
     side_y = [flux(strips[10, 0:8], side, c, 2) for c in range(4)]
 
-    def body(s, carry):
-        slot = DEPTH + s
+    def body(s):
+        slot = BASE + s
 
         def plane(f, at):
             return cells[f, at, 0:8, :]
@@ -364,12 +379,12 @@
             along = flux(wind_x, wide, c, 1)
             total += (pltpu.roll(along, 15, 0) - pltpu.roll(along, 1, 0))[0:8]
             along = flux(wind_y, middle, c, 2)
-            total += y_change(along, pltpu.roll(side_y[c], 124 - GROUP * slot, 1), lanes)
+            total += y_change(along, side_y[c], slot, lanes)
             out[0, c, z] = middle[c]
             out[1, c, z] = plane(upper_at + c, slot) + jnp.float32(0.5 * SCALE) * total - loss * middle[c]
-        return carry
-
-    lax.fori_loop(0, depth_z, body, 0)
+
+    for s in range(depth_z):
+        body(s)
 
 
 AXES = ("gx", "gy", "gz")
@@ -380,7 +395,8 @@
     pairs = []
     for place in np.ndindex(*counts):
         other = partner(*place, counts)
-        pairs.append((int(np.ravel_multi_index(place, counts)), int(np.ravel_multi_index(other, counts))))
+        if other is not None:
+            pairs.append((int(np.ravel_multi_index(place, counts)), int(np.ravel_multi_index(other, counts))))
     return lax.ppermute(block, AXES, pairs)
 
 
@@ -395,6 +411,11 @@
 def swap_xb(x, y, z, counts):
     other = x + 1 if x % 2 else x - 1
     return (other, y, z) if 0 <= other < counts[0] else (x, y ^ 1, z)
+
+
+def swap_xb_only(x, y, z, counts):
+    other = x + 1 if x % 2 else x - 1
+    return (other, y, z) if 0 <= other < counts[0] else None
 
 
 def swap_ring(x, y, z, counts):
@@ -445,34 +466,29 @@
         pack_kernel,
         4,
         [HBM] * 5,
-        [adjoint, wind_field, facade_slot, table, rows_of(depth_z), rows_of(len(E_PLANES)), rows_of(Y_ROWS), rows_of(D_ROWS)],
+        [adjoint, wind_field, facade_slot, table, rows_of(depth_z), rows_of(len(E_PLANES + R_PLANES)), rows_of(Y_ROWS), rows_of(D_ROWS)],
         [pltpu.VMEM(rates.shape, jnp.float32), pltpu.VMEM((8, 128), jnp.int32), pltpu.SemaphoreType.DMA((5,))],
     )(*map(in_hbm, (adjoint, wind_field, facade_slot, table, rates)))
-    zr, xa, xb = call(
-        pack_x_kernel, 2, [VMEM] * 3, [rows_of(len(R_PLANES))] + [rows_of(FIELDS * depth_z // 2)] * 2, cost=400000
+    xa, xb = call(
+        pack_x_kernel, 2, [VMEM] * 3, [rows_of(FIELDS * depth_z // 2)] * 2, cost=400000
     )(adjoint, wind, damping)
+    saved, = call(fetch_kernel, 1, [HBM], [saved_state], [pltpu.SemaphoreType.DMA], cost=4000000)(in_hbm(saved_state))
     zb = swap(zb, swap_z)
     ds = [swap(db, swap_y(side, True)) for side in range(sides)]
     ys = [swap(yb, swap_y(side, False)) for side in range(sides)]
     xa = swap(xa, swap_xa)
     xb = swap(xb, swap_xb)
-    zr = swap(zr, swap_z)
     edge_count = (len(E_PLANES) + Y_ROWS + D_ROWS + 1) // 2
     ea, eb = call(
         functools.partial(edge_kernel, sides), 2, [VMEM] * (1 + 2 * sides), [rows_of(edge_count)] * 2
     )(zb, *ys, *ds)
     ea = swap(ea, swap_xa)
-    eb = swap(eb, swap_xb)
-    cells = jax.ShapeDtypeStruct((FIELDS, DEPTH + depth_z + 1, 16, 128), jnp.float32)
+    eb = swap(eb, swap_xb_only)
+    cells = jax.ShapeDtypeStruct((FIELDS, BASE + depth_z + 1, 16, 128), jnp.float32)
     strips = jax.ShapeDtypeStruct((FIELDS, 16, 128), jnp.float32)
-    cells, strips, saved = call(
-        functools.partial(fill_kernel, sides),
-        2,
-        [VMEM] * 3 + [HBM] + [VMEM] * (4 + 2 * sides),
-        [cells, strips, saved_state],
-        [pltpu.SemaphoreType.DMA],
-        cost=4000000,
-    )(adjoint, wind, damping, in_hbm(saved_state), zb, zr, *ys, *ds, xa, xb)
+    cells, strips = call(
+        functools.partial(fill_kernel, sides), 2, [VMEM] * (6 + 2 * sides), [cells, strips], cost=4000000
+    )(adjoint, wind, damping, zb, *ys, *ds, xa, xb)
     row = jax.ShapeDtypeStruct((1, 128), jnp.float32)
     cells, strips, own, part_a, part_b = call(
         step_kernel,

time: 30 us -> 26.5 us (0.88)
  Pallas kernels: 10 us -> 6.22 us
  starting transfers between devices: 11.6 us -> 15 us
  waiting for transfers between devices: 6.92 us -> 3.92 us
    ppermute x10 -> x9, starting transfers between devices: 11.6 us -> 15 us  [swap(): return lax.ppermute(block, AXES, pairs)]
    ppermute x10 -> x9, waiting for transfers between devices: 6.92 us -> 3.92 us  [swap(): return lax.ppermute(block, AXES, pairs)]
    pallas_call x1, Pallas kernels: 5.68 us -> 2.76 us  [local(): call(step_kernel, 2, [VMEM] * 7, [cells, strips, row, row, row], [pltpu.V...]
    pallas_call x1, Pallas kernels: 1.9 us -> 0.92 us  [local(): call(last_kernel, 2, [VMEM] * 2, [adjoint], cost=4000000)(cells, strips)]
    pallas_call x2 -> x3, Pallas kernels: 1.14 us -> 1.24 us  [the longest x1 1.05 us: local(): call(fetch_kernel, 1, [HBM], [saved_state], [pltpu.SemaphoreType.DMA], co...]
  transfers between devices with their start and end apart: 10 -> 9, of which waited for: 3 -> 2; matrix products, arithmetic and copies ran while one was open for 0% -> 0% of each run, Pallas kernels for 10% -> 8%
where the time goes in v4:
time: 26.5 us; the launch traced here: 26.3 us
  starting transfers between devices  15 us (57%)
  Pallas kernels  6.22 us (23%)
  waiting for transfers between devices  3.92 us (15%)
  between operations  0.72 us (3%)
  local copies, waits for them, and re-layouts  0.51 us (2%)
    ppermute x9, starting transfers between devices, swap(): return lax.ppermute(block, AXES, pairs)  15 us
    ppermute x9, waiting for transfers between devices, swap(): return lax.ppermute(block, AXES, pairs)  3.92 us
    pallas_call x1, Pallas kernels, local(): call(step_kernel, 2, [VMEM] * 7, [cells, strips, row, row, row], [pltpu.V...  2.76 us
    pallas_call x1, Pallas kernels, local(): call(pack_kernel, 4, [HBM] * 5, [adjoint, wind_field, facade_slot, table,...  1.29 us
    pallas_call x1, Pallas kernels, local(): call(fetch_kernel, 1, [HBM], [saved_state], [pltpu.SemaphoreType.DMA], co...  1.05 us
    pallas_call x1, Pallas kernels, local(): call(last_kernel, 2, [VMEM] * 2, [adjoint], cost=4000000)(cells, strips)  0.92 us
  transfers between devices with their start and end apart: 9, of which 2 were waited for; matrix products, arithmetic and copies ran while one was open for 0% of the time, Pallas kernels for 8%

profile of v4, /device:TPU:0, one launch (start us, length us, event | category | flops | bytes accessed | tf_op | source)
XLA Modules:
  0.0 26.3 jit_solution(3902067378969046541)
XLA Ops:
  0.6 1.3 %shard_map.77 = (f32[2,4,8,8,128]{4,3,2,1,0:T(8,128)S(1)}, f32[3,8,8,128]{3,2,1,0:T(8,128)S(1)}, s32[8,8,128]{2,1,0:T(8,128)S(1)}, s32[1,64]{1,0:T(1,128)S(1)}, ...) custom-call(f32[2,4,8,8,128]{4,3,2,1,0:T(8,128)} %refs_0_.1, ...), custom_call_target="tpu_custom_call" | custom-call | tf_op jit(solution)/shard_map/pallas_call | solution.py:465
  1.9 3.0 %collective-permute-start = (f32[41,8,128]{2,1,0:T(8,128)S(1)}, f32[41,8,128]{2,1,0:T(8,128)S(1)}, u32[]{:S(2)}, u32[]{:S(2)}) collective-permute-start(f32[41,8,128]{2,1,0:T(8,128)S(1)} %get-tuple-element.24), channel_id=1, source_target_pairs={{0,1},{1,0},{2,3},{3,2},{4,5},{5,4},{6,7},{7,6},{8,9},{9,8},{10,11... | collective-permute-start | bytes 503816 | tf_op jit(solution)/shard_map/ppermute | solution.py:400
  5.0 0.1 shard_map.78
  5.0 0.1 collective-permute-start.3
  5.1 1.6 %collective-permute-start.4 = (f32[48,8,128]{2,1,0:T(8,128)S(1)}, f32[48,8,128]{2,1,0:T(8,128)S(1)}, u32[]{:S(2)}, u32[]{:S(2)}) collective-permute-start(f32[48,8,128]{2,1,0:T(8,128)S(1)} %get-tuple-element.28), channel_id=1, source_target_pairs={{0,2},{1,3},{2,0},{3,1},{4,8},{5,9},{6,10},{7,11},{8,4},{9,5},{10,... | collective-permute-start | bytes 589832 | tf_op jit(solution)/shard_map/ppermute | solution.py:400
  6.7 0.5 %collective-permute-start.1 = (f32[6,8,128]{2,1,0:T(8,128)S(1)}, f32[6,8,128]{2,1,0:T(8,128)S(1)}, u32[]{:S(2)}, u32[]{:S(2)}) collective-permute-start(f32[6,8,128]{2,1,0:T(8,128)S(1)} %get-tuple-element.25), channel_id=1, source_target_pairs={{0,2},{1,3},{2,0},{3,1},{4,6},{5,7},{6,4},{7,5},{8,10},{9,11},{10,... | collective-permute-start | bytes 73736 | tf_op jit(solution)/shard_map/ppermute | solution.py:400
  7.2 1.5 %collective-permute-start.2 = (f32[3,8,128]{2,1,0:T(8,128)S(1)}, f32[3,8,128]{2,1,0:T(8,128)S(1)}, u32[]{:S(2)}, u32[]{:S(2)}) collective-permute-start(f32[3,8,128]{2,1,0:T(8,128)S(1)} %get-tuple-element.26), channel_id=1, source_target_pairs={{0,3},{1,2},{2,1},{3,0},{4,7},{5,6},{6,5},{7,4},{8,11},{9,10},{10,... | collective-permute-start | bytes 36872 | tf_op jit(solution)/shard_map/ppermute | solution.py:400
  8.7 3.2 %collective-permute-done.2.rest_1_ = f32[3,8,128]{2,1,0:T(8,128)S(1)} collective-permute-done((f32[3,8,128]{2,1,0:T(8,128)S(1)}, f32[3,8,128]{2,1,0:T(8,128)S(1)}, u32[]{:S(2)}, u32[]{:S(2)}) %collective-permute-start.2) | collective-permute-done | bytes 12320 | tf_op jit(solution)/shard_map/ppermute | solution.py:400
  11.8 0.0 collective-permute-done.1.rest_0_
  11.9 0.0 collective-permute-done.zb
  11.9 0.1 collective-permute-start.5
  12.0 0.7 %collective-permute-start.6 = (f32[20,8,128]{2,1,0:T(8,128)S(1)}, f32[20,8,128]{2,1,0:T(8,128)S(1)}, u32[]{:S(2)}, u32[]{:S(2)}) collective-permute-start(f32[20,8,128]{2,1,0:T(8,128)S(1)} %get-tuple-element.32), channel_id=1, source_target_pairs={{4,8},{5,9},{6,10},{7,11},{8,4},{9,5},{10,6},{11,7},{12,16},{13,17... | collective-permute-start | bytes 245768 | tf_op jit(solution)/shard_map/ppermute | solution.py:400
  12.7 1.1 %shard_map.81.saved = f32[4,4,8,8,128]{4,3,2,1,0:T(8,128)S(1)} custom-call(f32[4,4,8,8,128]{4,3,2,1,0:T(8,128)} %source.1), custom_call_target="tpu_custom_call" | custom-call | flops 4000000 | bytes 4000000 | tf_op jit(solution)/shard_map/pallas_call | solution.py:475
  13.7 0.0 collective-permute-done.3.rest_2_
  13.7 0.0 collective-permute-done.4.rest_3_
  13.7 0.1 shard_map.79
  13.9 0.0 collective-permute-done.5.ea
  13.9 0.0 collective-permute-done.6.eb
  13.9 2.8 %shard_map.82 = (f32[12,14,16,128]{3,2,1,0:T(8,128)S(1)}, f32[12,16,128]{2,1,0:T(8,128)S(1)}, f32[1,128]{1,0:T(1,128)S(1)}, f32[1,128]{1,0:T(1,128)S(1)}, f32[1,128]{1,0:T(1,128)S(1)}) custom-call(f32[12,14,16,128]{3,2,1,0:T(8,128)S(1)} %get-tuple-element.29.cells_in, ...), custom_call_target="tpu_custom_call", output_to_operand_aliasing={{0}: (0, {}), {1}: (1, {})} | custom-call | tf_op jit(solution)/shard_map/pallas_call | solution.py:493
  16.7 4.4 %collective-permute-start.7 = (f32[1,128]{1,0:T(1,128)S(1)}, f32[1,128]{1,0:T(1,128)S(1)}, u32[]{:S(2)}, u32[]{:S(2)}) collective-permute-start(f32[1,128]{1,0:T(1,128)S(1)} %get-tuple-element.38), channel_id=1, source_target_pairs={{0,4},{1,5},{2,6},{3,7},{4,0},{5,1},{6,2},{7,3},{8,12},{9,13},{10,... | collective-permute-start | bytes 1544 | tf_op jit(solution)/shard_map/ppermute | solution.py:400
  21.0 3.1 %collective-permute-start.8 = (f32[1,128]{1,0:T(1,128)S(1)}, f32[1,128]{1,0:T(1,128)S(1)}, u32[]{:S(2)}, u32[]{:S(2)}) collective-permute-start(f32[1,128]{1,0:T(1,128)S(1)} %get-tuple-element.39), channel_id=1, source_target_pairs={{0,28},{1,29},{2,30},{3,31},{4,8},{5,9},{6,10},{7,11},{8,4},{9,5},... | collective-permute-start | bytes 1544 | tf_op jit(solution)/shard_map/ppermute | solution.py:400
  24.2 0.9 %shard_map.83 = f32[2,4,8,8,128]{4,3,2,1,0:T(8,128)} custom-call(f32[12,14,16,128]{3,2,1,0:T(8,128)S(1)} %get-tuple-element.35.cells, f32[12,16,128]{2,1,0:T(8,128)S(1)} %get-tuple-element.36.strips), custom_call_target="tpu_custom_call" | custom-call | flops 4000000 | bytes 4000000 | tf_op jit(solution)/shard_map/pallas_call | solution.py:503
  25.1 0.0 collective-permute-done.7
  25.1 0.7 %collective-permute-done.8 = f32[1,128]{1,0:T(1,128)S(1)} collective-permute-done((f32[1,128]{1,0:T(1,128)S(1)}, f32[1,128]{1,0:T(1,128)S(1)}, u32[]{:S(2)}, u32[]{:S(2)}) %collective-permute-start.8) | collective-permute-done | bytes 544 | tf_op jit(solution)/shard_map/ppermute | solution.py:400
  25.8 0.5 %slice_bitcast_fusion = f32[32]{0:T(128)} fusion(f32[1,128]{1,0:T(1,128)S(1)} %add_add_fusion), kind=kLoop, calls=%fused_computation | loop fusion | bytes 256 | tf_op jit(solution)/shard_map/squeeze | solution.py:504
  (2 shorter events, 0.0 us)
Async XLA Ops:
  1.9 9.9 %collective-permute-start = (f32[41,8,128]{2,1,0:T(8,128)S(1)}, f32[41,8,128]{2,1,0:T(8,128)S(1)}, u32[]{:S(2)}, u32[]{:S(2)}) collective-permute-start(f32[41,8,128]{2,1,0:T(8,128)S(1)} %get-tuple-element.24), channel_id=1, source_target_pairs={{0,1},{1,0},{2,3},{3,2},{4,5},{5,4},{6,7},{7,6},{8,9},{9,8},{10,11... | collective-permute-start | bytes 503816 | tf_op jit(solution)/shard_map/ppermute | solution.py:400
  5.0 8.7 %collective-permute-start.3 = (f32[48,8,128]{2,1,0:T(8,128)S(1)}, f32[48,8,128]{2,1,0:T(8,128)S(1)}, u32[]{:S(2)}, u32[]{:S(2)}) collective-permute-start(f32[48,8,128]{2,1,0:T(8,128)S(1)} %get-tuple-element.27), channel_id=1, source_target_pairs={{0,4},{1,5},{2,6},{3,7},{4,0},{5,1},{6,2},{7,3},{8,12},{9,13},{10,... | collective-permute-start | bytes 589832 | tf_op jit(solution)/shard_map/ppermute | solution.py:400
  5.1 8.6 %collective-permute-start.4 = (f32[48,8,128]{2,1,0:T(8,128)S(1)}, f32[48,8,128]{2,1,0:T(8,128)S(1)}, u32[]{:S(2)}, u32[]{:S(2)}) collective-permute-start(f32[48,8,128]{2,1,0:T(8,128)S(1)} %get-tuple-element.28), channel_id=1, source_target_pairs={{0,2},{1,3},{2,0},{3,1},{4,8},{5,9},{6,10},{7,11},{8,4},{9,5},{10,... | collective-permute-start | bytes 589832 | tf_op jit(solution)/shard_map/ppermute | solution.py:400
  6.7 5.2 %collective-permute-start.1 = (f32[6,8,128]{2,1,0:T(8,128)S(1)}, f32[6,8,128]{2,1,0:T(8,128)S(1)}, u32[]{:S(2)}, u32[]{:S(2)}) collective-permute-start(f32[6,8,128]{2,1,0:T(8,128)S(1)} %get-tuple-element.25), channel_id=1, source_target_pairs={{0,2},{1,3},{2,0},{3,1},{4,6},{5,7},{6,4},{7,5},{8,10},{9,11},{10,... | collective-permute-start | bytes 73736 | tf_op jit(solution)/shard_map/ppermute | solution.py:400
  7.2 4.7 %collective-permute-start.2 = (f32[3,8,128]{2,1,0:T(8,128)S(1)}, f32[3,8,128]{2,1,0:T(8,128)S(1)}, u32[]{:S(2)}, u32[]{:S(2)}) collective-permute-start(f32[3,8,128]{2,1,0:T(8,128)S(1)} %get-tuple-element.26), channel_id=1, source_target_pairs={{0,3},{1,2},{2,1},{3,0},{4,7},{5,6},{6,5},{7,4},{8,11},{9,10},{10,... | collective-permute-start | bytes 36872 | tf_op jit(solution)/shard_map/ppermute | solution.py:400
  11.9 2.0 %collective-permute-start.5 = (f32[20,8,128]{2,1,0:T(8,128)S(1)}, f32[20,8,128]{2,1,0:T(8,128)S(1)}, u32[]{:S(2)}, u32[]{:S(2)}) collective-permute-start(f32[20,8,128]{2,1,0:T(8,128)S(1)} %get-tuple-element.31), channel_id=1, source_target_pairs={{0,4},{1,5},{2,6},{3,7},{4,0},{5,1},{6,2},{7,3},{8,12},{9,13},{10,... | collective-permute-start | bytes 245768 | tf_op jit(solution)/shard_map/ppermute | solution.py:400
  12.0 1.9 %collective-permute-start.6 = (f32[20,8,128]{2,1,0:T(8,128)S(1)}, f32[20,8,128]{2,1,0:T(8,128)S(1)}, u32[]{:S(2)}, u32[]{:S(2)}) collective-permute-start(f32[20,8,128]{2,1,0:T(8,128)S(1)} %get-tuple-element.32), channel_id=1, source_target_pairs={{4,8},{5,9},{6,10},{7,11},{8,4},{9,5},{10,6},{11,7},{12,16},{13,17... | collective-permute-start | bytes 245768 | tf_op jit(solution)/shard_map/ppermute | solution.py:400
  16.7 8.4 %collective-permute-start.7 = (f32[1,128]{1,0:T(1,128)S(1)}, f32[1,128]{1,0:T(1,128)S(1)}, u32[]{:S(2)}, u32[]{:S(2)}) collective-permute-start(f32[1,128]{1,0:T(1,128)S(1)} %get-tuple-element.38), channel_id=1, source_target_pairs={{0,4},{1,5},{2,6},{3,7},{4,0},{5,1},{6,2},{7,3},{8,12},{9,13},{10,... | collective-permute-start | bytes 1544 | tf_op jit(solution)/shard_map/ppermute | solution.py:400
  21.0 4.8 %collective-permute-start.8 = (f32[1,128]{1,0:T(1,128)S(1)}, f32[1,128]{1,0:T(1,128)S(1)}, u32[]{:S(2)}, u32[]{:S(2)}) collective-permute-start(f32[1,128]{1,0:T(1,128)S(1)} %get-tuple-element.39), channel_id=1, source_target_pairs={{0,28},{1,29},{2,30},{3,31},{4,8},{5,9},{6,10},{7,11},{8,4},{9,5},... | collective-permute-start | bytes 1544 | tf_op jit(solution)/shard_map/ppermute | solution.py:400

commit v5 on v4

--- a/solution.py
+++ b/solution.py
@@ -17,7 +17,7 @@
 DEPTH = 4
 BASE = DEPTH + 1
 GROUP = 2 * DEPTH
-CHUNK = 6
+PASSES = 2
 E_PLANES = [(f, t) for t in (1, 2) for f in range(FIELDS)] + [(f, 3) for f in (0, 1, 2, 3, 8, 9)]
 R_PLANES = [(f, 3) for f in (4, 5, 6, 7, 10, 11)] + [(f, 4) for f in (0, 1, 2, 3, 8)]
 Y_ROWS = FIELDS // 2
@@ -142,7 +142,7 @@
 
 def pack_kernel(*refs):
     sources = refs[:5]
-    adjoint, wind, slots, table, damping, zb, yb, db, impedance, names, sems = refs[5:]
+    adjoint, wind, slots, table, damping, zb, zr, yb, db, impedance, names, sems = refs[5:]
     targets = (adjoint, wind, slots, table, impedance)
     copies = [pltpu.make_async_copy(a, b, sems.at[i]) for i, (a, b) in enumerate(zip(sources, targets))]
     for i in (3, 4, 2, 0, 1):
@@ -166,8 +166,9 @@
     copies[0].wait()
     copies[1].wait()
     load = loader(adjoint, wind, damping)
-    for i, (f, t) in enumerate(E_PLANES + R_PLANES):
-        zb[i] = load(f, t - 1)
+    for ref, planes in ((zb, E_PLANES), (zr, R_PLANES)):
+        for i, (f, t) in enumerate(planes):
+            ref[i] = load(f, t - 1)
     for i in range(Y_ROWS):
         yb[i] = pack_groups([(8 * j + s, (2 * i + j, s)) for j in range(2) for s in range(depth_z)], load)
     for i in range(D_ROWS):
@@ -211,7 +212,7 @@
     copy.wait()
 
 
-def fill_kernel(sides, adjoint, wind, damping, zb, *rest):
+def fill_kernel(sides, adjoint, wind, damping, zb, zr, *rest):
     y_rows = merged_rows(rest[:sides])
     d_rows = merged_rows(rest[sides:2 * sides])
     xa, xb, cells, strips = rest[2 * sides:]
@@ -222,8 +223,9 @@
     for (f, s), value in zip(planes, unpack_pairs(xa, xb)):
         put(cells, f, BASE + s, 0, load(f, s))
         put(cells, f, BASE + s, 1, value)
-    for i, (f, t) in enumerate(E_PLANES + R_PLANES):
-        put(cells, f, BASE - t, 0, zb[i])
+    for ref, places in ((zb, E_PLANES), (zr, R_PLANES)):
+        for i, (f, t) in enumerate(places):
+            put(cells, f, BASE - t, 0, ref[i])
     for f in range(FIELDS):
         strips[f, 0:8, :] = unpack_strip(f, y_rows, d_rows)
     for tx in range(2):
@@ -269,7 +271,8 @@
     sign = z_sign()
 
     def full_step(halo, middle_at, upper_at):
-        first = far - -(-(depth_z + halo) // CHUNK) * CHUNK
+        size = -(-(depth_z + halo) // PASSES)
+        first = far - size * PASSES
         side = [strips[middle_at + c] for c in range(4)]
         side_y = [flux(strips[10], side, c, 2) for c in range(4)]
 
@@ -292,12 +295,12 @@
             return tuple(seen)
 
         def chunk(i, joined):
-            for j in range(CHUNK):
-                joined = body(first + CHUNK * i + j, joined)
+            for j in range(size):
+                joined = body(first + size * i + j, joined)
             return joined
 
         zeros = tuple(jnp.zeros(tile, jnp.float32) for _ in range(4))
-        joined = lax.fori_loop(0, (far - first) // CHUNK, chunk, zeros)
+        joined = lax.fori_loop(0, PASSES, chunk, zeros)
         loss = SCALE * strips[11]
         for c in range(4):
             along = flux(strips[8], side, c, 0)
@@ -325,16 +328,17 @@
     level = iota(0, (slot_count, 128)) + 1
     acc[...] = jnp.zeros((slot_count, 128), jnp.float32)
 
-    def by_slot(z, carry):
+    def by_slot(i, carry):
         total = acc[...]
-        for row in range(8):
-            cell_slot = jnp.broadcast_to(slots[z, row:row + 1, :], (slot_count, 128))
-            term = jnp.broadcast_to(prod[z, row:row + 1, :], (slot_count, 128))
-            total = total + jnp.where(cell_slot == level, term, 0.0)
+        for z in range(4):
+            for row in range(8):
+                cell_slot = jnp.broadcast_to(slots[4 * i + z, row:row + 1, :], (slot_count, 128))
+                term = jnp.broadcast_to(prod[4 * i + z, row:row + 1, :], (slot_count, 128))
+                total = total + jnp.where(cell_slot == level, term, 0.0)
         acc[...] = total
         return carry
 
-    lax.fori_loop(0, depth_z, by_slot, 0)
+    lax.fori_loop(0, depth_z // 4, by_slot, 0)
     slot_terms = jnp.sum(acc[...], axis=1, keepdims=True)
     names = jnp.broadcast_to(table[...], (slot_count, slot_count))
     diagonal = iota(0, (slot_count, slot_count)) == iota(1, (slot_count, slot_count))
@@ -462,11 +466,11 @@
     sides = 1 if lax.axis_size("gy") == 2 else 2
     table = facade_table.reshape(1, -1)
     rates = impedance.reshape(-1, 128)
-    adjoint, wind, slots, table, damping, zb, yb, db = call(
+    adjoint, wind, slots, table, damping, zb, zr, yb, db = call(
         pack_kernel,
         4,
         [HBM] * 5,
-        [adjoint, wind_field, facade_slot, table, rows_of(depth_z), rows_of(len(E_PLANES + R_PLANES)), rows_of(Y_ROWS), rows_of(D_ROWS)],
+        [adjoint, wind_field, facade_slot, table, rows_of(depth_z), rows_of(len(E_PLANES)), rows_of(len(R_PLANES)), rows_of(Y_ROWS), rows_of(D_ROWS)],
         [pltpu.VMEM(rates.shape, jnp.float32), pltpu.VMEM((8, 128), jnp.int32), pltpu.SemaphoreType.DMA((5,))],
     )(*map(in_hbm, (adjoint, wind_field, facade_slot, table, rates)))
     xa, xb = call(
@@ -474,6 +478,7 @@
     )(adjoint, wind, damping)
     saved, = call(fetch_kernel, 1, [HBM], [saved_state], [pltpu.SemaphoreType.DMA], cost=4000000)(in_hbm(saved_state))
     zb = swap(zb, swap_z)
+    zr = swap(zr, swap_z)
     ds = [swap(db, swap_y(side, True)) for side in range(sides)]
     ys = [swap(yb, swap_y(side, False)) for side in range(sides)]
     xa = swap(xa, swap_xa)
@@ -487,8 +492,8 @@
     cells = jax.ShapeDtypeStruct((FIELDS, BASE + depth_z + 1, 16, 128), jnp.float32)
     strips = jax.ShapeDtypeStruct((FIELDS, 16, 128), jnp.float32)
     cells, strips = call(
-        functools.partial(fill_kernel, sides), 2, [VMEM] * (6 + 2 * sides), [cells, strips], cost=4000000
-    )(adjoint, wind, damping, zb, *ys, *ds, xa, xb)
+        functools.partial(fill_kernel, sides), 2, [VMEM] * (7 + 2 * sides), [cells, strips], cost=4000000
+    )(adjoint, wind, damping, zb, zr, *ys, *ds, xa, xb)
     row = jax.ShapeDtypeStruct((1, 128), jnp.float32)
     cells, strips, own, part_a, part_b = call(
         step_kernel,

time: 26.5 us -> 27.1 us (1.023)
  waiting for transfers between devices: 3.92 us -> 6.38 us
  starting transfers between devices: 15 us -> 13.2 us
    ppermute x9 -> x10, waiting for transfers between devices: 3.92 us -> 6.38 us  [swap(): return lax.ppermute(block, AXES, pairs)]
    ppermute x9 -> x10, starting transfers between devices: 15 us -> 13.2 us  [swap(): return lax.ppermute(block, AXES, pairs)]
  transfers between devices with their start and end apart: 9 -> 10, of which waited for: 2 -> 3; matrix products, arithmetic and copies ran while one was open for 0% -> 0% of each run, Pallas kernels for 8% -> 8%
where the time goes in v5:
time: 27.1 us; the launch traced here: 26.9 us
  starting transfers between devices  13.2 us (49%)
  waiting for transfers between devices  6.38 us (24%)
  Pallas kernels  6.04 us (22%)
  between operations  0.71 us (3%)
  local copies, waits for them, and re-layouts  0.51 us (2%)
    ppermute x10, starting transfers between devices, swap(): return lax.ppermute(block, AXES, pairs)  13.2 us
    ppermute x10, waiting for transfers between devices, swap(): return lax.ppermute(block, AXES, pairs)  6.38 us
    pallas_call x1, Pallas kernels, local(): call(step_kernel, 2, [VMEM] * 7, [cells, strips, row, row, row], [pltpu.V...  2.58 us
    pallas_call x1, Pallas kernels, local(): call(pack_kernel, 4, [HBM] * 5, [adjoint, wind_field, facade_slot, table,...  1.29 us
    pallas_call x1, Pallas kernels, local(): call(fetch_kernel, 1, [HBM], [saved_state], [pltpu.SemaphoreType.DMA], co...  1.05 us
    pallas_call x1, Pallas kernels, local(): call(last_kernel, 2, [VMEM] * 2, [adjoint], cost=4000000)(cells, strips)  0.92 us
  transfers between devices with their start and end apart: 10, of which 3 were waited for; matrix products, arithmetic and copies ran while one was open for 0% of the time, Pallas kernels for 8%

profile of v5, /device:TPU:0, one launch (start us, length us, event | category | flops | bytes accessed | tf_op | source)
XLA Modules:
  0.0 26.9 jit_solution(1283837165626099757)
XLA Ops:
  0.6 1.3 %shard_map.77 = (f32[2,4,8,8,128]{4,3,2,1,0:T(8,128)S(1)}, f32[3,8,8,128]{3,2,1,0:T(8,128)S(1)}, s32[8,8,128]{2,1,0:T(8,128)S(1)}, s32[1,64]{1,0:T(1,128)S(1)}, ...) custom-call(f32[2,4,8,8,128]{4,3,2,1,0:T(8,128)} %refs_0_.1, ...), custom_call_target="tpu_custom_call" | custom-call | tf_op jit(solution)/shard_map/pallas_call | solution.py:469
  1.9 3.0 %collective-permute-start = (f32[30,8,128]{2,1,0:T(8,128)S(1)}, f32[30,8,128]{2,1,0:T(8,128)S(1)}, u32[]{:S(2)}, u32[]{:S(2)}) collective-permute-start(f32[30,8,128]{2,1,0:T(8,128)S(1)} %get-tuple-element.25), channel_id=1, source_target_pairs={{0,1},{1,0},{2,3},{3,2},{4,5},{5,4},{6,7},{7,6},{8,9},{9,8},{10,11... | collective-permute-start | bytes 368648 | tf_op jit(solution)/shard_map/ppermute | solution.py:404
  5.0 0.1 shard_map.78
  5.0 0.1 collective-permute-start.4
  5.1 1.6 %collective-permute-start.5 = (f32[48,8,128]{2,1,0:T(8,128)S(1)}, f32[48,8,128]{2,1,0:T(8,128)S(1)}, u32[]{:S(2)}, u32[]{:S(2)}) collective-permute-start(f32[48,8,128]{2,1,0:T(8,128)S(1)} %get-tuple-element.30), channel_id=1, source_target_pairs={{0,2},{1,3},{2,0},{3,1},{4,8},{5,9},{6,10},{7,11},{8,4},{9,5},{10,... | collective-permute-start | bytes 589832 | tf_op jit(solution)/shard_map/ppermute | solution.py:404
  6.7 0.5 %collective-permute-start.2 = (f32[6,8,128]{2,1,0:T(8,128)S(1)}, f32[6,8,128]{2,1,0:T(8,128)S(1)}, u32[]{:S(2)}, u32[]{:S(2)}) collective-permute-start(f32[6,8,128]{2,1,0:T(8,128)S(1)} %get-tuple-element.27), channel_id=1, source_target_pairs={{0,2},{1,3},{2,0},{3,1},{4,6},{5,7},{6,4},{7,5},{8,10},{9,11},{10,... | collective-permute-start | bytes 73736 | tf_op jit(solution)/shard_map/ppermute | solution.py:404
  7.2 1.5 %collective-permute-start.3 = (f32[3,8,128]{2,1,0:T(8,128)S(1)}, f32[3,8,128]{2,1,0:T(8,128)S(1)}, u32[]{:S(2)}, u32[]{:S(2)}) collective-permute-start(f32[3,8,128]{2,1,0:T(8,128)S(1)} %get-tuple-element.28), channel_id=1, source_target_pairs={{0,3},{1,2},{2,1},{3,0},{4,7},{5,6},{6,5},{7,4},{8,11},{9,10},{10,... | collective-permute-start | bytes 36872 | tf_op jit(solution)/shard_map/ppermute | solution.py:404
  8.7 3.2 %collective-permute-done.3.rest_1_ = f32[3,8,128]{2,1,0:T(8,128)S(1)} collective-permute-done((f32[3,8,128]{2,1,0:T(8,128)S(1)}, f32[3,8,128]{2,1,0:T(8,128)S(1)}, u32[]{:S(2)}, u32[]{:S(2)}) %collective-permute-start.3) | collective-permute-done | bytes 12320 | tf_op jit(solution)/shard_map/ppermute | solution.py:404
  11.8 0.0 collective-permute-done.2.rest_0_
  11.9 0.0 collective-permute-done.zb
  11.9 0.1 collective-permute-start.6
  12.0 0.7 %collective-permute-start.7 = (f32[20,8,128]{2,1,0:T(8,128)S(1)}, f32[20,8,128]{2,1,0:T(8,128)S(1)}, u32[]{:S(2)}, u32[]{:S(2)}) collective-permute-start(f32[20,8,128]{2,1,0:T(8,128)S(1)} %get-tuple-element.34), channel_id=1, source_target_pairs={{4,8},{5,9},{6,10},{7,11},{8,4},{9,5},{10,6},{11,7},{12,16},{13,17... | collective-permute-start | bytes 245768 | tf_op jit(solution)/shard_map/ppermute | solution.py:404
  12.7 0.2 collective-permute-start.1
  12.9 1.0 %shard_map.81.saved = f32[4,4,8,8,128]{4,3,2,1,0:T(8,128)S(1)} custom-call(f32[4,4,8,8,128]{4,3,2,1,0:T(8,128)} %source.1), custom_call_target="tpu_custom_call" | custom-call | flops 4000000 | bytes 4000000 | tf_op jit(solution)/shard_map/pallas_call | solution.py:479
  14.0 2.8 %collective-permute-done.1.zr = f32[11,8,128]{2,1,0:T(8,128)S(1)} collective-permute-done((f32[11,8,128]{2,1,0:T(8,128)S(1)}, f32[11,8,128]{2,1,0:T(8,128)S(1)}, u32[]{:S(2)}, u32[]{:S(2)}) %collective-permute-start.1) | collective-permute-done | bytes 45088 | tf_op jit(solution)/shard_map/ppermute | solution.py:404
  16.8 0.0 collective-permute-done.4.rest_2_
  16.8 0.0 collective-permute-done.5.rest_3_
  16.8 0.1 shard_map.79
  16.9 0.0 collective-permute-done.6.ea
  16.9 0.0 collective-permute-done.7.eb
  16.9 2.6 %shard_map.82 = (f32[12,14,16,128]{3,2,1,0:T(8,128)S(1)}, f32[12,16,128]{2,1,0:T(8,128)S(1)}, f32[1,128]{1,0:T(1,128)S(1)}, f32[1,128]{1,0:T(1,128)S(1)}, f32[1,128]{1,0:T(1,128)S(1)}) custom-call(f32[12,14,16,128]{3,2,1,0:T(8,128)S(1)} %get-tuple-element.31.cells_in, ...), custom_call_target="tpu_custom_call", output_to_operand_aliasing={{0}: (0, {}), {1}: (1, {})} | custom-call | tf_op jit(solution)/shard_map/pallas_call | solution.py:498
  19.5 1.9 %collective-permute-start.8 = (f32[1,128]{1,0:T(1,128)S(1)}, f32[1,128]{1,0:T(1,128)S(1)}, u32[]{:S(2)}, u32[]{:S(2)}) collective-permute-start(f32[1,128]{1,0:T(1,128)S(1)} %get-tuple-element.40), channel_id=1, source_target_pairs={{0,4},{1,5},{2,6},{3,7},{4,0},{5,1},{6,2},{7,3},{8,12},{9,13},{10,... | collective-permute-start | bytes 1544 | tf_op jit(solution)/shard_map/ppermute | solution.py:404
  21.4 3.7 %collective-permute-start.9 = (f32[1,128]{1,0:T(1,128)S(1)}, f32[1,128]{1,0:T(1,128)S(1)}, u32[]{:S(2)}, u32[]{:S(2)}) collective-permute-start(f32[1,128]{1,0:T(1,128)S(1)} %get-tuple-element.41), channel_id=1, source_target_pairs={{0,28},{1,29},{2,30},{3,31},{4,8},{5,9},{6,10},{7,11},{8,4},{9,5},... | collective-permute-start | bytes 1544 | tf_op jit(solution)/shard_map/ppermute | solution.py:404
  25.1 0.9 %shard_map.83 = f32[2,4,8,8,128]{4,3,2,1,0:T(8,128)} custom-call(f32[12,14,16,128]{3,2,1,0:T(8,128)S(1)} %get-tuple-element.37.cells, f32[12,16,128]{2,1,0:T(8,128)S(1)} %get-tuple-element.38.strips), custom_call_target="tpu_custom_call" | custom-call | flops 4000000 | bytes 4000000 | tf_op jit(solution)/shard_map/pallas_call | solution.py:508
  26.0 0.0 collective-permute-done.8
  26.0 0.4 %collective-permute-done.9 = f32[1,128]{1,0:T(1,128)S(1)} collective-permute-done((f32[1,128]{1,0:T(1,128)S(1)}, f32[1,128]{1,0:T(1,128)S(1)}, u32[]{:S(2)}, u32[]{:S(2)}) %collective-permute-start.9) | collective-permute-done | bytes 544 | tf_op jit(solution)/shard_map/ppermute | solution.py:404
  26.4 0.5 %slice_bitcast_fusion = f32[32]{0:T(128)} fusion(f32[1,128]{1,0:T(1,128)S(1)} %add_add_fusion), kind=kLoop, calls=%fused_computation | loop fusion | bytes 256 | tf_op jit(solution)/shard_map/squeeze | solution.py:509
  (2 shorter events, 0.0 us)
Async XLA Ops:
  1.9 9.9 %collective-permute-start = (f32[30,8,128]{2,1,0:T(8,128)S(1)}, f32[30,8,128]{2,1,0:T(8,128)S(1)}, u32[]{:S(2)}, u32[]{:S(2)}) collective-permute-start(f32[30,8,128]{2,1,0:T(8,128)S(1)} %get-tuple-element.25), channel_id=1, source_target_pairs={{0,1},{1,0},{2,3},{3,2},{4,5},{5,4},{6,7},{7,6},{8,9},{9,8},{10,11... | collective-permute-start | bytes 368648 | tf_op jit(solution)/shard_map/ppermute | solution.py:404
  5.0 11.8 %collective-permute-start.4 = (f32[48,8,128]{2,1,0:T(8,128)S(1)}, f32[48,8,128]{2,1,0:T(8,128)S(1)}, u32[]{:S(2)}, u32[]{:S(2)}) collective-permute-start(f32[48,8,128]{2,1,0:T(8,128)S(1)} %get-tuple-element.29), channel_id=1, source_target_pairs={{0,4},{1,5},{2,6},{3,7},{4,0},{5,1},{6,2},{7,3},{8,12},{9,13},{10,... | collective-permute-start | bytes 589832 | tf_op jit(solution)/shard_map/ppermute | solution.py:404
  5.1 11.7 %collective-permute-start.5 = (f32[48,8,128]{2,1,0:T(8,128)S(1)}, f32[48,8,128]{2,1,0:T(8,128)S(1)}, u32[]{:S(2)}, u32[]{:S(2)}) collective-permute-start(f32[48,8,128]{2,1,0:T(8,128)S(1)} %get-tuple-element.30), channel_id=1, source_target_pairs={{0,2},{1,3},{2,0},{3,1},{4,8},{5,9},{6,10},{7,11},{8,4},{9,5},{10,... | collective-permute-start | bytes 589832 | tf_op jit(solution)/shard_map/ppermute | solution.py:404
  6.7 5.2 %collective-permute-start.2 = (f32[6,8,128]{2,1,0:T(8,128)S(1)}, f32[6,8,128]{2,1,0:T(8,128)S(1)}, u32[]{:S(2)}, u32[]{:S(2)}) collective-permute-start(f32[6,8,128]{2,1,0:T(8,128)S(1)} %get-tuple-element.27), channel_id=1, source_target_pairs={{0,2},{1,3},{2,0},{3,1},{4,6},{5,7},{6,4},{7,5},{8,10},{9,11},{10,... | collective-permute-start | bytes 73736 | tf_op jit(solution)/shard_map/ppermute | solution.py:404
  7.2 4.7 %collective-permute-start.3 = (f32[3,8,128]{2,1,0:T(8,128)S(1)}, f32[3,8,128]{2,1,0:T(8,128)S(1)}, u32[]{:S(2)}, u32[]{:S(2)}) collective-permute-start(f32[3,8,128]{2,1,0:T(8,128)S(1)} %get-tuple-element.28), channel_id=1, source_target_pairs={{0,3},{1,2},{2,1},{3,0},{4,7},{5,6},{6,5},{7,4},{8,11},{9,10},{10,... | collective-permute-start | bytes 36872 | tf_op jit(solution)/shard_map/ppermute | solution.py:404
  11.9 5.0 %collective-permute-start.6 = (f32[20,8,128]{2,1,0:T(8,128)S(1)}, f32[20,8,128]{2,1,0:T(8,128)S(1)}, u32[]{:S(2)}, u32[]{:S(2)}) collective-permute-start(f32[20,8,128]{2,1,0:T(8,128)S(1)} %get-tuple-element.33), channel_id=1, source_target_pairs={{0,4},{1,5},{2,6},{3,7},{4,0},{5,1},{6,2},{7,3},{8,12},{9,13},{10,... | collective-permute-start | bytes 245768 | tf_op jit(solution)/shard_map/ppermute | solution.py:404
  12.0 4.9 %collective-permute-start.7 = (f32[20,8,128]{2,1,0:T(8,128)S(1)}, f32[20,8,128]{2,1,0:T(8,128)S(1)}, u32[]{:S(2)}, u32[]{:S(2)}) collective-permute-start(f32[20,8,128]{2,1,0:T(8,128)S(1)} %get-tuple-element.34), channel_id=1, source_target_pairs={{4,8},{5,9},{6,10},{7,11},{8,4},{9,5},{10,6},{11,7},{12,16},{13,17... | collective-permute-start | bytes 245768 | tf_op jit(solution)/shard_map/ppermute | solution.py:404
  12.7 4.1 %collective-permute-start.1 = (f32[11,8,128]{2,1,0:T(8,128)S(1)}, f32[11,8,128]{2,1,0:T(8,128)S(1)}, u32[]{:S(2)}, u32[]{:S(2)}) collective-permute-start(f32[11,8,128]{2,1,0:T(8,128)S(1)} %get-tuple-element.26), channel_id=1, source_target_pairs={{0,1},{1,0},{2,3},{3,2},{4,5},{5,4},{6,7},{7,6},{8,9},{9,8},{10,11... | collective-permute-start | bytes 135176 | tf_op jit(solution)/shard_map/ppermute | solution.py:404
  19.5 6.5 %collective-permute-start.8 = (f32[1,128]{1,0:T(1,128)S(1)}, f32[1,128]{1,0:T(1,128)S(1)}, u32[]{:S(2)}, u32[]{:S(2)}) collective-permute-start(f32[1,128]{1,0:T(1,128)S(1)} %get-tuple-element.40), channel_id=1, source_target_pairs={{0,4},{1,5},{2,6},{3,7},{4,0},{5,1},{6,2},{7,3},{8,12},{9,13},{10,... | collective-permute-start | bytes 1544 | tf_op jit(solution)/shard_map/ppermute | solution.py:404
  21.4 5.0 %collective-permute-start.9 = (f32[1,128]{1,0:T(1,128)S(1)}, f32[1,128]{1,0:T(1,128)S(1)}, u32[]{:S(2)}, u32[]{:S(2)}) collective-permute-start(f32[1,128]{1,0:T(1,128)S(1)} %get-tuple-element.41), channel_id=1, source_target_pairs={{0,28},{1,29},{2,30},{3,31},{4,8},{5,9},{6,10},{7,11},{8,4},{9,5},... | collective-permute-start | bytes 1544 | tf_op jit(solution)/shard_map/ppermute | solution.py:404

commit v6 on v5

--- a/solution.py
+++ b/solution.py
@@ -206,6 +206,62 @@
     cells[f, slot, 8 * tx:8 * tx + 8, :] = value
 
 
+def y_change(main, side, slot, lanes):
+    above = pltpu.roll(side, 127 - DEPTH - GROUP * slot, 1)
+    below = pltpu.roll(side, 129 - DEPTH - GROUP * slot, 1)
+    up = jnp.where(lanes == 127, above, pltpu.roll(main, 127, 1))
+    return up - jnp.where(lanes == 0, below, pltpu.roll(main, 1, 1))
+
+
+def cell_factor():
+    rows = iota(0, (16, 128))
+    x = lax.axis_index("gx")
+    row_end = jnp.where(x == lax.axis_size("gx") - 1, 8, 12)
+    row_restart = jnp.where(x == 0, 16, 12)
+    return jnp.where((rows < row_end) | (rows >= row_restart), jnp.float32(0.5 * SCALE), 0.0)
+
+
+def side_fluxes(strips, middle_at):
+    side = [strips[middle_at + c] for c in range(4)]
+    return side, [flux(strips[10], side, c, 2) for c in range(4)]
+
+
+def step_layers(cells, first, size, passes, middle_at, upper_at, side_y, joined):
+    lanes = iota(1, (16, 128))
+    groups = lanes // GROUP
+    factor = cell_factor()
+    sign = z_sign()
+
+    def body(slot, joined):
+        middle = [cells[middle_at + c, slot] for c in range(4)]
+        above = [cells[middle_at + c, slot + 1] for c in range(4)]
+        below = [cells[middle_at + c, slot - 1] for c in range(4)]
+        wind_up, wind_down = cells[8, slot + 1], cells[8, slot - 1]
+        wind_x, wind_y = cells[9, slot], cells[10, slot]
+        loss = SCALE * cells[11, slot]
+        seen = []
+        for c in range(4):
+            total = sign * (flux(wind_up, above, c, 0) - flux(wind_down, below, c, 0))
+            along = flux(wind_x, middle, c, 1)
+            total += pltpu.roll(along, 15, 0) - pltpu.roll(along, 1, 0)
+            along = flux(wind_y, middle, c, 2)
+            total += y_change(along, side_y[c], slot, lanes)
+            seen.append(jnp.where(groups == slot, pltpu.roll(along, GROUP * slot + DEPTH, 1), joined[c]))
+            cells[upper_at + c, slot] = cells[upper_at + c, slot] + factor * total - loss * middle[c]
+        return tuple(seen)
+
+    def some(i, joined):
+        for j in range(size):
+            joined = body(first + size * i + j, joined)
+        return joined
+
+    return lax.fori_loop(0, passes, some, joined) if passes > 1 else some(0, joined)
+
+
+def no_edges():
+    return tuple(jnp.zeros((16, 128), jnp.float32) for _ in range(4))
+
+
 def fetch_kernel(source, target, sem):
     copy = pltpu.make_async_copy(source, target, sem)
     copy.start()
@@ -215,7 +271,7 @@
 def fill_kernel(sides, adjoint, wind, damping, zb, zr, *rest):
     y_rows = merged_rows(rest[:sides])
     d_rows = merged_rows(rest[sides:2 * sides])
-    xa, xb, cells, strips = rest[2 * sides:]
+    xa, xb, cells, strips, joined = rest[2 * sides:]
     depth_z = damping.shape[0]
     zero = jnp.zeros((8, 128), jnp.float32)
     load = loader(adjoint, wind, damping)
@@ -237,16 +293,14 @@
             put(cells, f, 1, tx, zero)
     for f, t in R_PLANES:
         put(cells, f, BASE - t, 1, zero)
-
-
-def y_change(main, side, slot, lanes):
-    above = pltpu.roll(side, 127 - DEPTH - GROUP * slot, 1)
-    below = pltpu.roll(side, 129 - DEPTH - GROUP * slot, 1)
-    up = jnp.where(lanes == 127, above, pltpu.roll(main, 127, 1))
-    return up - jnp.where(lanes == 0, below, pltpu.roll(main, 1, 1))
-
-
-def step_kernel(cells_in, strips_in, ea, eb, saved, slots, table, cells, strips, own, part_a, part_b, prod, acc):
+    for f in (0, 1, 2, 3, 10):
+        strips[f, 8:16, :] = zero
+    _, side_y = side_fluxes(strips, 0)
+    for c, value in enumerate(step_layers(cells, BASE + 1, depth_z - 1, 1, 0, 4, side_y, no_edges())):
+        joined[c] = value
+
+
+def step_kernel(cells_in, strips_in, early, ea, eb, saved, slots, table, cells, strips, own, part_a, part_b, prod, acc):
     del cells_in, strips_in
     depth_z = slots.shape[0]
     far = BASE + depth_z
@@ -258,49 +312,29 @@
         strips[f, 8:16, :] = unpack_strip(f, edges[start:start + Y_ROWS], edges[start + Y_ROWS:])
 
     tile = (16, 128)
-    rows, lanes = iota(0, tile), iota(1, tile)
-    groups, k = lanes // GROUP, lanes % GROUP
-    x, y = lax.axis_index("gx"), lax.axis_index("gy")
-    row_end = jnp.where(x == lax.axis_size("gx") - 1, 8, 12)
-    row_restart = jnp.where(x == 0, 16, 12)
-    inside = (rows < row_end) | (rows >= row_restart)
+    lanes = iota(1, tile)
+    k = lanes % GROUP
+    y = lax.axis_index("gy")
     k_first = jnp.where(y == 0, DEPTH, 0)
     k_end = jnp.where(y == lax.axis_size("gy") - 1, DEPTH, GROUP)
-    factor = jnp.where(inside, jnp.float32(0.5 * SCALE), 0.0)
+    factor = cell_factor()
     side_factor = jnp.where((k >= k_first) & (k < k_end) & (lanes < GROUP * far), factor, 0.0)
     sign = z_sign()
 
     def full_step(halo, middle_at, upper_at):
-        size = -(-(depth_z + halo) // PASSES)
-        first = far - size * PASSES
-        side = [strips[middle_at + c] for c in range(4)]
-        side_y = [flux(strips[10], side, c, 2) for c in range(4)]
-
-        def body(slot, joined):
-            middle = [cells[middle_at + c, slot] for c in range(4)]
-            above = [cells[middle_at + c, slot + 1] for c in range(4)]
-            below = [cells[middle_at + c, slot - 1] for c in range(4)]
-            wind_up, wind_down = cells[8, slot + 1], cells[8, slot - 1]
-            wind_x, wind_y = cells[9, slot], cells[10, slot]
-            loss = SCALE * cells[11, slot]
-            seen = []
-            for c in range(4):
-                total = sign * (flux(wind_up, above, c, 0) - flux(wind_down, below, c, 0))
-                along = flux(wind_x, middle, c, 1)
-                total += pltpu.roll(along, 15, 0) - pltpu.roll(along, 1, 0)
-                along = flux(wind_y, middle, c, 2)
-                total += y_change(along, side_y[c], slot, lanes)
-                seen.append(jnp.where(groups == slot, pltpu.roll(along, GROUP * slot + DEPTH, 1), joined[c]))
-                cells[upper_at + c, slot] = cells[upper_at + c, slot] + factor * total - loss * middle[c]
-            return tuple(seen)
-
-        def chunk(i, joined):
-            for j in range(size):
-                joined = body(first + size * i + j, joined)
-            return joined
-
-        zeros = tuple(jnp.zeros(tile, jnp.float32) for _ in range(4))
-        joined = lax.fori_loop(0, PASSES, chunk, zeros)
+        side, side_y = side_fluxes(strips, middle_at)
+        if halo == DEPTH - 1:
+            joined = tuple(early[c] for c in range(4))
+            joined = step_layers(cells, BASE - halo, halo + 1, 1, middle_at, upper_at, side_y, joined)
+            edge_factor = factor[8:16]
+            for slot in range(BASE + 1, far):
+                for c in range(4):
+                    extra = y_change(jnp.zeros((8, 128), jnp.float32), side_y[c][8:16], slot, lanes[8:16])
+                    cells[upper_at + c, slot, 8:16, :] = cells[upper_at + c, slot, 8:16, :] + edge_factor * extra
+        else:
+            size = -(-(depth_z + halo) // PASSES)
+            first = far - size * PASSES
+            joined = step_layers(cells, first, size, PASSES, middle_at, upper_at, side_y, no_edges())
         loss = SCALE * strips[11]
         for c in range(4):
             along = flux(strips[8], side, c, 0)
@@ -491,18 +525,22 @@
     eb = swap(eb, swap_xb_only)
     cells = jax.ShapeDtypeStruct((FIELDS, BASE + depth_z + 1, 16, 128), jnp.float32)
     strips = jax.ShapeDtypeStruct((FIELDS, 16, 128), jnp.float32)
-    cells, strips = call(
-        functools.partial(fill_kernel, sides), 2, [VMEM] * (7 + 2 * sides), [cells, strips], cost=4000000
+    cells, strips, early = call(
+        functools.partial(fill_kernel, sides),
+        2,
+        [VMEM] * (7 + 2 * sides),
+        [cells, strips, jax.ShapeDtypeStruct((4, 16, 128), jnp.float32)],
+        cost=4000000,
     )(adjoint, wind, damping, zb, zr, *ys, *ds, xa, xb)
     row = jax.ShapeDtypeStruct((1, 128), jnp.float32)
     cells, strips, own, part_a, part_b = call(
         step_kernel,
         2,
-        [VMEM] * 7,
+        [VMEM] * 8,
         [cells, strips, row, row, row],
         [pltpu.VMEM((depth_z, 8, 128), jnp.float32), pltpu.VMEM((table.shape[1], 128), jnp.float32)],
         aliases={0: 0, 1: 1},
-    )(cells, strips, ea, eb, saved, slots, table)
+    )(cells, strips, early, ea, eb, saved, slots, table)
     part_b = swap(part_b, swap_ring)
     part_a = swap(part_a, swap_xa)
     out, = call(last_kernel, 2, [VMEM] * 2, [adjoint], cost=4000000)(cells, strips)

time: 27.1 us -> 26.9 us (level)
    pallas_call x1, Pallas kernels: 2.58 us -> 2.12 us  [local(): call(step_kernel, 2, [VMEM] * 8, [cells, strips, row, row, row], [pltpu.V...]
    pallas_call x1, Pallas kernels: 0.12 us -> 0.45 us  [local(): call(functools.partial(fill_kernel, sides), 2, [VMEM] * (7 + 2 * sides),...]
  transfers between devices with their start and end apart: 10 -> 10, of which waited for: 3 -> 3; matrix products, arithmetic and copies ran while one was open for 0% -> 0% of each run, Pallas kernels for 8% -> 9%
where the time goes in v6:
time: 26.9 us; the launch traced here: 26.7 us
  starting transfers between devices  13.2 us (49%)
  waiting for transfers between devices  6.38 us (24%)
  Pallas kernels  5.91 us (22%)
  between operations  0.7 us (3%)
  local copies, waits for them, and re-layouts  0.51 us (2%)
    ppermute x10, starting transfers between devices, swap(): return lax.ppermute(block, AXES, pairs)  13.2 us
    ppermute x10, waiting for transfers between devices, swap(): return lax.ppermute(block, AXES, pairs)  6.38 us
    pallas_call x1, Pallas kernels, local(): call(step_kernel, 2, [VMEM] * 8, [cells, strips, row, row, row], [pltpu.V...  2.12 us
    pallas_call x1, Pallas kernels, local(): call(pack_kernel, 4, [HBM] * 5, [adjoint, wind_field, facade_slot, table,...  1.29 us
    pallas_call x1, Pallas kernels, local(): call(fetch_kernel, 1, [HBM], [saved_state], [pltpu.SemaphoreType.DMA], co...  1.05 us
    pallas_call x1, Pallas kernels, local(): call(last_kernel, 2, [VMEM] * 2, [adjoint], cost=4000000)(cells, strips)  0.92 us
  transfers between devices with their start and end apart: 10, of which 3 were waited for; matrix products, arithmetic and copies ran while one was open for 0% of the time, Pallas kernels for 9%

profile of v6, /device:TPU:0, one launch (start us, length us, event | category | flops | bytes accessed | tf_op | source)
XLA Modules:
  0.0 26.7 jit_solution(4926346259864983135)
XLA Ops:
  0.6 1.3 %shard_map.77 = (f32[2,4,8,8,128]{4,3,2,1,0:T(8,128)S(1)}, f32[3,8,8,128]{3,2,1,0:T(8,128)S(1)}, s32[8,8,128]{2,1,0:T(8,128)S(1)}, s32[1,64]{1,0:T(1,128)S(1)}, ...) custom-call(f32[2,4,8,8,128]{4,3,2,1,0:T(8,128)} %refs_0_.1, ...), custom_call_target="tpu_custom_call" | custom-call | tf_op jit(solution)/shard_map/pallas_call | solution.py:503
  1.9 3.0 %collective-permute-start = (f32[30,8,128]{2,1,0:T(8,128)S(1)}, f32[30,8,128]{2,1,0:T(8,128)S(1)}, u32[]{:S(2)}, u32[]{:S(2)}) collective-permute-start(f32[30,8,128]{2,1,0:T(8,128)S(1)} %get-tuple-element.26), channel_id=1, source_target_pairs={{0,1},{1,0},{2,3},{3,2},{4,5},{5,4},{6,7},{7,6},{8,9},{9,8},{10,11... | collective-permute-start | bytes 368648 | tf_op jit(solution)/shard_map/ppermute | solution.py:438
  5.0 0.1 shard_map.78
  5.0 0.1 collective-permute-start.4
  5.1 1.6 %collective-permute-start.5 = (f32[48,8,128]{2,1,0:T(8,128)S(1)}, f32[48,8,128]{2,1,0:T(8,128)S(1)}, u32[]{:S(2)}, u32[]{:S(2)}) collective-permute-start(f32[48,8,128]{2,1,0:T(8,128)S(1)} %get-tuple-element.31), channel_id=1, source_target_pairs={{0,2},{1,3},{2,0},{3,1},{4,8},{5,9},{6,10},{7,11},{8,4},{9,5},{10,... | collective-permute-start | bytes 589832 | tf_op jit(solution)/shard_map/ppermute | solution.py:438
  6.7 0.5 %collective-permute-start.2 = (f32[6,8,128]{2,1,0:T(8,128)S(1)}, f32[6,8,128]{2,1,0:T(8,128)S(1)}, u32[]{:S(2)}, u32[]{:S(2)}) collective-permute-start(f32[6,8,128]{2,1,0:T(8,128)S(1)} %get-tuple-element.28), channel_id=1, source_target_pairs={{0,2},{1,3},{2,0},{3,1},{4,6},{5,7},{6,4},{7,5},{8,10},{9,11},{10,... | collective-permute-start | bytes 73736 | tf_op jit(solution)/shard_map/ppermute | solution.py:438
  7.2 1.5 %collective-permute-start.3 = (f32[3,8,128]{2,1,0:T(8,128)S(1)}, f32[3,8,128]{2,1,0:T(8,128)S(1)}, u32[]{:S(2)}, u32[]{:S(2)}) collective-permute-start(f32[3,8,128]{2,1,0:T(8,128)S(1)} %get-tuple-element.29), channel_id=1, source_target_pairs={{0,3},{1,2},{2,1},{3,0},{4,7},{5,6},{6,5},{7,4},{8,11},{9,10},{10,... | collective-permute-start | bytes 36872 | tf_op jit(solution)/shard_map/ppermute | solution.py:438
  8.7 3.2 %collective-permute-done.3.rest_1_ = f32[3,8,128]{2,1,0:T(8,128)S(1)} collective-permute-done((f32[3,8,128]{2,1,0:T(8,128)S(1)}, f32[3,8,128]{2,1,0:T(8,128)S(1)}, u32[]{:S(2)}, u32[]{:S(2)}) %collective-permute-start.3) | collective-permute-done | bytes 12320 | tf_op jit(solution)/shard_map/ppermute | solution.py:438
  11.8 0.0 collective-permute-done.2.rest_0_
  11.9 0.0 collective-permute-done.zb
  11.9 0.1 collective-permute-start.6
  12.0 0.7 %collective-permute-start.7 = (f32[20,8,128]{2,1,0:T(8,128)S(1)}, f32[20,8,128]{2,1,0:T(8,128)S(1)}, u32[]{:S(2)}, u32[]{:S(2)}) collective-permute-start(f32[20,8,128]{2,1,0:T(8,128)S(1)} %get-tuple-element.36), channel_id=1, source_target_pairs={{4,8},{5,9},{6,10},{7,11},{8,4},{9,5},{10,6},{11,7},{12,16},{13,17... | collective-permute-start | bytes 245768 | tf_op jit(solution)/shard_map/ppermute | solution.py:438
  12.7 0.2 collective-permute-start.1
  12.9 1.0 %shard_map.81.saved = f32[4,4,8,8,128]{4,3,2,1,0:T(8,128)S(1)} custom-call(f32[4,4,8,8,128]{4,3,2,1,0:T(8,128)} %source.1), custom_call_target="tpu_custom_call" | custom-call | flops 4000000 | bytes 4000000 | tf_op jit(solution)/shard_map/pallas_call | solution.py:513
  14.0 2.8 %collective-permute-done.1.zr = f32[11,8,128]{2,1,0:T(8,128)S(1)} collective-permute-done((f32[11,8,128]{2,1,0:T(8,128)S(1)}, f32[11,8,128]{2,1,0:T(8,128)S(1)}, u32[]{:S(2)}, u32[]{:S(2)}) %collective-permute-start.1) | collective-permute-done | bytes 45088 | tf_op jit(solution)/shard_map/ppermute | solution.py:438
  16.8 0.0 collective-permute-done.4.rest_2_
  16.8 0.0 collective-permute-done.5.rest_3_
  16.8 0.5 %shard_map.79 = (f32[12,14,16,128]{3,2,1,0:T(8,128)S(1)}, f32[12,16,128]{2,1,0:T(8,128)S(1)}, f32[4,16,128]{2,1,0:T(8,128)S(1)}) custom-call(f32[2,4,8,8,128]{4,3,2,1,0:T(8,128)S(1)} %get-tuple-element.23.adjoint, f32[3,8,8,128]{3,2,1,0:T(8,128)S(1)} %get-tuple-element.24.wind, f32[8,8,128]{2,1,0:T(8,128)S(1)} %get-tuple-element.25.damping, ...), custom_call_target="tpu_custom_call" | custom-call | flops 4000000 | bytes 4000000 | tf_op jit(solution)/shard_map/pallas_call | solution.py:528
  17.2 0.0 collective-permute-done.6.ea
  17.3 0.0 collective-permute-done.7.eb
  17.3 2.1 %shard_map.82 = (f32[12,14,16,128]{3,2,1,0:T(8,128)S(1)}, f32[12,16,128]{2,1,0:T(8,128)S(1)}, f32[1,128]{1,0:T(1,128)S(1)}, f32[1,128]{1,0:T(1,128)S(1)}, f32[1,128]{1,0:T(1,128)S(1)}) custom-call(f32[12,14,16,128]{3,2,1,0:T(8,128)S(1)} %get-tuple-element.32.cells_in, ...), custom_call_target="tpu_custom_call", output_to_operand_aliasing={{0}: (0, {}), {1}: (1, {})} | custom-call | tf_op jit(solution)/shard_map/pallas_call | solution.py:536
  19.4 1.9 %collective-permute-start.8 = (f32[1,128]{1,0:T(1,128)S(1)}, f32[1,128]{1,0:T(1,128)S(1)}, u32[]{:S(2)}, u32[]{:S(2)}) collective-permute-start(f32[1,128]{1,0:T(1,128)S(1)} %get-tuple-element.42), channel_id=1, source_target_pairs={{0,4},{1,5},{2,6},{3,7},{4,0},{5,1},{6,2},{7,3},{8,12},{9,13},{10,... | collective-permute-start | bytes 1544 | tf_op jit(solution)/shard_map/ppermute | solution.py:438
  21.3 3.7 %collective-permute-start.9 = (f32[1,128]{1,0:T(1,128)S(1)}, f32[1,128]{1,0:T(1,128)S(1)}, u32[]{:S(2)}, u32[]{:S(2)}) collective-permute-start(f32[1,128]{1,0:T(1,128)S(1)} %get-tuple-element.43), channel_id=1, source_target_pairs={{0,28},{1,29},{2,30},{3,31},{4,8},{5,9},{6,10},{7,11},{8,4},{9,5},... | collective-permute-start | bytes 1544 | tf_op jit(solution)/shard_map/ppermute | solution.py:438
  24.9 0.9 %shard_map.83 = f32[2,4,8,8,128]{4,3,2,1,0:T(8,128)} custom-call(f32[12,14,16,128]{3,2,1,0:T(8,128)S(1)} %get-tuple-element.39.cells, f32[12,16,128]{2,1,0:T(8,128)S(1)} %get-tuple-element.40.strips), custom_call_target="tpu_custom_call" | custom-call | flops 4000000 | bytes 4000000 | tf_op jit(solution)/shard_map/pallas_call | solution.py:546
  25.8 0.0 collective-permute-done.8
  25.9 0.4 %collective-permute-done.9 = f32[1,128]{1,0:T(1,128)S(1)} collective-permute-done((f32[1,128]{1,0:T(1,128)S(1)}, f32[1,128]{1,0:T(1,128)S(1)}, u32[]{:S(2)}, u32[]{:S(2)}) %collective-permute-start.9) | collective-permute-done | bytes 544 | tf_op jit(solution)/shard_map/ppermute | solution.py:438
  26.2 0.5 %slice_bitcast_fusion = f32[32]{0:T(128)} fusion(f32[1,128]{1,0:T(1,128)S(1)} %add_add_fusion), kind=kLoop, calls=%fused_computation | loop fusion | bytes 256 | tf_op jit(solution)/shard_map/squeeze | solution.py:547
  (2 shorter events, 0.0 us)
Async XLA Ops:
  1.9 9.9 %collective-permute-start = (f32[30,8,128]{2,1,0:T(8,128)S(1)}, f32[30,8,128]{2,1,0:T(8,128)S(1)}, u32[]{:S(2)}, u32[]{:S(2)}) collective-permute-start(f32[30,8,128]{2,1,0:T(8,128)S(1)} %get-tuple-element.26), channel_id=1, source_target_pairs={{0,1},{1,0},{2,3},{3,2},{4,5},{5,4},{6,7},{7,6},{8,9},{9,8},{10,11... | collective-permute-start | bytes 368648 | tf_op jit(solution)/shard_map/ppermute | solution.py:438
  5.0 11.8 %collective-permute-start.4 = (f32[48,8,128]{2,1,0:T(8,128)S(1)}, f32[48,8,128]{2,1,0:T(8,128)S(1)}, u32[]{:S(2)}, u32[]{:S(2)}) collective-permute-start(f32[48,8,128]{2,1,0:T(8,128)S(1)} %get-tuple-element.30), channel_id=1, source_target_pairs={{0,4},{1,5},{2,6},{3,7},{4,0},{5,1},{6,2},{7,3},{8,12},{9,13},{10,... | collective-permute-start | bytes 589832 | tf_op jit(solution)/shard_map/ppermute | solution.py:438
  5.1 11.7 %collective-permute-start.5 = (f32[48,8,128]{2,1,0:T(8,128)S(1)}, f32[48,8,128]{2,1,0:T(8,128)S(1)}, u32[]{:S(2)}, u32[]{:S(2)}) collective-permute-start(f32[48,8,128]{2,1,0:T(8,128)S(1)} %get-tuple-element.31), channel_id=1, source_target_pairs={{0,2},{1,3},{2,0},{3,1},{4,8},{5,9},{6,10},{7,11},{8,4},{9,5},{10,... | collective-permute-start | bytes 589832 | tf_op jit(solution)/shard_map/ppermute | solution.py:438
  6.7 5.2 %collective-permute-start.2 = (f32[6,8,128]{2,1,0:T(8,128)S(1)}, f32[6,8,128]{2,1,0:T(8,128)S(1)}, u32[]{:S(2)}, u32[]{:S(2)}) collective-permute-start(f32[6,8,128]{2,1,0:T(8,128)S(1)} %get-tuple-element.28), channel_id=1, source_target_pairs={{0,2},{1,3},{2,0},{3,1},{4,6},{5,7},{6,4},{7,5},{8,10},{9,11},{10,... | collective-permute-start | bytes 73736 | tf_op jit(solution)/shard_map/ppermute | solution.py:438
  7.2 4.7 %collective-permute-start.3 = (f32[3,8,128]{2,1,0:T(8,128)S(1)}, f32[3,8,128]{2,1,0:T(8,128)S(1)}, u32[]{:S(2)}, u32[]{:S(2)}) collective-permute-start(f32[3,8,128]{2,1,0:T(8,128)S(1)} %get-tuple-element.29), channel_id=1, source_target_pairs={{0,3},{1,2},{2,1},{3,0},{4,7},{5,6},{6,5},{7,4},{8,11},{9,10},{10,... | collective-permute-start | bytes 36872 | tf_op jit(solution)/shard_map/ppermute | solution.py:438
  11.9 5.4 %collective-permute-start.6 = (f32[20,8,128]{2,1,0:T(8,128)S(1)}, f32[20,8,128]{2,1,0:T(8,128)S(1)}, u32[]{:S(2)}, u32[]{:S(2)}) collective-permute-start(f32[20,8,128]{2,1,0:T(8,128)S(1)} %get-tuple-element.35), channel_id=1, source_target_pairs={{0,4},{1,5},{2,6},{3,7},{4,0},{5,1},{6,2},{7,3},{8,12},{9,13},{10,... | collective-permute-start | bytes 245768 | tf_op jit(solution)/shard_map/ppermute | solution.py:438
  12.0 5.3 %collective-permute-start.7 = (f32[20,8,128]{2,1,0:T(8,128)S(1)}, f32[20,8,128]{2,1,0:T(8,128)S(1)}, u32[]{:S(2)}, u32[]{:S(2)}) collective-permute-start(f32[20,8,128]{2,1,0:T(8,128)S(1)} %get-tuple-element.36), channel_id=1, source_target_pairs={{4,8},{5,9},{6,10},{7,11},{8,4},{9,5},{10,6},{11,7},{12,16},{13,17... | collective-permute-start | bytes 245768 | tf_op jit(solution)/shard_map/ppermute | solution.py:438
  12.7 4.1 %collective-permute-start.1 = (f32[11,8,128]{2,1,0:T(8,128)S(1)}, f32[11,8,128]{2,1,0:T(8,128)S(1)}, u32[]{:S(2)}, u32[]{:S(2)}) collective-permute-start(f32[11,8,128]{2,1,0:T(8,128)S(1)} %get-tuple-element.27), channel_id=1, source_target_pairs={{0,1},{1,0},{2,3},{3,2},{4,5},{5,4},{6,7},{7,6},{8,9},{9,8},{10,11... | collective-permute-start | bytes 135176 | tf_op jit(solution)/shard_map/ppermute | solution.py:438
  19.4 6.5 %collective-permute-start.8 = (f32[1,128]{1,0:T(1,128)S(1)}, f32[1,128]{1,0:T(1,128)S(1)}, u32[]{:S(2)}, u32[]{:S(2)}) collective-permute-start(f32[1,128]{1,0:T(1,128)S(1)} %get-tuple-element.42), channel_id=1, source_target_pairs={{0,4},{1,5},{2,6},{3,7},{4,0},{5,1},{6,2},{7,3},{8,12},{9,13},{10,... | collective-permute-start | bytes 1544 | tf_op jit(solution)/shard_map/ppermute | solution.py:438
  21.3 5.0 %collective-permute-start.9 = (f32[1,128]{1,0:T(1,128)S(1)}, f32[1,128]{1,0:T(1,128)S(1)}, u32[]{:S(2)}, u32[]{:S(2)}) collective-permute-start(f32[1,128]{1,0:T(1,128)S(1)} %get-tuple-element.43), channel_id=1, source_target_pairs={{0,28},{1,29},{2,30},{3,31},{4,8},{5,9},{6,10},{7,11},{8,4},{9,5},... | collective-permute-start | bytes 1544 | tf_op jit(solution)/shard_map/ppermute | solution.py:438
